TPU v7x, 32 devices: a whole 2x2x4 slice. The times are simulated.
32 devices in a mesh: sample: 2 (over y), gx: 8 (over z, x), gy: 2 (over core).
Axes of the slice: x: 2, y: 2, z: 4, core: 2. Of those that a mesh axis runs over, the one named last changes fastest.
Arguments:
- body_force: float32 [3, 64, 32, 256], P(None, 'sample', 'gx', 'gy'), parts along dimension 1, may hold values from -36 to 36
- modulus: float32 [64, 32, 256], P('sample', 'gx', 'gy'), parts along dimension 0, may hold values from 0.12 to 8.2
Outputs:
- solution_field: float32 [3, 64, 32, 256], P(None, 'sample', 'gx', 'gy'), parts along dimension 1
- stress: float32 [6, 64, 32, 256], P(None, 'sample', 'gx', 'gy'), parts along dimension 1
There are 2 independent parts, one for each index of `sample`. A program takes and returns all parts, laid end to end along the dimension named above; each array names one. Nothing has to cross between parts.
All inputs are finite; a program needn't handle non-finite values.
Results may differ from a plain program's by a relative error of at most 0.0039.
Values sent between devices are 32-bit elements; how exact they have to be, the bound alone decides.
No kernel may reach another device: no remote copies, remote signals or barrier semaphores. Data moves between devices by JAX's collectives and lax.ppermute only.
A program may use at most 64 MiB of HBM per device.

v0:
```python
import math

import jax
import jax.numpy as jnp
import numpy as np
from jax import lax
from jax.sharding import PartitionSpec as P

ITERS = 2


def shifted(value, axis, by):
    size = lax.axis_size(axis)
    pairs = [(i, i + by) for i in range(size) if 0 <= i + by < size]
    return lax.ppermute(value, axis, pairs)


def corner_list():
    return [(off_z, off_x, off_y) for off_z in (0, 1) for off_x in (0, 1) for off_y in (0, 1)]


def strain_matrix(point):
    corners = corner_list()
    grads = np.zeros((3, 8))
    for corner, offsets in enumerate(corners):
        for axis in range(3):
            value = 1.0 if offsets[axis] else -1.0
            for other in range(3):
                if other != axis:
                    value = value * (point[other] if offsets[other] else 1.0 - point[other])
            grads[axis, corner] = value
    strain = np.zeros((6, 24))
    for corner in range(8):
        for axis in range(3):
            strain[axis, axis * 8 + corner] = grads[axis, corner]
        strain[3, 0 * 8 + corner] = grads[1, corner]
        strain[3, 1 * 8 + corner] = grads[0, corner]
        strain[4, 1 * 8 + corner] = grads[2, corner]
        strain[4, 2 * 8 + corner] = grads[1, corner]
        strain[5, 0 * 8 + corner] = grads[2, corner]
        strain[5, 2 * 8 + corner] = grads[0, corner]
    return strain


def tables():
    poisson = 0.3
    lame_first = poisson / ((1.0 + poisson) * (1.0 - 2.0 * poisson))
    shear_mod = 1.0 / (2.0 * (1.0 + poisson))
    elastic = np.zeros((6, 6))
    elastic[:3, :3] = lame_first
    for axis in range(3):
        elastic[axis, axis] += 2.0 * shear_mod
        elastic[axis + 3, axis + 3] = shear_mod
    gauss_pts = [0.5 - 0.5 / math.sqrt(3.0), 0.5 + 0.5 / math.sqrt(3.0)]
    stiffness = np.zeros((24, 24))
    for first in gauss_pts:
        for second in gauss_pts:
            for third in gauss_pts:
                strain = strain_matrix((first, second, third))
                stiffness += strain.T @ elastic @ strain / 8.0
    stress_map = elastic @ strain_matrix((0.5, 0.5, 0.5))
    return (jnp.asarray(stiffness, jnp.float32), jnp.asarray(stress_map, jnp.float32))


def element_values(padded, modulus, matrix):
    z_cells, x_cells, y_cells = modulus.shape
    pieces = [
        padded[channel, off_z : off_z + z_cells, off_x : off_x + x_cells, off_y : off_y + y_cells]
        for channel in range(3)
        for off_z, off_x, off_y in corner_list()
    ]
    stacked = jnp.stack(pieces)
    result = jnp.einsum("pq,qzxy->pzxy", matrix, stacked, precision=lax.Precision.HIGHEST)
    return result * modulus


def spread(values, per_corner):
    summed = None
    for corner, (off_z, off_x, off_y) in enumerate(corner_list()):
        corner_part = values[corner::8] if per_corner else values
        placed = jnp.pad(
            corner_part, ((0, 0), (off_z, 1 - off_z), (off_x, 1 - off_x), (off_y, 1 - off_y))
        )
        summed = placed if summed is None else summed + placed
    return summed


def lower_ghost(field_in):
    below = shifted(field_in[:, :, -1:, :], "gx", 1)
    extended = jnp.concatenate([below, field_in], axis=2)
    beside = shifted(extended[:, :, :, -1:], "gy", 1)
    extended = jnp.concatenate([beside, extended], axis=3)
    return jnp.pad(extended, ((0, 0), (1, 0), (0, 0), (0, 0)))


def fold_back(summed):
    arrived = shifted(summed[:, :, :, :1], "gy", -1)
    summed = jnp.concatenate([summed[:, :, :, 1:-1], summed[:, :, :, -1:] + arrived], axis=3)
    arrived = shifted(summed[:, :, :1, :], "gx", -1)
    summed = jnp.concatenate([summed[:, :, 1:-1, :], summed[:, :, -1:, :] + arrived], axis=2)
    return summed[:, 1:]


def local_factor(cells, offset, total):
    nodes = offset + jnp.arange(cells, dtype=jnp.int32) + 1
    return jnp.where(nodes < total, jnp.float32(2.0), jnp.float32(1.0))


def residual_norm(current):
    return lax.psum(jnp.sum(current * current), ("gx", "gy"))


def per_device(body_force, modulus):
    stiffness, stress_map = tables()
    z_cells, x_cells, y_cells = modulus.shape

    def assemble(field_in, matrix, per_corner):
        padded = lower_ghost(field_in)
        return fold_back(spread(element_values(padded, modulus, matrix), per_corner))

    solution_field = jnp.zeros_like(body_force)
    residual = body_force
    direction = body_force
    norm_now = residual_norm(residual)
    for iteration in range(ITERS):
        image_vec = assemble(direction, stiffness, True)
        step_len = norm_now / lax.psum(jnp.sum(direction * image_vec), ("gx", "gy"))
        solution_field = solution_field + step_len * direction
        residual = residual - step_len * image_vec
        norm_next = residual_norm(residual)
        direction = residual + norm_next / norm_now * direction
        norm_now = norm_next
    summed = assemble(solution_field, stress_map, False)
    x_offset = lax.axis_index("gx") * x_cells
    y_offset = lax.axis_index("gy") * y_cells
    counts = (
        local_factor(z_cells, 0, z_cells)[:, None, None]
        * local_factor(x_cells, x_offset, x_cells * lax.axis_size("gx"))[None, :, None]
        * local_factor(y_cells, y_offset, y_cells * lax.axis_size("gy"))[None, None, :]
    )
    stress = summed / counts
    return (solution_field, stress)


def solution(mesh):
    return jax.shard_map(
        per_device,
        mesh=mesh,
        in_specs=(P(None, "sample", "gx", "gy"), P("sample", "gx", "gy")),
        out_specs=(P(None, "sample", "gx", "gy"), P(None, "sample", "gx", "gy")),
        check_vma=False,
    )
```

profile of v0, /device:TPU:0, one launch (start us, length us, event | category | flops | bytes accessed | tf_op | source)
XLA Modules:
  0.0 243.6 jit_solution(11771306178316561756)
XLA Ops:
  1.7 4.8 %collective-permute-start = (f32[3,32,1,128]{3,0,2,1:T(4,128)S(1)}, f32[3,32,1,128]{3,0,2,1:T(4,128)S(1)}, u32[]{:S(2)}, u32[]{:S(2)}) collective-permute-start(f32[3,32,1,128]{3,0,2,1:T(4,128)S(1)} %copy.37), channel_id=1, source_target_pairs={{0,2},{2,4},{4,6},{6,8},{8,10},{10,12},{12,14},{1,3},{3,5},{5,7},{... | collective-permute-start | bytes 147464 | tf_op jit(solution)/shard_map/ppermute | solution.py:15
  14.8 2.5 %stack.9 = f32[24,32,4,128]{3,0,2,1:T(8,128)S(1)} concatenate(f32[1,32,4,128]{3,0,2,1:T(1,128)S(1)} %get-tuple-element.61, f32[1,32,4,128]{3,0,2,1:T(1,128)S(1)} %get-tuple-element.51, f32[1,32,4,128]{3,0,2,1:T(1,128)S(1)} %get-tuple-element.52, f32[1,32,4,128]{3,0,2,1:T(1,128)S(1)} %get-tuple-element.53, f32[1,32,4,128]{3,0,2,1:T(1,128)S(1)} %get-tuple-element.45, ...), dimensions={0} | concatenate | bytes 3145728 | tf_op jit(solution)/shard_map/stack | solution.py:72
  24.0 9.7 %slice.440 = f32[3,32,4,128]{3,0,2,1:T(4,128)} slice(f32[24,32,4,128]{3,0,2,1:T(8,128)S(1)} %multiply_bitcast_fusion.1), slice={[6:24:8], [0:32:1], [0:4:1], [0:128:1]} | slice | bytes 393216 | tf_op jit(solution)/shard_map/slice | solution.py:80
  33.7 9.8 %slice.441 = f32[3,32,4,128]{3,0,2,1:T(4,128)} slice(f32[24,32,4,128]{3,0,2,1:T(8,128)S(1)} %multiply_bitcast_fusion.1), slice={[7:24:8], [0:32:1], [0:4:1], [0:128:1]} | slice | bytes 393216 | tf_op jit(solution)/shard_map/slice | solution.py:80
  43.5 2.2 pad_add_fusion.2
  47.3 2.0 collective-permute-done.2
  51.0 5.2 %collective-permute-done.3 = f32[3,33,1,128]{3,0,2,1:T(4,128)S(1)} collective-permute-done((f32[3,33,1,128]{3,0,2,1:T(4,128)S(1)}, f32[3,33,1,128]{3,0,2,1:T(4,128)S(1)}, u32[]{:S(2)}, u32[]{:S(2)}) %collective-permute-start.3) | collective-permute-done | bytes 50720 | tf_op jit(solution)/shard_map/ppermute | solution.py:15
  57.1 32.9 %all-reduce.27 = (f32[]{:T(128)}, f32[]{:T(128)}) all-reduce(f32[]{:T(128)} %multiply_reduce_fusion.2, f32[]{:T(128)} %multiply_reduce_fusion.1), channel_id=1, replica_groups=mesh['sample'=2,'gx'=8,'gy'=2] {'gx','gy'}, use_global_device_ids=true, to_apply=%region_1.0 | all-reduce | flops 2 | bytes 16 | tf_op jit(solution)/shard_map/psum | solution.py:110
  92.1 30.2 %psum.30 = f32[]{:T(128)} all-reduce(f32[]{:T(128)} %multiply_reduce_fusion), channel_id=1, replica_groups=mesh['sample'=2,'gx'=8,'gy'=2] {'gx','gy'}, use_global_device_ids=true, to_apply=%region_5.6 | all-reduce | flops 1 | bytes 8 | tf_op jit(solution)/shard_map/psum | solution.py:110
  125.1 1.9 collective-permute-done.4
  127.2 1.5 collective-permute-start.5
  131.5 4.6 %stack.10 = f32[24,32,4,128]{3,0,2,1:T(8,128)} concatenate(f32[1,32,4,128]{3,0,2,1:T(1,128)S(1)} %get-tuple-element.43, f32[1,32,4,128]{3,0,2,1:T(1,128)S(1)} %get-tuple-element.27, f32[1,32,4,128]{3,0,2,1:T(1,128)S(1)} %get-tuple-element.28, f32[1,32,4,128]{3,0,2,1:T(1,128)S(1)} %get-tuple-element.29, f32[1,32,4,128]{3,0,2,1:T(1,128)S(1)} %get-tuple-element.42, ...), dimensions={0} | concatenate | bytes 3145728 | tf_op jit(solution)/shard_map/stack | solution.py:72
  136.0 2.8 %multiply_bitcast_fusion = f32[24,32,4,128]{3,0,2,1:T(8,128)S(1)} fusion(f32[24,32,4,128]{3,0,2,1:T(8,128)} %stack.10, f32[24,24,1,1]{1,0,3,2:T(8,128)S(1)} %copy-done.2, f32[32,4,128]{2,1,0:T(4,128)S(1)} %copy-done.1), kind=kOutput, calls=%fused_computation | convolution fusion | flops 113639424 | bytes 3213568 | tf_op jit(solution)/shard_map/pq,qzxy->pzxy/dot_general | solution.py:73
  143.2 9.7 %slice.480 = f32[3,32,4,128]{3,0,2,1:T(4,128)} slice(f32[24,32,4,128]{3,0,2,1:T(8,128)S(1)} %multiply_bitcast_fusion), slice={[5:24:8], [0:32:1], [0:4:1], [0:128:1]} | slice | bytes 393216 | tf_op jit(solution)/shard_map/slice | solution.py:80
  153.0 9.7 %slice.481 = f32[3,32,4,128]{3,0,2,1:T(4,128)} slice(f32[24,32,4,128]{3,0,2,1:T(8,128)S(1)} %multiply_bitcast_fusion), slice={[6:24:8], [0:32:1], [0:4:1], [0:128:1]} | slice | bytes 393216 | tf_op jit(solution)/shard_map/slice | solution.py:80
  162.7 9.8 %slice.482 = f32[3,32,4,128]{3,0,2,1:T(4,128)} slice(f32[24,32,4,128]{3,0,2,1:T(8,128)S(1)} %multiply_bitcast_fusion), slice={[7:24:8], [0:32:1], [0:4:1], [0:128:1]} | slice | bytes 393216 | tf_op jit(solution)/shard_map/slice | solution.py:80
  172.5 2.2 pad_add_fusion.1
  176.4 1.9 collective-permute-done.6
  180.0 5.2 %collective-permute-done.7 = f32[3,33,1,128]{3,0,2,1:T(4,128)S(1)} collective-permute-done((f32[3,33,1,128]{3,0,2,1:T(4,128)S(1)}, f32[3,33,1,128]{3,0,2,1:T(4,128)S(1)}, u32[]{:S(2)}, u32[]{:S(2)}) %collective-permute-start.7) | collective-permute-done | bytes 50720 | tf_op jit(solution)/shard_map/ppermute | solution.py:15
  186.1 30.1 %psum.31 = f32[]{:T(128)} all-reduce(f32[]{:T(128)} %fusion.6), channel_id=1, replica_groups=mesh['sample'=2,'gx'=8,'gy'=2] {'gx','gy'}, use_global_device_ids=true, to_apply=%region_7.8 | all-reduce | flops 1 | bytes 8 | tf_op jit(solution)/shard_map/psum | solution.py:127
  219.0 1.9 collective-permute-done.8
  221.1 1.5 collective-permute-start.9
  225.4 2.5 %stack.11 = f32[24,32,4,128]{3,0,2,1:T(8,128)S(1)} concatenate(f32[1,32,4,128]{3,0,2,1:T(1,128)S(1)} %get-tuple-element.25, f32[1,32,4,128]{3,0,2,1:T(1,128)S(1)} %get-tuple-element.9, f32[1,32,4,128]{3,0,2,1:T(1,128)S(1)} %get-tuple-element.10, f32[1,32,4,128]{3,0,2,1:T(1,128)S(1)} %get-tuple-element.11, f32[1,32,4,128]{3,0,2,1:T(1,128)S(1)} %get-tuple-element.24, ...), dimensions={0} | concatenate | bytes 3145728 | tf_op jit(solution)/shard_map/stack | solution.py:72
  235.6 7.0 %collective-permute-done.11 = f32[6,33,1,128]{3,0,2,1:T(8,128)S(1)} collective-permute-done((f32[6,33,1,128]{3,0,2,1:T(8,128)S(1)}, f32[6,33,1,128]{3,0,2,1:T(8,128)S(1)}, u32[]{:S(2)}, u32[]{:S(2)}) %collective-permute-start.11) | collective-permute-done | bytes 101408 | tf_op jit(solution)/shard_map/ppermute | solution.py:15
  (92 shorter events, 46.8 us)
Async XLA Ops:
  0.6 10.5 %copy-start = (f32[3,32,4,128]{3,2,1,0:T(4,128)S(1)}, f32[3,32,4,128]{3,2,1,0:T(4,128)}, u32[]{:S(2)}) copy-start(f32[3,32,4,128]{3,2,1,0:T(4,128)} %param.4) | copy-start | bytes 589828
  1.7 6.7 %collective-permute-start = (f32[3,32,1,128]{3,0,2,1:T(4,128)S(1)}, f32[3,32,1,128]{3,0,2,1:T(4,128)S(1)}, u32[]{:S(2)}, u32[]{:S(2)}) collective-permute-start(f32[3,32,1,128]{3,0,2,1:T(4,128)S(1)} %copy.37), channel_id=1, source_target_pairs={{0,2},{2,4},{4,6},{6,8},{8,10},{10,12},{12,14},{1,3},{3,5},{5,7},{... | collective-permute-start | bytes 147464 | tf_op jit(solution)/shard_map/ppermute | solution.py:15
  9.8 2.5 %collective-permute-start.1 = (f32[3,32,5,1]{3,0,2,1:T(4,128)S(1)}, f32[3,32,5,1]{3,0,2,1:T(4,128)S(1)}, u32[]{:S(2)}, u32[]{:S(2)}) collective-permute-start(f32[3,32,5,1]{3,0,2,1:T(4,128)S(1)} %slice.524), channel_id=1, source_target_pairs={{0,1},{2,3},{4,5},{6,7},{8,9},{10,11},{12,13},{14,15},{16,17},{18,... | collective-permute-start | bytes 5768 | tf_op jit(solution)/shard_map/ppermute | solution.py:15
  14.8 2.5 %copy-start.1 = (f32[32,4,128]{2,1,0:T(4,128)S(1)}, f32[32,4,128]{2,1,0:T(4,128)}, u32[]{:S(2)}) copy-start(f32[32,4,128]{2,1,0:T(4,128)} %param.5) | copy-start | bytes 196612
  14.8 2.5 %copy-start.2 = (f32[24,24,1,1]{1,0,3,2:T(8,128)S(1)}, f32[24,24,1,1]{1,0,3,2:T(8,128)}, u32[]{:S(2)}) copy-start(f32[24,24,1,1]{1,0,3,2:T(8,128)} %constant.91) | copy-start | bytes 6916
  45.7 3.5 %collective-permute-start.2 = (f32[3,33,5,1]{3,0,2,1:T(4,128)S(1)}, f32[3,33,5,1]{3,0,2,1:T(4,128)S(1)}, u32[]{:S(2)}, u32[]{:S(2)}) collective-permute-start(f32[3,33,5,1]{3,0,2,1:T(4,128)S(1)} %slice.542), channel_id=1, source_target_pairs={{1,0},{3,2},{5,4},{7,6},{9,8},{11,10},{13,12},{15,14},{17,16},{19,... | collective-permute-start | bytes 5948 | tf_op jit(solution)/shard_map/ppermute | solution.py:15
  49.5 6.7 %collective-permute-start.3 = (f32[3,33,1,128]{3,0,2,1:T(4,128)S(1)}, f32[3,33,1,128]{3,0,2,1:T(4,128)S(1)}, u32[]{:S(2)}, u32[]{:S(2)}) collective-permute-start(f32[3,33,1,128]{3,0,2,1:T(4,128)S(1)} %pad_maximum_fusion.6), channel_id=1, source_target_pairs={{2,0},{4,2},{6,4},{8,6},{10,8},{12,10},{14,12},{3,1},{5,3},{7,5},{... | collective-permute-start | bytes 152072 | tf_op jit(solution)/shard_map/ppermute | solution.py:15
  123.8 3.2 %collective-permute-start.4 = (f32[3,32,1,128]{3,0,2,1:T(4,128)S(1)}, f32[3,32,1,128]{3,0,2,1:T(4,128)S(1)}, u32[]{:S(2)}, u32[]{:S(2)}) collective-permute-start(f32[3,32,1,128]{3,0,2,1:T(4,128)S(1)} %slice.547), channel_id=1, source_target_pairs={{0,2},{2,4},{4,6},{6,8},{8,10},{10,12},{12,14},{1,3},{3,5},{5,7},{... | collective-permute-start | bytes 147464 | tf_op jit(solution)/shard_map/ppermute | solution.py:15
  127.2 2.5 %collective-permute-start.5 = (f32[3,32,5,1]{3,0,2,1:T(4,128)S(1)}, f32[3,32,5,1]{3,0,2,1:T(4,128)S(1)}, u32[]{:S(2)}, u32[]{:S(2)}) collective-permute-start(f32[3,32,5,1]{3,0,2,1:T(4,128)S(1)} %fusion.4), channel_id=1, source_target_pairs={{0,1},{2,3},{4,5},{6,7},{8,9},{10,11},{12,13},{14,15},{16,17},{18,... | collective-permute-start | bytes 5768 | tf_op jit(solution)/shard_map/ppermute | solution.py:15
  174.8 3.5 %collective-permute-start.6 = (f32[3,33,5,1]{3,0,2,1:T(4,128)S(1)}, f32[3,33,5,1]{3,0,2,1:T(4,128)S(1)}, u32[]{:S(2)}, u32[]{:S(2)}) collective-permute-start(f32[3,33,5,1]{3,0,2,1:T(4,128)S(1)} %slice.565), channel_id=1, source_target_pairs={{1,0},{3,2},{5,4},{7,6},{9,8},{11,10},{13,12},{15,14},{17,16},{19,... | collective-permute-start | bytes 5948 | tf_op jit(solution)/shard_map/ppermute | solution.py:15
  178.5 6.7 %collective-permute-start.7 = (f32[3,33,1,128]{3,0,2,1:T(4,128)S(1)}, f32[3,33,1,128]{3,0,2,1:T(4,128)S(1)}, u32[]{:S(2)}, u32[]{:S(2)}) collective-permute-start(f32[3,33,1,128]{3,0,2,1:T(4,128)S(1)} %pad_maximum_fusion.5), channel_id=1, source_target_pairs={{2,0},{4,2},{6,4},{8,6},{10,8},{12,10},{14,12},{3,1},{5,3},{7,5},{... | collective-permute-start | bytes 152072 | tf_op jit(solution)/shard_map/ppermute | solution.py:15
  217.7 3.2 %collective-permute-start.8 = (f32[3,32,1,128]{3,0,2,1:T(4,128)S(1)}, f32[3,32,1,128]{3,0,2,1:T(4,128)S(1)}, u32[]{:S(2)}, u32[]{:S(2)}) collective-permute-start(f32[3,32,1,128]{3,0,2,1:T(4,128)S(1)} %slice.570), channel_id=1, source_target_pairs={{0,2},{2,4},{4,6},{6,8},{8,10},{10,12},{12,14},{1,3},{3,5},{5,7},{... | collective-permute-start | bytes 147464 | tf_op jit(solution)/shard_map/ppermute | solution.py:15
  221.1 2.5 %collective-permute-start.9 = (f32[3,32,5,1]{3,0,2,1:T(4,128)S(1)}, f32[3,32,5,1]{3,0,2,1:T(4,128)S(1)}, u32[]{:S(2)}, u32[]{:S(2)}) collective-permute-start(f32[3,32,5,1]{3,0,2,1:T(4,128)S(1)} %fusion.3), channel_id=1, source_target_pairs={{0,1},{2,3},{4,5},{6,7},{8,9},{10,11},{12,13},{14,15},{16,17},{18,... | collective-permute-start | bytes 5768 | tf_op jit(solution)/shard_map/ppermute | solution.py:15
  225.4 2.5 %copy-start.3 = (f32[6,24,1,1]{1,0,3,2:T(8,128)S(1)}, f32[6,24,1,1]{1,0,3,2:T(8,128)}, u32[]{:S(2)}) copy-start(f32[6,24,1,1]{1,0,3,2:T(8,128)} %constant.92) | copy-start | bytes 1732
  230.4 3.1 %collective-permute-start.10 = (f32[6,33,5,1]{1,3,2,0:T(1,128)S(1)}, f32[6,33,5,1]{1,3,2,0:T(1,128)S(1)}, u32[]{:S(2)}, u32[]{:S(2)}) collective-permute-start(f32[6,33,5,1]{1,3,2,0:T(1,128)S(1)} %copy.26), channel_id=1, source_target_pairs={{1,0},{3,2},{5,4},{7,6},{9,8},{11,10},{13,12},{15,14},{17,16},{19,... | collective-permute-start | bytes 11888 | tf_op jit(solution)/shard_map/ppermute | solution.py:15
  234.1 8.4 %collective-permute-start.11 = (f32[6,33,1,128]{3,0,2,1:T(8,128)S(1)}, f32[6,33,1,128]{3,0,2,1:T(8,128)S(1)}, u32[]{:S(2)}, u32[]{:S(2)}) collective-permute-start(f32[6,33,1,128]{3,0,2,1:T(8,128)S(1)} %pad_maximum_fusion.4), channel_id=1, source_target_pairs={{2,0},{4,2},{6,4},{8,6},{10,8},{12,10},{14,12},{3,1},{5,3},{7,5},{... | collective-permute-start | bytes 304136 | tf_op jit(solution)/shard_map/ppermute | solution.py:15
where the time goes:
time: 244 us
  blocking collectives  93.2 us (38%)
  local copies, waits for them, and re-layouts  78 us (32%)
  waiting for transfers between devices  28.7 us (12%)
  starting transfers between devices  19.5 us (8%)
  other arithmetic  13.8 us (6%)
  matrix products  5.21 us (2%)
  between operations  5.18 us (2%)
    psum x2, blocking collectives, residual_norm(): return lax.psum(jnp.sum(current * current), ('gx', 'gy'))  63.1 us
    slice x16, local copies, waits for them, and re-layouts, spread(): corner_part = values[corner::8] if per_corner else values  58.2 us
    psum x1, blocking collectives, per_device(): step_len = norm_now / lax.psum(jnp.sum(direction * image_vec), ('gx', 'gy'))  30.1 us
    ppermute x12, waiting for transfers between devices, shifted(): return lax.ppermute(value, axis, pairs)  28.7 us
    ppermute x12, starting transfers between devices, shifted(): return lax.ppermute(value, axis, pairs)  19.5 us
    another operation x3, local copies, waits for them, and re-layouts, element_values(): stacked = jnp.stack(pieces)  9.54 us
    add x3, other arithmetic, spread(): summed = placed if summed is None else summed + placed  5.56 us
    dot_general x3, matrix products, element_values(): jnp.einsum('pq,qzxy->pzxy', matrix, stacked, precision=lax.Precision.HIGH...  5.21 us
  transfers between devices with their start and end apart: 12, of which 12 were waited for; matrix products, arithmetic and copies ran while one was open for 2% of the time, Pallas kernels for 0%

commit v1 on v0

v1 whole, which is shorter than its diff:
```python
import functools

import jax
import jax.numpy as jnp
from jax import lax
from jax.experimental import pallas as pl
from jax.experimental.pallas import tpu as pltpu
from jax.sharding import PartitionSpec as P

POISSON = 0.3
LAME = POISSON / ((1.0 + POISSON) * (1.0 - 2.0 * POISSON))
SHEAR = 1.0 / (2.0 * (1.0 + POISSON))
RATIO = LAME / SHEAR
ONE = SHEAR / 16.0
TWO = SHEAR / 48.0
THREE = (LAME + 4.0 * SHEAR) / 144.0

VMEM = pl.BlockSpec(memory_space=pltpu.VMEM)
LIMIT = pltpu.CompilerParams(vmem_limit_bytes=48 << 20)


def lanes(shape):
    return lax.broadcasted_iota(jnp.int32, shape, len(shape) - 1)


def from_left(first, second):
    edge = lanes(first.shape) == 0
    turned, turned2 = pltpu.roll(first, 1, 1), pltpu.roll(second, 1, 1)
    return jnp.where(edge, 0.0, turned), jnp.where(edge, turned, turned2)


def from_right(first, second):
    edge = lanes(first.shape) == first.shape[1] - 1
    turned, turned2 = (pltpu.roll(v, v.shape[1] - 1, 1) for v in (first, second))
    return jnp.where(edge, turned2, turned), jnp.where(edge, 0.0, turned2)


def pack_kernel(force_ref, modulus_ref, own_ref, same_ref, cross_ref):
    core = lax.axis_index("gy")
    cells = own_ref.shape[2]

    def plane(field, x):
        rows = pl.ds(x, cells, stride=4)
        return force_ref[field, rows, :] if field < 3 else modulus_ref[rows, :]

    for field in range(4):
        for x in range(4):
            own_ref[x, field] = plane(field, x)
        for i in range(2):
            same_ref[i, field] = plane(field, 2 * (1 - core) + i)
            cross_ref[i, field] = plane(field, 2 * core + i)


def gather_planes(own_ref, mate_ref, same_ref, cross_ref, node_ref, elem_ref):
    core = lax.axis_index("gy")
    cells = own_ref.shape[2]
    node_ref[:, :, :, 0:8, :] = jnp.zeros((6, 3, 2, 8, own_ref.shape[3]), jnp.float32)
    for x in range(4):
        at = 2 * (1 - core) + x
        for ref, block in ((own_ref, core), (mate_ref, 1 - core)):
            for field in range(3):
                node_ref[at, field, block, 8 : 8 + cells, :] = ref[x, field]
            elem_ref[at, block] = ref[x, 3]
    for x in range(2):
        at = 4 * core + x
        for ref, block in ((same_ref, core), (cross_ref, 1 - core)):
            for field in range(3):
                node_ref[at, field, block, 8 : 8 + cells, :] = ref[x, field]
            elem_ref[at, block] = ref[x, 3]


def plane_modes(read, cells):
    sums, diffs = [], []
    for block in range(2):
        high, low = read(block, 8, cells), read(block, 7, cells)
        sums.append(high + low)
        diffs.append(high - low)
    sums_left, diffs_left = from_left(*sums), from_left(*diffs)
    out = []
    for block in range(2):
        s, d, sl, dl = sums[block], diffs[block], sums_left[block], diffs_left[block]
        out.append((s + sl, d + dl, s - sl, d - dl))
    return out


def element_modes(low, high):
    found = []
    for component in range(3):
        modes = {}
        for kind, (z, y) in enumerate(((0, 0), (1, 0), (0, 1), (1, 1))):
            lo, hi = low[component][kind], high[component][kind]
            if (z, y) != (0, 0):
                modes[z, 0, y] = hi + lo
            modes[z, 1, y] = hi - lo
        found.append(modes)
    return found


def mode_forces(modes, modulus):
    u, v, w = modes
    one, two, three = modulus * ONE, modulus * TWO, modulus * THREE
    trace = RATIO * (u[1, 0, 0] + v[0, 1, 0] + w[0, 0, 1])
    shear_zx = one * (u[0, 1, 0] + v[1, 0, 0])
    shear_xy = one * (v[0, 0, 1] + w[0, 1, 0])
    shear_zy = one * (u[0, 0, 1] + w[1, 0, 0])
    trace_z = RATIO * (v[1, 1, 0] + w[1, 0, 1])
    trace_x = RATIO * (u[1, 1, 0] + w[0, 1, 1])
    trace_y = RATIO * (u[1, 0, 1] + v[0, 1, 1])
    mixed_zx = u[0, 1, 1] + v[1, 0, 1]
    mixed_xy = v[1, 0, 1] + w[1, 1, 0]
    mixed_zy = u[0, 1, 1] + w[1, 1, 0]
    return (
        {
            (1, 0, 0): one * (trace + 2.0 * u[1, 0, 0]),
            (0, 1, 0): shear_zx,
            (0, 0, 1): shear_zy,
            (1, 1, 0): two * (trace_x + 3.0 * u[1, 1, 0]),
            (1, 0, 1): two * (trace_y + 3.0 * u[1, 0, 1]),
            (0, 1, 1): two * (mixed_zx + mixed_zy),
            (1, 1, 1): three * u[1, 1, 1],
        },
        {
            (0, 1, 0): one * (trace + 2.0 * v[0, 1, 0]),
            (1, 0, 0): shear_zx,
            (0, 0, 1): shear_xy,
            (1, 1, 0): two * (trace_z + 3.0 * v[1, 1, 0]),
            (0, 1, 1): two * (trace_y + 3.0 * v[0, 1, 1]),
            (1, 0, 1): two * (mixed_zx + mixed_xy),
            (1, 1, 1): three * v[1, 1, 1],
        },
        {
            (0, 0, 1): one * (trace + 2.0 * w[0, 0, 1]),
            (1, 0, 0): shear_zy,
            (0, 1, 0): shear_xy,
            (1, 0, 1): two * (trace_z + 3.0 * w[1, 0, 1]),
            (0, 1, 1): two * (trace_x + 3.0 * w[0, 1, 1]),
            (1, 1, 0): two * (mixed_xy + mixed_zy),
            (1, 1, 1): three * w[1, 1, 1],
        },
    )


def mode_energy(modes, modulus):
    u, v, w = modes
    square = lambda value: value * value
    a, b, c = u[1, 0, 0], v[0, 1, 0], w[0, 0, 1]
    one = RATIO * square(a + b + c) + 2.0 * (square(a) + square(b) + square(c))
    one = one + square(u[0, 1, 0] + v[1, 0, 0]) + square(v[0, 0, 1] + w[0, 1, 0]) + square(u[0, 0, 1] + w[1, 0, 0])
    d, e, f = u[1, 1, 0], u[1, 0, 1], v[1, 1, 0]
    g, h, k = v[0, 1, 1], w[1, 0, 1], w[0, 1, 1]
    two = RATIO * (square(f + h) + square(d + k) + square(e + g))
    two = two + 3.0 * (square(d) + square(e) + square(f) + square(g) + square(h) + square(k))
    m, n, o = u[0, 1, 1], v[1, 0, 1], w[1, 1, 0]
    two = two + square(m + n) + square(n + o) + square(m + o)
    three = square(u[1, 1, 1]) + square(v[1, 1, 1]) + square(w[1, 1, 1])
    return modulus * (ONE * one + TWO * two + THREE * three)


def spread_kernel(own_ref, mate_ref, same_ref, cross_ref, image_ref, sums_ref, node_ref, elem_ref, mode_ref, part_ref):
    core, slab = lax.axis_index("gy"), lax.axis_index("gx")
    cells, width = own_ref.shape[2:]
    tiles = cells // 8
    gather_planes(own_ref, mate_ref, same_ref, cross_ref, node_ref, elem_ref)

    @pl.loop(0, 6)
    def _(j):
        for field in range(3):
            read = lambda block, start, size: node_ref[j, field, block, start : start + size, :]
            for block, kinds in enumerate(plane_modes(read, cells)):
                for kind, value in enumerate(kinds):
                    mode_ref[j, 4 * field + kind, block] = value

    part_ref[:, :, :, cells : cells + 8, :] = jnp.zeros((4, 12, 2, 8, width), jnp.float32)

    @pl.loop(0, 2 * tiles)
    def _(t):
        block, rows = t // tiles, pl.ds(pl.multiple_of((t % tiles) * 8, 8), 8)
        load = lambda j: [[mode_ref[j, 4 * f + k, block, rows, :] for k in range(4)] for f in range(3)]
        low, kept = load(0), None
        for j in range(1, 6):
            high = load(j)
            forces = mode_forces(element_modes(low, high), elem_ref[j, block, rows, :])
            after = []
            for f in range(3):
                upper, lower = [], []
                for z, y in ((0, 0), (1, 0), (0, 1), (1, 1)):
                    diff, both = forces[f][z, 1, y], forces[f].get((z, 0, y))
                    upper.append(diff if both is None else both + diff)
                    lower.append(-diff if both is None else both - diff)
                after.append(upper)
                if kept is not None:
                    ss, ds, sd, dd = (p + q for p, q in zip(kept[f], lower))
                    here, back = ss + ds, ss - ds
                    here_y, back_y = sd + dd, sd - dd
                    part_ref[j - 2, 4 * f, block, rows, :] = here + here_y
                    part_ref[j - 2, 4 * f + 1, block, rows, :] = here - here_y
                    part_ref[j - 2, 4 * f + 2, block, rows, :] = back + back_y
                    part_ref[j - 2, 4 * f + 3, block, rows, :] = back - back_y
            low, kept = high, after

    image_ref[:, :, :, 0:8, :] = jnp.zeros((4, 3, 2, 8, width), jnp.float32)
    clamped = jnp.where((core == 0) & (slab == 0), 0.0, 1.0)
    fold = lambda value: value.reshape(tiles, 8, width).sum(0)
    zero = jnp.zeros((8, width), jnp.float32)
    norm, cross, square = zero, zero, zero
    for j in range(4):
        for f in range(3):
            here = lambda k, block: part_ref[j, 4 * f + k, block, 0:cells, :]
            above = lambda k, block: part_ref[j, 4 * f + k, block, 1 : cells + 1, :]
            beside = from_right(*(here(1, block) + above(3, block) for block in range(2)))
            for block in range(2):
                value = here(0, block) + above(2, block) + beside[block]
                if j == 0:
                    value = value * clamped
                image_ref[j, f, block, 8 : 8 + cells, :] = value
                if j in (1, 2):
                    force = node_ref[j + 1, f, block, 8 : 8 + cells, :]
                    norm = norm + fold(force * force)
                    cross = cross + fold(force * value)
                    square = square + fold(value * value)

    @pl.loop(0, 3)
    def _(j):
        for field in range(3):
            read = lambda block, start, size: image_ref[j, field, block, start : start + size, :]
            for block, kinds in enumerate(plane_modes(read, cells)):
                for kind, value in enumerate(kinds):
                    mode_ref[j, 4 * field + kind, block] = value

    def energy_of(t, total):
        block, rows = t // tiles, pl.ds(pl.multiple_of((t % tiles) * 8, 8), 8)
        load = lambda j: [[mode_ref[j, 4 * f + k, block, rows, :] for k in range(4)] for f in range(3)]
        low = load(0)
        for j in range(1, 3):
            high = load(j)
            total = total + mode_energy(element_modes(low, high), elem_ref[j + 1, block, rows, :])
            low = high
        return total

    energy = lax.fori_loop(0, 2 * tiles, energy_of, zero)
    row = lax.broadcasted_iota(jnp.int32, (8, width), 0)
    packed = zero
    for k, value in enumerate((norm, cross, square, energy)):
        packed = jnp.where(row == k, jnp.sum(value, axis=0, keepdims=True), packed)
    sums_ref[...] = jnp.broadcast_to(packed[None], sums_ref.shape)


def stress_kernel(own_ref, mate_ref, same_ref, cross_ref, image_ref, keep_ref, send_ref, node_ref, elem_ref, mode_ref, part_ref):
    core, slab = lax.axis_index("gy"), lax.axis_index("gx")
    last = (core == 1) & (slab == lax.axis_size("gx") - 1)
    cells, width = own_ref.shape[2:]
    tiles = cells // 8
    gather_planes(own_ref, mate_ref, same_ref, cross_ref, node_ref, elem_ref)
    part_ref[:, :, :, cells : cells + 8, :] = jnp.zeros((2, 6, 2, 8, width), jnp.float32)
    row = lax.broadcasted_iota(jnp.int32, (cells, width), 0)
    lane = lanes((cells, width))

    for which in range(2):

        @pl.loop(0, 4)
        def _(j):
            for field in range(3):
                if which == 0:
                    read = lambda block, start, size: node_ref[j + 1, field, block, start : start + size, :]
                else:
                    read = lambda block, start, size: image_ref[j, field, block, start : start + size, :]
                for block, kinds in enumerate(plane_modes(read, cells)):
                    for kind in range(3):
                        mode_ref[j, 3 * field + kind, block] = kinds[kind]

        @pl.loop(0, 2 * tiles)
        def _(t):
            block, rows = t // tiles, pl.ds(pl.multiple_of((t % tiles) * 8, 8), 8)
            load = lambda j: [[mode_ref[j, 3 * f + k, block, rows, :] for k in range(3)] for f in range(3)]
            low, kept = load(0), None
            for j in range(1, 4):
                high = load(j)
                by_z = [high[f][1] + low[f][1] for f in range(3)]
                by_x = [high[f][0] - low[f][0] for f in range(3)]
                by_y = [high[f][2] + low[f][2] for f in range(3)]
                scaled = elem_ref[j + 1, block, rows, :] * (0.25 * SHEAR)
                trace = RATIO * (by_z[0] + by_x[1] + by_y[2])
                now = [
                    scaled * (trace + 2.0 * by_z[0]),
                    scaled * (trace + 2.0 * by_x[1]),
                    scaled * (trace + 2.0 * by_y[2]),
                    scaled * (by_x[0] + by_z[1]),
                    scaled * (by_y[1] + by_x[2]),
                    scaled * (by_y[0] + by_z[2]),
                ]
                if kept is not None:
                    for k in range(6):
                        part_ref[j - 2, k, block, rows, :] = kept[k] + now[k]
                low, kept = high, now

        for i in range(2):
            count_x = jnp.where(last, 1.0, 0.5) if i == 1 else 0.5
            count_z = jnp.where(row == cells - 1, 1.0, 0.5) * count_x
            counts = (count_z * 0.5, count_z * jnp.where(lane == width - 1, 1.0, 0.5))
            for k in range(6):
                both = [part_ref[i, k, block, 0:cells, :] + part_ref[i, k, block, 1 : cells + 1, :] for block in range(2)]
                beside = from_right(*both)
                values = [(both[block] + beside[block]) * counts[block] for block in range(2)]
                keep_ref[i, 6 * which + k] = jnp.where(core == 0, values[0], values[1])
                send_ref[i, 6 * which + k] = jnp.where(core == 0, values[1], values[0])
    for i in range(2):
        for f in range(3):
            keep_ref[i, 12 + f] = image_ref[i + 1, f, core, 8 : 8 + cells, :]
            send_ref[i, 12 + f] = image_ref[i + 1, f, 1 - core, 8 : 8 + cells, :]


def combine_kernel(sums_ref, own_ref, keep_ref, mate_ref, field_ref, stress_ref):
    core = lax.axis_index("gy")
    cells = own_ref.shape[2]
    total = jnp.sum(jnp.sum(sums_ref[...], axis=0), axis=1, keepdims=True)
    norm, cross, square, energy = (total[k : k + 1, :] for k in range(4))
    first = norm / cross
    norm_next = norm - 2.0 * first * cross + first * first * square
    ratio = norm_next / norm
    grown = 1.0 + ratio
    curvature = grown * grown * cross - 2.0 * grown * first * square + first * first * energy
    second = norm_next / curvature
    weight = first + second * grown
    weight_image = -second * first
    shape = (cells, own_ref.shape[3])
    weight = jnp.broadcast_to(weight, shape)
    weight_image = jnp.broadcast_to(weight_image, shape)
    for ref, base in ((keep_ref, 2 * core), (mate_ref, 2 * (1 - core))):
        for i in range(2):
            rows = pl.ds(base + i, cells, stride=4)
            for f in range(3):
                field_ref[f, rows, :] = weight * own_ref[base + i, f] + weight_image * ref[i, 12 + f]
            for k in range(6):
                stress_ref[k, rows, :] = weight * ref[i, k] + weight_image * ref[i, 6 + k]


def per_device(body_force, modulus):
    cells, planes, width = modulus.shape
    slabs, cores = lax.axis_size("gx"), lax.axis_size("gy")
    assert planes == 4 and cores == 2 and cells % 8 == 0
    both = ("gx", "gy")
    f32 = jnp.float32
    shape = lambda *dims: jax.ShapeDtypeStruct(dims, f32)

    own, same, cross = pl.pallas_call(
        pack_kernel,
        out_shape=(shape(4, 4, cells, width), shape(2, 4, cells, width), shape(2, 4, cells, width)),
        in_specs=[VMEM] * 2,
        out_specs=[VMEM] * 3,
        compiler_params=LIMIT,
        name="pack",
    )(body_force.reshape(3, cells * 4, width), modulus.reshape(cells * 4, width))

    up = [(2 * g, 2 * g + 2) for g in range(slabs - 1)]
    down = [(2 * g + 3, 2 * g + 1) for g in range(slabs - 1)]
    pairs = [(2 * g + 1, 2 * g + 2) for g in range(slabs - 1)]
    mate = lax.ppermute(own, "gy", [(0, 1), (1, 0)])
    cross_in = lax.ppermute(cross, both, pairs + [(q, p) for p, q in pairs])
    same_in = lax.ppermute(same, both, up + down)
    slabs_in = (own, mate, same_in, cross_in)

    node = pltpu.VMEM((6, 3, 2, cells + 8, width), f32)
    elem = pltpu.VMEM((6, 2, cells, width), f32)
    image, sums = pl.pallas_call(
        spread_kernel,
        out_shape=(shape(4, 3, 2, cells + 8, width), shape(slabs * cores, 8, width)),
        in_specs=[VMEM] * 4,
        out_specs=[VMEM] * 2,
        scratch_shapes=[
            node,
            elem,
            pltpu.VMEM((6, 12, 2, cells, width), f32),
            pltpu.VMEM((4, 12, 2, cells + 8, width), f32),
        ],
        compiler_params=LIMIT,
        name="spread",
    )(*slabs_in)

    sums = lax.all_to_all(sums, both, 0, 0)
    keep, send = pl.pallas_call(
        stress_kernel,
        out_shape=(shape(2, 15, cells, width), shape(2, 15, cells, width)),
        in_specs=[VMEM] * 5,
        out_specs=[VMEM] * 2,
        scratch_shapes=[
            node,
            elem,
            pltpu.VMEM((4, 9, 2, cells, width), f32),
            pltpu.VMEM((2, 6, 2, cells + 8, width), f32),
        ],
        compiler_params=LIMIT,
        cost_estimate=pl.CostEstimate(flops=10_000_000, bytes_accessed=3_000_000, transcendentals=0),
        name="stress",
    )(*slabs_in, image)
    received = lax.ppermute(send, "gy", [(0, 1), (1, 0)])

    field, stress = pl.pallas_call(
        combine_kernel,
        out_shape=(shape(3, cells * 4, width), shape(6, cells * 4, width)),
        in_specs=[VMEM] * 4,
        out_specs=[VMEM] * 2,
        compiler_params=LIMIT,
        name="combine",
    )(sums, own, keep, received)
    return field.reshape(3, cells, 4, width), stress.reshape(6, cells, 4, width)


def solution(mesh):
    return jax.shard_map(
        per_device,
        mesh=mesh,
        in_specs=(P(None, "sample", "gx", "gy"), P("sample", "gx", "gy")),
        out_specs=(P(None, "sample", "gx", "gy"), P(None, "sample", "gx", "gy")),
        check_vma=False,
    )
```

time: 244 us -> 32.6 us (0.13)
  blocking collectives: 93.2 us -> 12.6 us
  local copies, waits for them, and re-layouts: 78 us -> 1.76 us
  waiting for transfers between devices: 28.7 us -> 3.2 us
  other arithmetic: 13.8 us -> 0 us
  starting transfers between devices: 19.5 us -> 8.67 us
  Pallas kernels: 0 us -> 5.51 us
  matrix products: 5.21 us -> 0 us
  between operations: 5.18 us -> 0.68 us
    psum x3 -> x0, blocking collectives: 93.2 us -> none  [the longest x2 63.1 us: residual_norm(): return lax.psum(jnp.sum(current * current), ('gx', 'gy'))]
    slice x34 -> x0, local copies, waits for them, and re-layouts: 65.4 us -> none  [the longest x16 58.2 us: spread(): corner_part = values[corner::8] if per_corner else values]
    ppermute x12 -> x4, waiting for transfers between devices: 28.7 us -> 3.2 us  [the longest x1 3.19 us: per_device(): same_in = lax.ppermute(same, both, up + down)]
    all_to_all x0 -> x1, blocking collectives: none -> 12.6 us  [per_device(): sums = lax.all_to_all(sums, both, 0, 0)]
    ppermute x12 -> x4, starting transfers between devices: 19.5 us -> 8.67 us  [the longest x1 4.41 us: per_device(): same_in = lax.ppermute(same, both, up + down)]
    another operation x3 -> x0, local copies, waits for them, and re-layouts: 9.54 us -> none  [element_values(): stacked = jnp.stack(pieces)]
    add x11 -> x0, other arithmetic: 6.53 us -> none  [the longest x3 5.56 us: spread(): summed = placed if summed is None else summed + placed]
    pallas_call x0 -> x4, Pallas kernels: none -> 5.51 us  [the longest x1 2.54 us: per_device(): pl.pallas_call(spread_kernel, out_shape=(shape(4, 3, 2, cells + 8, width)...]
  transfers between devices with their start and end apart: 12 -> 4, of which waited for: 12 -> 1; matrix products, arithmetic and copies ran while one was open for 2% -> 0% of each run, Pallas kernels for 0% -> 0%
where the time goes in v1:
time: 32.6 us; the launch traced here: 32.4 us
  blocking collectives  12.6 us (39%)
  starting transfers between devices  8.67 us (27%)
  Pallas kernels  5.51 us (17%)
  waiting for transfers between devices  3.2 us (10%)
  local copies, waits for them, and re-layouts  1.76 us (5%)
  between operations  0.68 us (2%)
    all_to_all x1, blocking collectives, per_device(): sums = lax.all_to_all(sums, both, 0, 0)  12.6 us
    ppermute x1, starting transfers between devices, per_device(): same_in = lax.ppermute(same, both, up + down)  4.41 us
    ppermute x1, waiting for transfers between devices, per_device(): same_in = lax.ppermute(same, both, up + down)  3.19 us
    ppermute x1, starting transfers between devices, per_device(): received = lax.ppermute(send, 'gy', [(0, 1), (1, 0)])  3.07 us
    pallas_call x1, Pallas kernels, per_device(): pl.pallas_call(spread_kernel, out_shape=(shape(4, 3, 2, cells + 8, width)...  2.54 us
    pallas_call x1, Pallas kernels, per_device(): pl.pallas_call(stress_kernel, out_shape=(shape(2, 15, cells, width), shap...  1.9 us
    unnamed x4, local copies, waits for them, and re-layouts  1.76 us
    pallas_call x1, Pallas kernels, per_device(): pl.pallas_call(combine_kernel, out_shape=(shape(3, cells * 4, width), sha...  1.03 us
  transfers between devices with their start and end apart: 4, of which 1 were waited for; matrix products, arithmetic and copies ran while one was open for 0% of the time, Pallas kernels for 0%

profile of v1, /device:TPU:0, one launch (start us, length us, event | category | flops | bytes accessed | tf_op | source)
XLA Modules:
  0.0 32.4 jit_solution(16164994195478669095)
XLA Ops:
  0.6 0.0 copy-start
  0.6 0.9 %copy-done = f32[3,32,4,128]{3,2,1,0:T(4,128)S(1)} copy-done((f32[3,32,4,128]{3,2,1,0:T(4,128)S(1)}, f32[3,32,4,128]{3,2,1,0:T(4,128)}, u32[]{:S(2)}) %copy-start) | copy-done | bytes 196632
  1.6 0.0 copy-start.1
  1.6 0.8 %copy-done.1 = f32[32,4,128]{2,1,0:T(4,128)S(1)} copy-done((f32[32,4,128]{2,1,0:T(4,128)S(1)}, f32[32,4,128]{2,1,0:T(4,128)}, u32[]{:S(2)}) %copy-start.1) | copy-done | bytes 65560
  2.4 0.5 %collective-permute-start = (f32[4,4,32,128]{3,2,1,0:T(8,128)S(1)}, f32[4,4,32,128]{3,2,1,0:T(8,128)S(1)}, u32[]{:S(2)}, u32[]{:S(2)}) collective-permute-start(f32[4,4,32,128]{3,2,1,0:T(8,128)S(1)} %get-tuple-element.11.own_ref), channel_id=1, source_target_pairs={{0,1},{1,0},{2,3},{3,2},{4,5},{5,4},{6,7},{7,6},{8,9},{9,8},{10,11... | collective-permute-start | bytes 786440 | tf_op jit(solution)/shard_map/ppermute | solution.py:357
  3.0 4.4 %collective-permute-start.1 = (f32[2,4,32,128]{3,2,1,0:T(8,128)S(1)}, f32[2,4,32,128]{3,2,1,0:T(8,128)S(1)}, u32[]{:S(2)}, u32[]{:S(2)}) collective-permute-start(f32[2,4,32,128]{3,2,1,0:T(8,128)S(1)} %get-tuple-element.12), channel_id=1, source_target_pairs={{0,2},{2,4},{4,6},{6,8},{8,10},{10,12},{12,14},{3,1},{5,3},{7,5},{... | collective-permute-start | bytes 393224 | tf_op jit(solution)/shard_map/ppermute | solution.py:359
  7.4 0.7 %collective-permute-start.2 = (f32[2,4,32,128]{3,2,1,0:T(8,128)S(1)}, f32[2,4,32,128]{3,2,1,0:T(8,128)S(1)}, u32[]{:S(2)}, u32[]{:S(2)}) collective-permute-start(f32[2,4,32,128]{3,2,1,0:T(8,128)S(1)} %get-tuple-element.13), channel_id=1, source_target_pairs={{1,2},{3,4},{5,6},{7,8},{9,10},{11,12},{13,14},{2,1},{4,3},{6,5},{... | collective-permute-start | bytes 393224 | tf_op jit(solution)/shard_map/ppermute | solution.py:358
  8.1 3.2 %collective-permute-done.1.same_ref = f32[2,4,32,128]{3,2,1,0:T(8,128)S(1)} collective-permute-done((f32[2,4,32,128]{3,2,1,0:T(8,128)S(1)}, f32[2,4,32,128]{3,2,1,0:T(8,128)S(1)}, u32[]{:S(2)}, u32[]{:S(2)}) %collective-permute-start.1) | collective-permute-done | bytes 131104 | tf_op jit(solution)/shard_map/ppermute | solution.py:359
  11.2 0.0 collective-permute-done.2.cross_ref
  11.2 0.0 collective-permute-done.mate_ref
  11.2 2.5 %spread.1 = (f32[4,3,2,40,128]{4,3,2,1,0:T(8,128)S(1)}, f32[16,8,128]{2,1,0:T(8,128)S(1)}) custom-call(f32[4,4,32,128]{3,2,1,0:T(8,128)S(1)} %get-tuple-element.11.own_ref, f32[4,4,32,128]{3,2,1,0:T(8,128)S(1)} %collective-permute-done.mate_ref, f32[2,4,32,128]{3,2,1,0:T(8,128)S(1)} %collective-permute-done.1.same_ref, ...), custom_call_target="tpu_custom_call" | custom-call | tf_op jit(solution)/shard_map/spread/pallas_call | solution.py:364
  13.8 1.9 %stress.1 = (f32[2,15,32,128]{3,2,1,0:T(8,128)S(1)}, f32[2,15,32,128]{3,2,1,0:T(8,128)S(1)}) custom-call(f32[4,4,32,128]{3,2,1,0:T(8,128)S(1)} %get-tuple-element.11.own_ref, f32[4,4,32,128]{3,2,1,0:T(8,128)S(1)} %collective-permute-done.mate_ref, f32[2,4,32,128]{3,2,1,0:T(8,128)S(1)} %collective-permute-done.1.same_ref, ...), custom_call_target="tpu_custom_call" | custom-call | flops 10000000 | bytes 3000000 | tf_op jit(solution)/shard_map/stress/pallas_call | solution.py:380
  15.7 3.1 %collective-permute-start.3 = (f32[2,15,32,128]{3,2,1,0:T(8,128)S(1)}, f32[2,15,32,128]{3,2,1,0:T(8,128)S(1)}, u32[]{:S(2)}, u32[]{:S(2)}) collective-permute-start(f32[2,15,32,128]{3,2,1,0:T(8,128)S(1)} %get-tuple-element.17), channel_id=1, source_target_pairs={{0,1},{1,0},{2,3},{3,2},{4,5},{5,4},{6,7},{7,6},{8,9},{9,8},{10,11... | collective-permute-start | bytes 1474568 | tf_op jit(solution)/shard_map/ppermute | solution.py:395
  18.8 12.6 %all_to_all.5.sums_ref = f32[16,8,128]{2,1,0:T(8,128)S(1)} all-to-all(f32[16,8,128]{2,1,0:T(8,128)S(1)} %get-tuple-element.14), channel_id=1, replica_groups=mesh['sample'=2,'gx'=8,'gy'=2] {'gx','gy'}, dimensions={0} | all-to-all | bytes 131072 | tf_op jit(solution)/shard_map/all_to_all | solution.py:379
  31.3 0.0 collective-permute-done.3.mate_ref
  31.3 1.0 %combine.1 = (f32[3,128,128]{2,1,0:T(8,128)}, f32[6,128,128]{2,1,0:T(8,128)}) custom-call(f32[16,8,128]{2,1,0:T(8,128)S(1)} %all_to_all.5.sums_ref, f32[4,4,32,128]{3,2,1,0:T(8,128)S(1)} %get-tuple-element.11.own_ref, f32[2,15,32,128]{3,2,1,0:T(8,128)S(1)} %get-tuple-element.16.keep_ref, f32[2,15,32,128]{3,2,1,0:T(8,128)S(1)} %collective-permute-done.3.mate_ref), custom_call_target="tpu_custom_call" | custom-call | tf_op jit(solution)/shard_map/combine/pallas_call | solution.py:397
  (1 shorter events, 0.0 us)
Async XLA Ops:
  0.6 0.9 %copy-start = (f32[3,32,4,128]{3,2,1,0:T(4,128)S(1)}, f32[3,32,4,128]{3,2,1,0:T(4,128)}, u32[]{:S(2)}) copy-start(f32[3,32,4,128]{3,2,1,0:T(4,128)} %param.2) | copy-start | bytes 589828
  1.6 0.8 %copy-start.1 = (f32[32,4,128]{2,1,0:T(4,128)S(1)}, f32[32,4,128]{2,1,0:T(4,128)}, u32[]{:S(2)}) copy-start(f32[32,4,128]{2,1,0:T(4,128)} %param.3) | copy-start | bytes 196612
  2.4 8.8 %collective-permute-start = (f32[4,4,32,128]{3,2,1,0:T(8,128)S(1)}, f32[4,4,32,128]{3,2,1,0:T(8,128)S(1)}, u32[]{:S(2)}, u32[]{:S(2)}) collective-permute-start(f32[4,4,32,128]{3,2,1,0:T(8,128)S(1)} %get-tuple-element.11.own_ref), channel_id=1, source_target_pairs={{0,1},{1,0},{2,3},{3,2},{4,5},{5,4},{6,7},{7,6},{8,9},{9,8},{10,11... | collective-permute-start | bytes 786440 | tf_op jit(solution)/shard_map/ppermute | solution.py:357
  3.0 8.3 %collective-permute-start.1 = (f32[2,4,32,128]{3,2,1,0:T(8,128)S(1)}, f32[2,4,32,128]{3,2,1,0:T(8,128)S(1)}, u32[]{:S(2)}, u32[]{:S(2)}) collective-permute-start(f32[2,4,32,128]{3,2,1,0:T(8,128)S(1)} %get-tuple-element.12), channel_id=1, source_target_pairs={{0,2},{2,4},{4,6},{6,8},{8,10},{10,12},{12,14},{3,1},{5,3},{7,5},{... | collective-permute-start | bytes 393224 | tf_op jit(solution)/shard_map/ppermute | solution.py:359
  7.4 3.9 %collective-permute-start.2 = (f32[2,4,32,128]{3,2,1,0:T(8,128)S(1)}, f32[2,4,32,128]{3,2,1,0:T(8,128)S(1)}, u32[]{:S(2)}, u32[]{:S(2)}) collective-permute-start(f32[2,4,32,128]{3,2,1,0:T(8,128)S(1)} %get-tuple-element.13), channel_id=1, source_target_pairs={{1,2},{3,4},{5,6},{7,8},{9,10},{11,12},{13,14},{2,1},{4,3},{6,5},{... | collective-permute-start | bytes 393224 | tf_op jit(solution)/shard_map/ppermute | solution.py:358
  15.7 15.6 %collective-permute-start.3 = (f32[2,15,32,128]{3,2,1,0:T(8,128)S(1)}, f32[2,15,32,128]{3,2,1,0:T(8,128)S(1)}, u32[]{:S(2)}, u32[]{:S(2)}) collective-permute-start(f32[2,15,32,128]{3,2,1,0:T(8,128)S(1)} %get-tuple-element.17), channel_id=1, source_target_pairs={{0,1},{1,0},{2,3},{3,2},{4,5},{5,4},{6,7},{7,6},{8,9},{9,8},{10,11... | collective-permute-start | bytes 1474568 | tf_op jit(solution)/shard_map/ppermute | solution.py:395

commit v2 on v1

v2 whole, which is shorter than its diff:
```python
import functools

import jax
import jax.numpy as jnp
from jax import lax
from jax.experimental import pallas as pl
from jax.experimental.pallas import tpu as pltpu
from jax.sharding import PartitionSpec as P

POISSON = 0.3
LAME = POISSON / ((1.0 + POISSON) * (1.0 - 2.0 * POISSON))
SHEAR = 1.0 / (2.0 * (1.0 + POISSON))
RATIO = LAME / SHEAR
ONE = SHEAR / 16.0
TWO = SHEAR / 48.0
THREE = (LAME + 4.0 * SHEAR) / 144.0

VMEM = pl.BlockSpec(memory_space=pltpu.VMEM)
LIMIT = pltpu.CompilerParams(vmem_limit_bytes=48 << 20)


def lanes(shape):
    return lax.broadcasted_iota(jnp.int32, shape, len(shape) - 1)


def from_left(first, second):
    edge = lanes(first.shape) == 0
    turned, turned2 = pltpu.roll(first, 1, 1), pltpu.roll(second, 1, 1)
    return jnp.where(edge, 0.0, turned), jnp.where(edge, turned, turned2)


def from_right(first, second):
    edge = lanes(first.shape) == first.shape[1] - 1
    turned, turned2 = (pltpu.roll(v, v.shape[1] - 1, 1) for v in (first, second))
    return jnp.where(edge, turned2, turned), jnp.where(edge, 0.0, turned2)


def pack_kernel(force_hbm, modulus_hbm, force_ref, own_ref, same_ref, cross_ref, modulus_ref, sem):
    core = lax.axis_index("gy")
    cells = own_ref.shape[2]
    copies = [
        pltpu.make_async_copy(force_hbm, force_ref, sem.at[0]),
        pltpu.make_async_copy(modulus_hbm, modulus_ref, sem.at[1]),
    ]
    for copy in copies:
        copy.start()
    for copy in copies:
        copy.wait()

    def plane(field, x):
        rows = pl.ds(x, cells, stride=4)
        return force_ref[field, rows, :] if field < 3 else modulus_ref[rows, :]

    for field in range(4):
        for x in range(4):
            own_ref[x, field] = plane(field, x)
        for i in range(2):
            same_ref[i, field] = plane(field, 2 * (1 - core) + i)
            cross_ref[i, field] = plane(field, 2 * core + i)


def plane_modes(read, cells):
    sums, diffs = [], []
    for block in range(2):
        high, low = read(block, 8, cells), read(block, 7, cells)
        sums.append(high + low)
        diffs.append(high - low)
    sums_left, diffs_left = from_left(*sums), from_left(*diffs)
    out = []
    for block in range(2):
        s, d, sl, dl = sums[block], diffs[block], sums_left[block], diffs_left[block]
        out.append((s + sl, d + dl, s - sl, d - dl))
    return out


def element_modes(low, high):
    found = []
    for component in range(3):
        modes = {}
        for kind, (z, y) in enumerate(((0, 0), (1, 0), (0, 1), (1, 1))):
            lo, hi = low[component][kind], high[component][kind]
            if (z, y) != (0, 0):
                modes[z, 0, y] = hi + lo
            modes[z, 1, y] = hi - lo
        found.append(modes)
    return found


def mode_forces(modes, modulus):
    u, v, w = modes
    one, two, three = modulus * ONE, modulus * TWO, modulus * THREE
    trace = RATIO * (u[1, 0, 0] + v[0, 1, 0] + w[0, 0, 1])
    shear_zx = one * (u[0, 1, 0] + v[1, 0, 0])
    shear_xy = one * (v[0, 0, 1] + w[0, 1, 0])
    shear_zy = one * (u[0, 0, 1] + w[1, 0, 0])
    trace_z = RATIO * (v[1, 1, 0] + w[1, 0, 1])
    trace_x = RATIO * (u[1, 1, 0] + w[0, 1, 1])
    trace_y = RATIO * (u[1, 0, 1] + v[0, 1, 1])
    mixed_zx = u[0, 1, 1] + v[1, 0, 1]
    mixed_xy = v[1, 0, 1] + w[1, 1, 0]
    mixed_zy = u[0, 1, 1] + w[1, 1, 0]
    return (
        {
            (1, 0, 0): one * (trace + 2.0 * u[1, 0, 0]),
            (0, 1, 0): shear_zx,
            (0, 0, 1): shear_zy,
            (1, 1, 0): two * (trace_x + 3.0 * u[1, 1, 0]),
            (1, 0, 1): two * (trace_y + 3.0 * u[1, 0, 1]),
            (0, 1, 1): two * (mixed_zx + mixed_zy),
            (1, 1, 1): three * u[1, 1, 1],
        },
        {
            (0, 1, 0): one * (trace + 2.0 * v[0, 1, 0]),
            (1, 0, 0): shear_zx,
            (0, 0, 1): shear_xy,
            (1, 1, 0): two * (trace_z + 3.0 * v[1, 1, 0]),
            (0, 1, 1): two * (trace_y + 3.0 * v[0, 1, 1]),
            (1, 0, 1): two * (mixed_zx + mixed_xy),
            (1, 1, 1): three * v[1, 1, 1],
        },
        {
            (0, 0, 1): one * (trace + 2.0 * w[0, 0, 1]),
            (1, 0, 0): shear_zy,
            (0, 1, 0): shear_xy,
            (1, 0, 1): two * (trace_z + 3.0 * w[1, 0, 1]),
            (0, 1, 1): two * (trace_x + 3.0 * w[0, 1, 1]),
            (1, 1, 0): two * (mixed_xy + mixed_zy),
            (1, 1, 1): three * w[1, 1, 1],
        },
    )


def mode_energy(modes, modulus):
    u, v, w = modes
    square = lambda value: value * value
    a, b, c = u[1, 0, 0], v[0, 1, 0], w[0, 0, 1]
    one = RATIO * square(a + b + c) + 2.0 * (square(a) + square(b) + square(c))
    one = one + square(u[0, 1, 0] + v[1, 0, 0]) + square(v[0, 0, 1] + w[0, 1, 0]) + square(u[0, 0, 1] + w[1, 0, 0])
    d, e, f = u[1, 1, 0], u[1, 0, 1], v[1, 1, 0]
    g, h, k = v[0, 1, 1], w[1, 0, 1], w[0, 1, 1]
    two = RATIO * (square(f + h) + square(d + k) + square(e + g))
    two = two + 3.0 * (square(d) + square(e) + square(f) + square(g) + square(h) + square(k))
    m, n, o = u[0, 1, 1], v[1, 0, 1], w[1, 1, 0]
    two = two + square(m + n) + square(n + o) + square(m + o)
    three = square(u[1, 1, 1]) + square(v[1, 1, 1]) + square(w[1, 1, 1])
    return modulus * (ONE * one + TWO * two + THREE * three)


def store_modes(mode_ref, at, field, kinds, read, cells):
    for block, found in enumerate(plane_modes(read, cells)):
        for kind in range(kinds):
            mode_ref[at, kinds * field + kind, block] = found[kind]


def face_forces(forces):
    upper, lower = [], []
    for component in range(3):
        up, down = [], []
        for z, y in ((0, 0), (1, 0), (0, 1), (1, 1)):
            diff, both = forces[component][z, 1, y], forces[component].get((z, 0, y))
            up.append(diff if both is None else both + diff)
            down.append(-diff if both is None else both - diff)
        upper.append(up)
        lower.append(down)
    return upper, lower


def corner_forces(modes):
    ss, ds, sd, dd = modes
    here, back = ss + ds, ss - ds
    here_y, back_y = sd + dd, sd - dd
    return here + here_y, here - here_y, back + back_y, back - back_y


def plus(first, second):
    return [[p + q for p, q in zip(a, b)] for a, b in zip(first, second)]


def assembled(part_ref, at, field, cells):
    here = lambda k, block: part_ref[at, 4 * field + k, block, 0:cells, :]
    above = lambda k, block: part_ref[at, 4 * field + k, block, 1 : cells + 1, :]
    beside = from_right(*(here(1, block) + above(3, block) for block in range(2)))
    return [here(0, block) + above(2, block) + beside[block] for block in range(2)]


def inner_kernel(own_ref, mate_ref, node_ref, elem_ref, image_ref, edge_mode_ref, edge_part_ref, sums_ref, mode_ref, part_ref):
    core = lax.axis_index("gy")
    cells, width = own_ref.shape[2:]
    tiles = cells // 8
    zeros = lambda *dims: jnp.zeros(dims, jnp.float32)
    node_ref[:, :, :, 0:8, :] = zeros(4, 3, 2, 8, width)
    for x in range(4):
        for ref, block in ((own_ref, core), (mate_ref, 1 - core)):
            for field in range(3):
                node_ref[x, field, block, 8 : 8 + cells, :] = ref[x, field]
            elem_ref[x, block] = ref[x, 3]

    @pl.loop(0, 4)
    def _(x):
        for field in range(3):
            read = lambda block, start, size: node_ref[x, field, block, start : start + size, :]
            store_modes(mode_ref, x, field, 4, read, cells)

    edge_mode_ref[...] = mode_ref[3 * core]
    part_ref[:, :, :, cells : cells + 8, :] = zeros(2, 12, 2, 8, width)

    @pl.loop(0, 2 * tiles)
    def _(t):
        block, rows = t // tiles, pl.ds(pl.multiple_of((t % tiles) * 8, 8), 8)
        load = lambda x: [[mode_ref[x, 4 * f + k, block, rows, :] for k in range(4)] for f in range(3)]
        low, kept, outer = load(0), None, None
        for x in range(1, 4):
            high = load(x)
            upper, lower = face_forces(mode_forces(element_modes(low, high), elem_ref[x, block, rows, :]))
            if kept is None:
                outer = lower
            else:
                for f, modes in enumerate(plus(kept, lower)):
                    for k, value in enumerate(corner_forces(modes)):
                        part_ref[x - 2, 4 * f + k, block, rows, :] = value
            low, kept = high, upper
        for f in range(3):
            for k in range(4):
                edge_part_ref[4 * f + k, block, rows, :] = jnp.where(core == 0, outer[f][k], kept[f][k])

    fold = lambda value: value.reshape(tiles, 8, width).sum(0)
    norm = cross = square = zeros(8, width)
    for i in range(2):
        mine = jnp.where(core == i, 1.0, 0.0)
        for f in range(3):
            for block, value in enumerate(assembled(part_ref, i, f, cells)):
                image_ref[i, f, block] = value
                force = node_ref[i + 1, f, block, 8 : 8 + cells, :]
                norm = norm + mine * fold(force * force)
                cross = cross + mine * fold(force * value)
                square = square + mine * fold(value * value)
    for k, value in enumerate((norm, cross, square)):
        sums_ref[k] = value


def outer_kernel(
    node_ref, elem_ref, image_ref, edge_mode_ref, edge_part_ref, part_sums_ref, same_ref, cross_ref,
    give_ref, sums_ref, halo_ref, halo_elem_ref, mode_ref, part_ref, image_mode_ref,
):
    core, slab = lax.axis_index("gy"), lax.axis_index("gx")
    cells, width = same_ref.shape[2:]
    tiles = cells // 8
    zeros = lambda *dims: jnp.zeros(dims, jnp.float32)
    near = 1 - core
    halo_ref[:, :, :, 0:8, :] = zeros(2, 3, 2, 8, width)
    for i in range(2):
        for ref, block in ((same_ref, core), (cross_ref, 1 - core)):
            for field in range(3):
                halo_ref[i, field, block, 8 : 8 + cells, :] = ref[i, field]
            halo_elem_ref[i, block] = ref[i, 3]

    mode_ref[2 * near] = edge_mode_ref[...]

    @pl.loop(0, 2)
    def _(i):
        for field in range(3):
            read = lambda block, start, size: halo_ref[i, field, block, start : start + size, :]
            store_modes(mode_ref, core + i, field, 4, read, cells)

    part_ref[:, :, :, cells : cells + 8, :] = zeros(2, 12, 2, 8, width)

    @pl.loop(0, 2 * tiles)
    def _(t):
        block, rows = t // tiles, pl.ds(pl.multiple_of((t % tiles) * 8, 8), 8)
        load = lambda x: [[mode_ref[x, 4 * f + k, block, rows, :] for k in range(4)] for f in range(3)]
        planes = [load(x) for x in range(3)]
        first = jnp.where(core == 0, halo_elem_ref[1, block, rows, :], halo_elem_ref[0, block, rows, :])
        second = jnp.where(core == 0, elem_ref[0, block, rows, :], halo_elem_ref[1, block, rows, :])
        upper, lower = face_forces(mode_forces(element_modes(planes[0], planes[1]), first))
        upper2, lower2 = face_forces(mode_forces(element_modes(planes[1], planes[2]), second))
        for f, modes in enumerate(plus(upper, lower2)):
            for k, value in enumerate(corner_forces(modes)):
                part_ref[0, 4 * f + k, block, rows, :] = value
        for f in range(3):
            modes = [
                edge_part_ref[4 * f + k, block, rows, :] + jnp.where(core == 0, upper2[f][k], lower[f][k]) for k in range(4)
            ]
            for k, value in enumerate(corner_forces(modes)):
                part_ref[1, 4 * f + k, block, rows, :] = value

    clamped = jnp.where((core == 0) & (slab == 0), 0.0, 1.0)
    fold = lambda value: value.reshape(tiles, 8, width).sum(0)
    norm, cross, square = (part_sums_ref[k] for k in range(3))
    row = lax.broadcasted_iota(jnp.int32, (cells, width), 0)
    below = lambda value: jnp.where(row == 0, 0.0, pltpu.roll(value, 1, 0))
    for f in range(3):
        value = assembled(part_ref, 0, f, cells)
        for block in range(2):
            give_ref[f, block] = value[block] * clamped
            give_ref[6 + f, block] = halo_ref[near, f, block, 8 : 8 + cells, :]
        for block, value in enumerate(assembled(part_ref, 1, f, cells)):
            give_ref[3 + f, block] = value
            force = node_ref[3 * core, f, block, 8 : 8 + cells, :]
            norm = norm + fold(force * force)
            cross = cross + fold(force * value)
            square = square + fold(value * value)
    for block in range(2):
        give_ref[9, block] = halo_elem_ref[near, block]

    @pl.loop(0, 3)
    def _(i):
        for field in range(3):
            def read(block, start, size):
                inner = image_ref[jnp.where(core == 0, 0, jnp.minimum(i, 1)), field, block]
                outer = give_ref[jnp.where(core == 0, 3 * jnp.minimum(i, 1), 3) + field, block]
                value = jnp.where((i == 2) == (core == 0), inner, outer)
                return value if start == 8 else below(value)
            store_modes(image_mode_ref, i, field, 4, read, cells)

    def energy_of(t, total):
        block, rows = t // tiles, pl.ds(pl.multiple_of((t % tiles) * 8, 8), 8)
        load = lambda x: [[image_mode_ref[x, 4 * f + k, block, rows, :] for k in range(4)] for f in range(3)]
        low = load(0)
        for x in range(2):
            high = load(x + 1)
            total = total + mode_energy(element_modes(low, high), elem_ref[2 * core + x, block, rows, :])
            low = high
        return total

    energy = lax.fori_loop(0, 2 * tiles, energy_of, zeros(8, width))
    line = lax.broadcasted_iota(jnp.int32, (8, width), 0)
    packed = zeros(8, width)
    for k, value in enumerate((norm, cross, square, energy)):
        packed = jnp.where(line == k, jnp.sum(value, axis=0, keepdims=True), packed)
    sums_ref[...] = jnp.broadcast_to(packed[None], sums_ref.shape)


def stress_kernel(
    node_ref, elem_ref, image_ref, give_ref, take_ref, basis_ref, plane_ref, outer_elem_ref, mode_ref, part_ref,
):
    core, slab = lax.axis_index("gy"), lax.axis_index("gx")
    last = slab == lax.axis_size("gx") - 1
    cells, width = elem_ref.shape[2:]
    tiles = cells // 8
    row = lax.broadcasted_iota(jnp.int32, (cells, width), 0)
    lane = lanes((cells, width))
    below = lambda value: jnp.where(row == 0, 0.0, pltpu.roll(value, 1, 0))
    part_ref[:, :, :, cells : cells + 8, :] = jnp.zeros((4, 6, 2, 8, width), jnp.float32)
    mine, other = 5 * core, 5 * (1 - core)

    for which in range(2):
        for f in range(3):
            for block in range(2):
                if which == 0:
                    plane_ref[mine, f, block] = give_ref[6 + f, block]
                    plane_ref[other, f, block] = take_ref[6 + f, block]
                    for x in range(4):
                        plane_ref[1 + x, f, block] = node_ref[x, f, block, 8 : 8 + cells, :]
                else:
                    plane_ref[mine, f, block] = give_ref[f, block]
                    plane_ref[other, f, block] = take_ref[f, block]
                    plane_ref[1 + 3 * core, f, block] = give_ref[3 + f, block]
                    plane_ref[4 - 3 * core, f, block] = take_ref[3 + f, block]
                    for x in range(2):
                        plane_ref[2 + x, f, block] = image_ref[x, f, block]
        if which == 0:
            for block in range(2):
                outer_elem_ref[block] = jnp.where(core == 0, take_ref[9, block], give_ref[9, block])

        @pl.loop(0, 6)
        def _(x):
            for field in range(3):
                def read(block, start, size):
                    value = plane_ref[x, field, block]
                    return value if start == 8 else below(value)
                store_modes(mode_ref, x, field, 3, read, cells)

        @pl.loop(0, 2 * tiles)
        def _(t):
            block, rows = t // tiles, pl.ds(pl.multiple_of((t % tiles) * 8, 8), 8)
            load = lambda x: [[mode_ref[x, 3 * f + k, block, rows, :] for k in range(3)] for f in range(3)]
            low, kept = load(0), None
            for x in range(1, 6):
                high = load(x)
                by_z = [high[f][1] + low[f][1] for f in range(3)]
                by_x = [high[f][0] - low[f][0] for f in range(3)]
                by_y = [high[f][2] + low[f][2] for f in range(3)]
                scaled = (elem_ref[x - 1, block, rows, :] if x < 5 else outer_elem_ref[block, rows, :]) * (0.25 * SHEAR)
                trace = RATIO * (by_z[0] + by_x[1] + by_y[2])
                now = [
                    scaled * (trace + 2.0 * by_z[0]),
                    scaled * (trace + 2.0 * by_x[1]),
                    scaled * (trace + 2.0 * by_y[2]),
                    scaled * (by_x[0] + by_z[1]),
                    scaled * (by_y[1] + by_x[2]),
                    scaled * (by_y[0] + by_z[2]),
                ]
                if kept is not None:
                    for k in range(6):
                        part_ref[x - 2, k, block, rows, :] = kept[k] + now[k]
                low, kept = high, now

        for x in range(4):
            count = jnp.where(row == cells - 1, 1.0, 0.5) * (jnp.where(last, 1.0, 0.5) if x == 3 else 0.5)
            count = count * jnp.where((lane == width - 1) & (core == 1), 1.0, 0.5)
            for k in range(6):
                both = [part_ref[x, k, block, 0:cells, :] + part_ref[x, k, block, 1 : cells + 1, :] for block in range(2)]
                beside = from_right(*both)
                value = jnp.where(core == 0, both[0] + beside[0], both[1] + beside[1])
                basis_ref[6 * which + k, pl.ds(x, cells, stride=4), :] = value * count
    for x in range(4):
        for f in range(3):
            basis_ref[12 + f, pl.ds(x, cells, stride=4), :] = plane_ref[1 + x, f, core]


def combine_kernel(sums_ref, force_ref, basis_ref, field_ref, stress_ref):
    total = jnp.sum(jnp.sum(sums_ref[...], axis=0), axis=1, keepdims=True)
    norm, cross, square, energy = (total[k : k + 1, :] for k in range(4))
    first = norm / cross
    norm_next = norm - 2.0 * first * cross + first * first * square
    ratio = norm_next / norm
    grown = 1.0 + ratio
    curvature = grown * grown * cross - 2.0 * grown * first * square + first * first * energy
    second = norm_next / curvature
    weight = jnp.broadcast_to(first + second * grown, force_ref.shape[1:])
    weight_image = jnp.broadcast_to(-second * first, force_ref.shape[1:])
    for f in range(3):
        field_ref[f] = weight * force_ref[f] + weight_image * basis_ref[12 + f]
    for k in range(6):
        stress_ref[k] = weight * basis_ref[k] + weight_image * basis_ref[6 + k]


def cost(flops, size):
    return pl.CostEstimate(flops=flops, bytes_accessed=size, transcendentals=0)


def per_device(body_force, modulus):
    cells, planes, width = modulus.shape
    slabs, cores = lax.axis_size("gx"), lax.axis_size("gy")
    assert planes == 4 and cores == 2 and cells % 8 == 0
    both = ("gx", "gy")
    f32 = jnp.float32
    shape = lambda *dims: jax.ShapeDtypeStruct(dims, f32)
    scratch = lambda *dims: pltpu.VMEM(dims, f32)

    force, own, same, cross = pl.pallas_call(
        pack_kernel,
        out_shape=(shape(3, cells * 4, width), shape(4, 4, cells, width), shape(2, 4, cells, width), shape(2, 4, cells, width)),
        in_specs=[pl.BlockSpec(memory_space=pl.ANY)] * 2,
        out_specs=[VMEM] * 4,
        scratch_shapes=[scratch(cells * 4, width), pltpu.SemaphoreType.DMA((2,))],
        compiler_params=LIMIT,
        name="pack",
    )(
        pltpu.with_memory_space_constraint(body_force.reshape(3, cells * 4, width), pltpu.HBM),
        pltpu.with_memory_space_constraint(modulus.reshape(cells * 4, width), pltpu.HBM),
    )

    up = [(2 * g, 2 * g + 2) for g in range(slabs - 1)]
    down = [(2 * g + 3, 2 * g + 1) for g in range(slabs - 1)]
    pairs = [(2 * g + 1, 2 * g + 2) for g in range(slabs - 1)]
    mate = lax.ppermute(own, "gy", [(0, 1), (1, 0)])
    cross_in = lax.ppermute(cross, both, pairs + [(q, p) for p, q in pairs])
    same_in = lax.ppermute(same, both, up + down)

    node, elem, image, edge_mode, edge_part, part_sums = pl.pallas_call(
        inner_kernel,
        out_shape=(
            shape(4, 3, 2, 8 + cells, width),
            shape(4, 2, cells, width),
            shape(2, 3, 2, cells, width),
            shape(12, 2, cells, width),
            shape(12, 2, cells, width),
            shape(3, 8, width),
        ),
        in_specs=[VMEM] * 2,
        out_specs=[VMEM] * 6,
        scratch_shapes=[scratch(4, 12, 2, cells, width), scratch(2, 12, 2, 8 + cells, width)],
        compiler_params=LIMIT,
        cost_estimate=cost(20_000_000, 4_000_000),
        name="inner",
    )(own, mate)
    give, sums = pl.pallas_call(
        outer_kernel,
        out_shape=(shape(10, 2, cells, width), shape(slabs * cores, 8, width)),
        in_specs=[VMEM] * 8,
        out_specs=[VMEM] * 2,
        scratch_shapes=[
            scratch(2, 3, 2, 8 + cells, width),
            scratch(2, 2, cells, width),
            scratch(3, 12, 2, cells, width),
            scratch(2, 12, 2, 8 + cells, width),
            scratch(3, 12, 2, cells, width),
        ],
        compiler_params=LIMIT,
        cost_estimate=cost(10_000_000, 3_000_000),
        name="outer",
    )(node, elem, image, edge_mode, edge_part, part_sums, same_in, cross_in)

    take = lax.ppermute(give, "gy", [(0, 1), (1, 0)])
    sums = lax.all_to_all(sums, both, 0, 0)
    basis = pl.pallas_call(
        stress_kernel,
        out_shape=shape(15, cells * 4, width),
        in_specs=[VMEM] * 5,
        out_specs=VMEM,
        scratch_shapes=[
            scratch(6, 3, 2, cells, width),
            scratch(2, cells, width),
            scratch(6, 9, 2, cells, width),
            scratch(4, 6, 2, 8 + cells, width),
        ],
        compiler_params=LIMIT,
        cost_estimate=cost(20_000_000, 4_000_000),
        name="stress",
    )(node, elem, image, give, take)

    field, stress = pl.pallas_call(
        combine_kernel,
        out_shape=(shape(3, cells * 4, width), shape(6, cells * 4, width)),
        in_specs=[VMEM] * 3,
        out_specs=[VMEM] * 2,
        compiler_params=LIMIT,
        name="combine",
    )(sums, force, basis)
    return field.reshape(3, cells, 4, width), stress.reshape(6, cells, 4, width)


def solution(mesh):
    return jax.shard_map(
        per_device,
        mesh=mesh,
        in_specs=(P(None, "sample", "gx", "gy"), P("sample", "gx", "gy")),
        out_specs=(P(None, "sample", "gx", "gy"), P(None, "sample", "gx", "gy")),
        check_vma=False,
    )
```

time: 32.6 us -> 29.7 us (0.911)
  blocking collectives: 12.6 us -> 0 us
  starting transfers between devices: 8.67 us -> 14.5 us
  waiting for transfers between devices: 3.2 us -> 6.01 us
  Pallas kernels: 5.51 us -> 8.3 us
  local copies, waits for them, and re-layouts: 1.76 us -> 0 us
    all_to_all x1 -> x0, blocking collectives: 12.6 us -> none  [per_device(): sums = lax.all_to_all(sums, both, 0, 0)]
    all_to_all x0 -> x1, starting transfers between devices: none -> 5.89 us  [per_device(): sums = lax.all_to_all(sums, both, 0, 0)]
    all_to_all x0 -> x1, waiting for transfers between devices: none -> 4.12 us  [per_device(): sums = lax.all_to_all(sums, both, 0, 0)]
    pallas_call x3 -> x4, Pallas kernels: 4.47 us -> 7.31 us  [the longest x1 2.76 us: per_device(): pl.pallas_call(stress_kernel, out_shape=shape(15, cells * 4, width), in_s...]
    unnamed x4 -> x0, local copies, waits for them, and re-layouts: 1.76 us -> none
    ppermute x1, waiting for transfers between devices: 3.19 us -> 1.88 us  [per_device(): same_in = lax.ppermute(same, both, up + down)]
  transfers between devices with their start and end apart: 4 -> 5, of which waited for: 1 -> 2; matrix products, arithmetic and copies ran while one was open for 0% -> 0% of each run, Pallas kernels for 0% -> 14%
where the time goes in v2:
time: 29.7 us; the launch traced here: 29.5 us
  starting transfers between devices  14.5 us (49%)
  Pallas kernels  8.3 us (28%)
  waiting for transfers between devices  6.01 us (20%)
  between operations  0.69 us (2%)
    all_to_all x1, starting transfers between devices, per_device(): sums = lax.all_to_all(sums, both, 0, 0)  5.89 us
    ppermute x1, starting transfers between devices, per_device(): same_in = lax.ppermute(same, both, up + down)  4.41 us
    all_to_all x1, waiting for transfers between devices, per_device(): sums = lax.all_to_all(sums, both, 0, 0)  4.12 us
    ppermute x1, starting transfers between devices, per_device(): take = lax.ppermute(give, 'gy', [(0, 1), (1, 0)])  3 us
    pallas_call x1, Pallas kernels, per_device(): pl.pallas_call(stress_kernel, out_shape=shape(15, cells * 4, width), in_s...  2.76 us
    pallas_call x1, Pallas kernels, per_device(): pl.pallas_call(outer_kernel, out_shape=(shape(10, 2, cells, width), shape...  2.28 us
    ppermute x1, waiting for transfers between devices, per_device(): same_in = lax.ppermute(same, both, up + down)  1.88 us
    pallas_call x1, Pallas kernels, per_device(): pl.pallas_call(inner_kernel, out_shape=(shape(4, 3, 2, 8 + cells, width),...  1.29 us
  transfers between devices with their start and end apart: 5, of which 2 were waited for; matrix products, arithmetic and copies ran while one was open for 0% of the time, Pallas kernels for 14%

profile of v2, /device:TPU:0, one launch (start us, length us, event | category | flops | bytes accessed | tf_op | source)
XLA Modules:
  0.0 29.5 jit_solution(6459338576791302731)
XLA Ops:
  0.6 1.0 %pack.1 = (f32[3,128,128]{2,1,0:T(8,128)S(1)}, f32[4,4,32,128]{3,2,1,0:T(8,128)S(1)}, f32[2,4,32,128]{3,2,1,0:T(8,128)S(1)}, f32[2,4,32,128]{3,2,1,0:T(8,128)S(1)}) custom-call(f32[3,128,128]{2,1,0:T(8,128)} %bitcast.4, f32[128,128]{1,0:T(8,128)} %bitcast.5), custom_call_target="tpu_custom_call" | custom-call | tf_op jit(solution)/shard_map/pack/pallas_call | solution.py:441
  1.6 0.5 %collective-permute-start = (f32[4,4,32,128]{3,2,1,0:T(8,128)S(1)}, f32[4,4,32,128]{3,2,1,0:T(8,128)S(1)}, u32[]{:S(2)}, u32[]{:S(2)}) collective-permute-start(f32[4,4,32,128]{3,2,1,0:T(8,128)S(1)} %get-tuple-element.16.own_ref), channel_id=1, source_target_pairs={{0,1},{1,0},{2,3},{3,2},{4,5},{5,4},{6,7},{7,6},{8,9},{9,8},{10,11... | collective-permute-start | bytes 786440 | tf_op jit(solution)/shard_map/ppermute | solution.py:457
  2.1 4.4 %collective-permute-start.1 = (f32[2,4,32,128]{3,2,1,0:T(8,128)S(1)}, f32[2,4,32,128]{3,2,1,0:T(8,128)S(1)}, u32[]{:S(2)}, u32[]{:S(2)}) collective-permute-start(f32[2,4,32,128]{3,2,1,0:T(8,128)S(1)} %get-tuple-element.23), channel_id=1, source_target_pairs={{0,2},{2,4},{4,6},{6,8},{8,10},{10,12},{12,14},{3,1},{5,3},{7,5},{... | collective-permute-start | bytes 393224 | tf_op jit(solution)/shard_map/ppermute | solution.py:459
  6.6 0.7 %collective-permute-start.2 = (f32[2,4,32,128]{3,2,1,0:T(8,128)S(1)}, f32[2,4,32,128]{3,2,1,0:T(8,128)S(1)}, u32[]{:S(2)}, u32[]{:S(2)}) collective-permute-start(f32[2,4,32,128]{3,2,1,0:T(8,128)S(1)} %get-tuple-element.24), channel_id=1, source_target_pairs={{1,2},{3,4},{5,6},{7,8},{9,10},{11,12},{13,14},{2,1},{4,3},{6,5},{... | collective-permute-start | bytes 393224 | tf_op jit(solution)/shard_map/ppermute | solution.py:458
  7.2 0.0 collective-permute-done.mate_ref
  7.2 1.3 %inner.1 = (f32[4,3,2,40,128]{4,3,2,1,0:T(8,128)S(1)}, f32[4,2,32,128]{3,2,1,0:T(8,128)S(1)}, f32[2,3,2,32,128]{4,3,2,1,0:T(8,128)S(1)}, f32[12,2,32,128]{3,2,1,...) custom-call(f32[4,4,32,128]{3,2,1,0:T(8,128)S(1)} %get-tuple-element.16.own_ref, ...), custom_call_target="tpu_custom_call" | custom-call | flops 20000000 | bytes 4000000 | tf_op jit(solution)/shard_map/inner/pallas_call | solution.py:461
  8.5 1.9 %collective-permute-done.1.same_ref = f32[2,4,32,128]{3,2,1,0:T(8,128)S(1)} collective-permute-done((f32[2,4,32,128]{3,2,1,0:T(8,128)S(1)}, f32[2,4,32,128]{3,2,1,0:T(8,128)S(1)}, u32[]{:S(2)}, u32[]{:S(2)}) %collective-permute-start.1) | collective-permute-done | bytes 131104 | tf_op jit(solution)/shard_map/ppermute | solution.py:459
  10.4 0.0 collective-permute-done.2.cross_ref
  10.4 2.3 %outer.1 = (f32[10,2,32,128]{3,2,1,0:T(8,128)S(1)}, f32[16,8,128]{2,1,0:T(8,128)}) custom-call(f32[4,3,2,40,128]{4,3,2,1,0:T(8,128)S(1)} %get-tuple-element.17.node_ref, f32[4,2,32,128]{3,2,1,0:T(8,128)S(1)} %get-tuple-element.18.elem_ref, f32[2,3,2,32,128]{4,3,2,1,0:T(8,128)S(1)} %get-tuple-element.19.image_ref, ...), custom_call_target="tpu_custom_call" | custom-call | flops 10000000 | bytes 3000000 | tf_op jit(solution)/shard_map/outer/pallas_call | solution.py:478
  12.7 3.0 %collective-permute-start.3 = (f32[10,2,32,128]{3,2,1,0:T(8,128)S(1)}, f32[10,2,32,128]{3,2,1,0:T(8,128)S(1)}, u32[]{:S(2)}, u32[]{:S(2)}) collective-permute-start(f32[10,2,32,128]{3,2,1,0:T(8,128)S(1)} %get-tuple-element.27.give_ref), channel_id=1, source_target_pairs={{0,1},{1,0},{2,3},{3,2},{4,5},{5,4},{6,7},{7,6},{8,9},{9,8},{10,11... | collective-permute-start | bytes 983048 | tf_op jit(solution)/shard_map/ppermute | solution.py:495
  15.7 5.9 %all-to-all-start = ((f32[16,8,128]{2,1,0:T(8,128)}), f32[16,8,128]{2,1,0:T(8,128)S(1)}, u32[]{:S(2)}, u32[]{:S(2)}) async-start(f32[16,8,128]{2,1,0:T(8,128)} %get-tuple-element.25), calls=%async_computation | async-start | bytes 131072 | tf_op jit(solution)/shard_map/all_to_all | solution.py:496
  21.6 0.0 collective-permute-done.3.take_ref
  21.6 2.8 %stress.1.basis_ref = f32[15,128,128]{2,1,0:T(8,128)S(1)} custom-call(f32[4,3,2,40,128]{4,3,2,1,0:T(8,128)S(1)} %get-tuple-element.17.node_ref, f32[4,2,32,128]{3,2,1,0:T(8,128)S(1)} %get-tuple-element.18.elem_ref, f32[2,3,2,32,128]{4,3,2,1,0:T(8,128)S(1)} %get-tuple-element.19.image_ref, f32[10,2,32,128]{3,2,1,0:T(8,128)S(1)} %get-tuple-element.27.give_ref, ...), custom_call_target="tpu_custom_call" | custom-call | flops 20000000 | bytes 4000000 | tf_op jit(solution)/shard_map/stress/pallas_call | solution.py:497
  24.4 4.1 %all-to-all-done.sums_ref = f32[16,8,128]{2,1,0:T(8,128)S(1)} async-done(((f32[16,8,128]{2,1,0:T(8,128)}), f32[16,8,128]{2,1,0:T(8,128)S(1)}, u32[]{:S(2)}, u32[]{:S(2)}) %all-to-all-start) | async-done | bytes 65568 | tf_op jit(solution)/shard_map/all_to_all | solution.py:496
  28.5 1.0 %combine.1 = (f32[3,128,128]{2,1,0:T(8,128)}, f32[6,128,128]{2,1,0:T(8,128)}) custom-call(f32[16,8,128]{2,1,0:T(8,128)S(1)} %all-to-all-done.sums_ref, f32[3,128,128]{2,1,0:T(8,128)S(1)} %get-tuple-element.26.force_ref, f32[15,128,128]{2,1,0:T(8,128)S(1)} %stress.1.basis_ref), custom_call_target="tpu_custom_call" | custom-call | tf_op jit(solution)/shard_map/combine/pallas_call | solution.py:513
Async XLA Ops:
  1.6 5.6 %collective-permute-start = (f32[4,4,32,128]{3,2,1,0:T(8,128)S(1)}, f32[4,4,32,128]{3,2,1,0:T(8,128)S(1)}, u32[]{:S(2)}, u32[]{:S(2)}) collective-permute-start(f32[4,4,32,128]{3,2,1,0:T(8,128)S(1)} %get-tuple-element.16.own_ref), channel_id=1, source_target_pairs={{0,1},{1,0},{2,3},{3,2},{4,5},{5,4},{6,7},{7,6},{8,9},{9,8},{10,11... | collective-permute-start | bytes 786440 | tf_op jit(solution)/shard_map/ppermute | solution.py:457
  2.1 8.3 %collective-permute-start.1 = (f32[2,4,32,128]{3,2,1,0:T(8,128)S(1)}, f32[2,4,32,128]{3,2,1,0:T(8,128)S(1)}, u32[]{:S(2)}, u32[]{:S(2)}) collective-permute-start(f32[2,4,32,128]{3,2,1,0:T(8,128)S(1)} %get-tuple-element.23), channel_id=1, source_target_pairs={{0,2},{2,4},{4,6},{6,8},{8,10},{10,12},{12,14},{3,1},{5,3},{7,5},{... | collective-permute-start | bytes 393224 | tf_op jit(solution)/shard_map/ppermute | solution.py:459
  6.6 3.9 %collective-permute-start.2 = (f32[2,4,32,128]{3,2,1,0:T(8,128)S(1)}, f32[2,4,32,128]{3,2,1,0:T(8,128)S(1)}, u32[]{:S(2)}, u32[]{:S(2)}) collective-permute-start(f32[2,4,32,128]{3,2,1,0:T(8,128)S(1)} %get-tuple-element.24), channel_id=1, source_target_pairs={{1,2},{3,4},{5,6},{7,8},{9,10},{11,12},{13,14},{2,1},{4,3},{6,5},{... | collective-permute-start | bytes 393224 | tf_op jit(solution)/shard_map/ppermute | solution.py:458
  12.7 8.9 %collective-permute-start.3 = (f32[10,2,32,128]{3,2,1,0:T(8,128)S(1)}, f32[10,2,32,128]{3,2,1,0:T(8,128)S(1)}, u32[]{:S(2)}, u32[]{:S(2)}) collective-permute-start(f32[10,2,32,128]{3,2,1,0:T(8,128)S(1)} %get-tuple-element.27.give_ref), channel_id=1, source_target_pairs={{0,1},{1,0},{2,3},{3,2},{4,5},{5,4},{6,7},{7,6},{8,9},{9,8},{10,11... | collective-permute-start | bytes 983048 | tf_op jit(solution)/shard_map/ppermute | solution.py:495
  15.7 12.8 %all-to-all-start = ((f32[16,8,128]{2,1,0:T(8,128)}), f32[16,8,128]{2,1,0:T(8,128)S(1)}, u32[]{:S(2)}, u32[]{:S(2)}) async-start(f32[16,8,128]{2,1,0:T(8,128)} %get-tuple-element.25), calls=%async_computation | async-start | bytes 131072 | tf_op jit(solution)/shard_map/all_to_all | solution.py:496

commit v3 on v2

--- a/solution.py
+++ b/solution.py
@@ -59,18 +59,27 @@
             cross_ref[i, field] = plane(field, 2 * core + i)
 
 
-def plane_modes(read, cells):
-    sums, diffs = [], []
-    for block in range(2):
-        high, low = read(block, 8, cells), read(block, 7, cells)
-        sums.append(high + low)
-        diffs.append(high - low)
+def below(value):
+    row = lax.broadcasted_iota(jnp.int32, value.shape, 0)
+    return jnp.where(row == 0, 0.0, pltpu.roll(value, 1, 0))
+
+
+def plane_modes(high, low):
+    sums = [h + l for h, l in zip(high, low)]
+    diffs = [h - l for h, l in zip(high, low)]
     sums_left, diffs_left = from_left(*sums), from_left(*diffs)
     out = []
     for block in range(2):
         s, d, sl, dl = sums[block], diffs[block], sums_left[block], diffs_left[block]
         out.append((s + sl, d + dl, s - sl, d - dl))
     return out
+
+
+def store_modes(mode_ref, at, field, kinds, high, low=None):
+    found = plane_modes(high, [below(value) for value in high] if low is None else low)
+    for block in range(2):
+        for kind in range(kinds):
+            mode_ref[at, kinds * field + kind, block] = found[block][kind]
 
 
 def element_modes(low, high):
@@ -146,12 +155,6 @@
     return modulus * (ONE * one + TWO * two + THREE * three)
 
 
-def store_modes(mode_ref, at, field, kinds, read, cells):
-    for block, found in enumerate(plane_modes(read, cells)):
-        for kind in range(kinds):
-            mode_ref[at, kinds * field + kind, block] = found[kind]
-
-
 def face_forces(forces):
     upper, lower = [], []
     for component in range(3):
@@ -183,7 +186,7 @@
     return [here(0, block) + above(2, block) + beside[block] for block in range(2)]
 
 
-def inner_kernel(own_ref, mate_ref, node_ref, elem_ref, image_ref, edge_mode_ref, edge_part_ref, sums_ref, mode_ref, part_ref):
+def inner_kernel(own_ref, mate_ref, node_ref, elem_ref, image_ref, edge_part_ref, sums_ref, outer_mode_ref, image_mode_ref, mode_ref, part_ref):
     core = lax.axis_index("gy")
     cells, width = own_ref.shape[2:]
     tiles = cells // 8
@@ -198,13 +201,13 @@
     @pl.loop(0, 4)
     def _(x):
         for field in range(3):
-            read = lambda block, start, size: node_ref[x, field, block, start : start + size, :]
-            store_modes(mode_ref, x, field, 4, read, cells)
-
-    edge_mode_ref[...] = mode_ref[3 * core]
+            high, low = ([node_ref[x, field, block, at : at + cells, :] for block in range(2)] for at in (8, 7))
+            store_modes(mode_ref, x, field, 4, high, low)
+
+    outer_mode_ref[2 * (1 - core)] = mode_ref[3 * core]
     part_ref[:, :, :, cells : cells + 8, :] = zeros(2, 12, 2, 8, width)
 
-    @pl.loop(0, 2 * tiles)
+    @pl.loop(0, 2 * tiles, unroll=True)
     def _(t):
         block, rows = t // tiles, pl.ds(pl.multiple_of((t % tiles) * 8, 8), 8)
         load = lambda x: [[mode_ref[x, 4 * f + k, block, rows, :] for k in range(4)] for f in range(3)]
@@ -228,7 +231,9 @@
     for i in range(2):
         mine = jnp.where(core == i, 1.0, 0.0)
         for f in range(3):
-            for block, value in enumerate(assembled(part_ref, i, f, cells)):
+            values = assembled(part_ref, i, f, cells)
+            store_modes(image_mode_ref, jnp.where(core == 0, 2 + i, i), f, 4, values)
+            for block, value in enumerate(values):
                 image_ref[i, f, block] = value
                 force = node_ref[i + 1, f, block, 8 : 8 + cells, :]
                 norm = norm + mine * fold(force * force)
@@ -239,78 +244,62 @@
 
 
 def outer_kernel(
-    node_ref, elem_ref, image_ref, edge_mode_ref, edge_part_ref, part_sums_ref, same_ref, cross_ref,
-    give_ref, sums_ref, halo_ref, halo_elem_ref, mode_ref, part_ref, image_mode_ref,
+    node_ref, elem_ref, edge_part_ref, part_sums_ref, same_ref, cross_ref, _outer_mode, _image_mode,
+    give_ref, sums_ref, mode_ref, image_mode_ref, part_ref, halo_elem_ref,
 ):
     core, slab = lax.axis_index("gy"), lax.axis_index("gx")
     cells, width = same_ref.shape[2:]
     tiles = cells // 8
     zeros = lambda *dims: jnp.zeros(dims, jnp.float32)
     near = 1 - core
-    halo_ref[:, :, :, 0:8, :] = zeros(2, 3, 2, 8, width)
+    first_core = core == 0
     for i in range(2):
-        for ref, block in ((same_ref, core), (cross_ref, 1 - core)):
-            for field in range(3):
-                halo_ref[i, field, block, 8 : 8 + cells, :] = ref[i, field]
-            halo_elem_ref[i, block] = ref[i, 3]
-
-    mode_ref[2 * near] = edge_mode_ref[...]
-
-    @pl.loop(0, 2)
-    def _(i):
-        for field in range(3):
-            read = lambda block, start, size: halo_ref[i, field, block, start : start + size, :]
-            store_modes(mode_ref, core + i, field, 4, read, cells)
+        for f in range(4):
+            same, cross = same_ref[i, f], cross_ref[i, f]
+            values = [jnp.where(first_core, same, cross), jnp.where(first_core, cross, same)]
+            if f < 3:
+                store_modes(mode_ref, core + i, f, 4, values)
+            else:
+                halo_elem_ref[i, 0], halo_elem_ref[i, 1] = values
+    for f in range(4):
+        give_ref[6 + f, core] = same_ref[near, f]
+        give_ref[6 + f, near] = cross_ref[near, f]
 
     part_ref[:, :, :, cells : cells + 8, :] = zeros(2, 12, 2, 8, width)
 
-    @pl.loop(0, 2 * tiles)
+    @pl.loop(0, 2 * tiles, unroll=True)
     def _(t):
         block, rows = t // tiles, pl.ds(pl.multiple_of((t % tiles) * 8, 8), 8)
         load = lambda x: [[mode_ref[x, 4 * f + k, block, rows, :] for k in range(4)] for f in range(3)]
         planes = [load(x) for x in range(3)]
-        first = jnp.where(core == 0, halo_elem_ref[1, block, rows, :], halo_elem_ref[0, block, rows, :])
-        second = jnp.where(core == 0, elem_ref[0, block, rows, :], halo_elem_ref[1, block, rows, :])
+        first = halo_elem_ref[near, block, rows, :]
+        second = jnp.where(first_core, elem_ref[0, block, rows, :], halo_elem_ref[1, block, rows, :])
         upper, lower = face_forces(mode_forces(element_modes(planes[0], planes[1]), first))
         upper2, lower2 = face_forces(mode_forces(element_modes(planes[1], planes[2]), second))
         for f, modes in enumerate(plus(upper, lower2)):
             for k, value in enumerate(corner_forces(modes)):
                 part_ref[0, 4 * f + k, block, rows, :] = value
         for f in range(3):
-            modes = [
-                edge_part_ref[4 * f + k, block, rows, :] + jnp.where(core == 0, upper2[f][k], lower[f][k]) for k in range(4)
-            ]
+            modes = [edge_part_ref[4 * f + k, block, rows, :] + jnp.where(first_core, upper2[f][k], lower[f][k]) for k in range(4)]
             for k, value in enumerate(corner_forces(modes)):
                 part_ref[1, 4 * f + k, block, rows, :] = value
 
-    clamped = jnp.where((core == 0) & (slab == 0), 0.0, 1.0)
+    clamped = jnp.where(first_core & (slab == 0), 0.0, 1.0)
     fold = lambda value: value.reshape(tiles, 8, width).sum(0)
     norm, cross, square = (part_sums_ref[k] for k in range(3))
-    row = lax.broadcasted_iota(jnp.int32, (cells, width), 0)
-    below = lambda value: jnp.where(row == 0, 0.0, pltpu.roll(value, 1, 0))
     for f in range(3):
-        value = assembled(part_ref, 0, f, cells)
+        values = [value * clamped for value in assembled(part_ref, 0, f, cells)]
+        store_modes(image_mode_ref, 3 * core, f, 4, values)
         for block in range(2):
-            give_ref[f, block] = value[block] * clamped
-            give_ref[6 + f, block] = halo_ref[near, f, block, 8 : 8 + cells, :]
-        for block, value in enumerate(assembled(part_ref, 1, f, cells)):
+            give_ref[f, block] = values[block]
+        values = assembled(part_ref, 1, f, cells)
+        store_modes(image_mode_ref, 1 + core, f, 4, values)
+        for block, value in enumerate(values):
             give_ref[3 + f, block] = value
             force = node_ref[3 * core, f, block, 8 : 8 + cells, :]
             norm = norm + fold(force * force)
             cross = cross + fold(force * value)
             square = square + fold(value * value)
-    for block in range(2):
-        give_ref[9, block] = halo_elem_ref[near, block]
-
-    @pl.loop(0, 3)
-    def _(i):
-        for field in range(3):
-            def read(block, start, size):
-                inner = image_ref[jnp.where(core == 0, 0, jnp.minimum(i, 1)), field, block]
-                outer = give_ref[jnp.where(core == 0, 3 * jnp.minimum(i, 1), 3) + field, block]
-                value = jnp.where((i == 2) == (core == 0), inner, outer)
-                return value if start == 8 else below(value)
-            store_modes(image_mode_ref, i, field, 4, read, cells)
 
     def energy_of(t, total):
         block, rows = t // tiles, pl.ds(pl.multiple_of((t % tiles) * 8, 8), 8)
@@ -322,7 +311,7 @@
             low = high
         return total
 
-    energy = lax.fori_loop(0, 2 * tiles, energy_of, zeros(8, width))
+    energy = lax.fori_loop(0, 2 * tiles, energy_of, zeros(8, width), unroll=True)
     line = lax.broadcasted_iota(jnp.int32, (8, width), 0)
     packed = zeros(8, width)
     for k, value in enumerate((norm, cross, square, energy)):
@@ -339,7 +328,6 @@
     tiles = cells // 8
     row = lax.broadcasted_iota(jnp.int32, (cells, width), 0)
     lane = lanes((cells, width))
-    below = lambda value: jnp.where(row == 0, 0.0, pltpu.roll(value, 1, 0))
     part_ref[:, :, :, cells : cells + 8, :] = jnp.zeros((4, 6, 2, 8, width), jnp.float32)
     mine, other = 5 * core, 5 * (1 - core)
 
@@ -365,12 +353,9 @@
         @pl.loop(0, 6)
         def _(x):
             for field in range(3):
-                def read(block, start, size):
-                    value = plane_ref[x, field, block]
-                    return value if start == 8 else below(value)
-                store_modes(mode_ref, x, field, 3, read, cells)
-
-        @pl.loop(0, 2 * tiles)
+                store_modes(mode_ref, x, field, 3, [plane_ref[x, field, block] for block in range(2)])
+
+        @pl.loop(0, 2 * tiles, unroll=True)
         def _(t):
             block, rows = t // tiles, pl.ds(pl.multiple_of((t % tiles) * 8, 8), 8)
             load = lambda x: [[mode_ref[x, 3 * f + k, block, rows, :] for k in range(3)] for f in range(3)]
@@ -458,42 +443,39 @@
     cross_in = lax.ppermute(cross, both, pairs + [(q, p) for p, q in pairs])
     same_in = lax.ppermute(same, both, up + down)
 
-    node, elem, image, edge_mode, edge_part, part_sums = pl.pallas_call(
+    modes = lambda planes: shape(planes, 12, 2, cells, width)
+    node, elem, image, edge_part, part_sums, outer_mode, image_mode = pl.pallas_call(
         inner_kernel,
         out_shape=(
             shape(4, 3, 2, 8 + cells, width),
             shape(4, 2, cells, width),
             shape(2, 3, 2, cells, width),
             shape(12, 2, cells, width),
-            shape(12, 2, cells, width),
             shape(3, 8, width),
+            modes(3),
+            modes(4),
         ),
         in_specs=[VMEM] * 2,
-        out_specs=[VMEM] * 6,
+        out_specs=[VMEM] * 7,
         scratch_shapes=[scratch(4, 12, 2, cells, width), scratch(2, 12, 2, 8 + cells, width)],
         compiler_params=LIMIT,
         cost_estimate=cost(20_000_000, 4_000_000),
         name="inner",
     )(own, mate)
-    give, sums = pl.pallas_call(
+    give, sums, _, _ = pl.pallas_call(
         outer_kernel,
-        out_shape=(shape(10, 2, cells, width), shape(slabs * cores, 8, width)),
+        out_shape=(shape(10, 2, cells, width), shape(slabs * cores, 8, width), modes(3), modes(4)),
         in_specs=[VMEM] * 8,
-        out_specs=[VMEM] * 2,
-        scratch_shapes=[
-            scratch(2, 3, 2, 8 + cells, width),
-            scratch(2, 2, cells, width),
-            scratch(3, 12, 2, cells, width),
-            scratch(2, 12, 2, 8 + cells, width),
-            scratch(3, 12, 2, cells, width),
-        ],
+        out_specs=[VMEM] * 4,
+        input_output_aliases={6: 2, 7: 3},
+        scratch_shapes=[scratch(2, 12, 2, 8 + cells, width), scratch(2, 2, cells, width)],
         compiler_params=LIMIT,
         cost_estimate=cost(10_000_000, 3_000_000),
         name="outer",
-    )(node, elem, image, edge_mode, edge_part, part_sums, same_in, cross_in)
+    )(node, elem, edge_part, part_sums, same_in, cross_in, outer_mode, image_mode)
 
     take = lax.ppermute(give, "gy", [(0, 1), (1, 0)])
-    sums = lax.all_to_all(sums, both, 0, 0)
+    sums = lax.all_to_all(sums, both, 0, 0, axis_index_groups=[list(range(slabs * cores))[::-1]])
     basis = pl.pallas_call(
         stress_kernel,
         out_shape=shape(15, cells * 4, width),

time: 29.7 us -> 26.5 us (0.89)
  waiting for transfers between devices: 6.01 us -> 2.25 us
  starting transfers between devices: 14.5 us -> 15.8 us
  Pallas kernels: 8.3 us -> 7.57 us
    all_to_all x1, waiting for transfers between devices: 4.12 us -> 0.44 us  [per_device(): lax.all_to_all(sums, both, 0, 0, axis_index_groups=[list(range(slabs * co...]
    all_to_all x1, starting transfers between devices: 5.89 us -> 7.19 us  [per_device(): lax.all_to_all(sums, both, 0, 0, axis_index_groups=[list(range(slabs * co...]
    pallas_call x1, Pallas kernels: 2.28 us -> 1.73 us  [per_device(): pl.pallas_call(outer_kernel, out_shape=(shape(10, 2, cells, width), shape...]
  transfers between devices with their start and end apart: 5 -> 5, of which waited for: 2 -> 2; matrix products, arithmetic and copies ran while one was open for 0% -> 0% of each run, Pallas kernels for 14% -> 15%
where the time goes in v3:
time: 26.5 us; the launch traced here: 26.3 us
  starting transfers between devices  15.8 us (60%)
  Pallas kernels  7.57 us (29%)
  waiting for transfers between devices  2.25 us (8%)
  between operations  0.68 us (3%)
    all_to_all x1, starting transfers between devices, per_device(): lax.all_to_all(sums, both, 0, 0, axis_index_groups=[list(range(slabs * co...  7.19 us
    ppermute x1, starting transfers between devices, per_device(): same_in = lax.ppermute(same, both, up + down)  4.41 us
    ppermute x1, starting transfers between devices, per_device(): take = lax.ppermute(give, 'gy', [(0, 1), (1, 0)])  3.01 us
    pallas_call x1, Pallas kernels, per_device(): pl.pallas_call(stress_kernel, out_shape=shape(15, cells * 4, width), in_s...  2.5 us
    ppermute x1, waiting for transfers between devices, per_device(): same_in = lax.ppermute(same, both, up + down)  1.8 us
    pallas_call x1, Pallas kernels, per_device(): pl.pallas_call(outer_kernel, out_shape=(shape(10, 2, cells, width), shape...  1.73 us
    pallas_call x1, Pallas kernels, per_device(): pl.pallas_call(inner_kernel, out_shape=(shape(4, 3, 2, 8 + cells, width),...  1.37 us
    pallas_call x1, Pallas kernels, per_device(): pl.pallas_call(combine_kernel, out_shape=(shape(3, cells * 4, width), sha...  0.99 us
  transfers between devices with their start and end apart: 5, of which 2 were waited for; matrix products, arithmetic and copies ran while one was open for 0% of the time, Pallas kernels for 15%

profile of v3, /device:TPU:0, one launch (start us, length us, event | category | flops | bytes accessed | tf_op | source)
XLA Modules:
  0.0 26.3 jit_solution(1827585999167961323)
XLA Ops:
  0.6 1.0 %pack.1 = (f32[3,128,128]{2,1,0:T(8,128)S(1)}, f32[4,4,32,128]{3,2,1,0:T(8,128)S(1)}, f32[2,4,32,128]{3,2,1,0:T(8,128)S(1)}, f32[2,4,32,128]{3,2,1,0:T(8,128)S(1)}) custom-call(f32[3,128,128]{2,1,0:T(8,128)} %bitcast.4, f32[128,128]{1,0:T(8,128)} %bitcast.5), custom_call_target="tpu_custom_call" | custom-call | tf_op jit(solution)/shard_map/pack/pallas_call | solution.py:426
  1.6 0.5 %collective-permute-start = (f32[4,4,32,128]{3,2,1,0:T(8,128)S(1)}, f32[4,4,32,128]{3,2,1,0:T(8,128)S(1)}, u32[]{:S(2)}, u32[]{:S(2)}) collective-permute-start(f32[4,4,32,128]{3,2,1,0:T(8,128)S(1)} %get-tuple-element.17.own_ref), channel_id=1, source_target_pairs={{0,1},{1,0},{2,3},{3,2},{4,5},{5,4},{6,7},{7,6},{8,9},{9,8},{10,11... | collective-permute-start | bytes 786440 | tf_op jit(solution)/shard_map/ppermute | solution.py:442
  2.1 4.4 %collective-permute-start.1 = (f32[2,4,32,128]{3,2,1,0:T(8,128)S(1)}, f32[2,4,32,128]{3,2,1,0:T(8,128)S(1)}, u32[]{:S(2)}, u32[]{:S(2)}) collective-permute-start(f32[2,4,32,128]{3,2,1,0:T(8,128)S(1)} %get-tuple-element.22), channel_id=1, source_target_pairs={{0,2},{2,4},{4,6},{6,8},{8,10},{10,12},{12,14},{3,1},{5,3},{7,5},{... | collective-permute-start | bytes 393224 | tf_op jit(solution)/shard_map/ppermute | solution.py:444
  6.6 0.7 %collective-permute-start.2 = (f32[2,4,32,128]{3,2,1,0:T(8,128)S(1)}, f32[2,4,32,128]{3,2,1,0:T(8,128)S(1)}, u32[]{:S(2)}, u32[]{:S(2)}) collective-permute-start(f32[2,4,32,128]{3,2,1,0:T(8,128)S(1)} %get-tuple-element.23), channel_id=1, source_target_pairs={{1,2},{3,4},{5,6},{7,8},{9,10},{11,12},{13,14},{2,1},{4,3},{6,5},{... | collective-permute-start | bytes 393224 | tf_op jit(solution)/shard_map/ppermute | solution.py:443
  7.2 0.0 collective-permute-done.mate_ref
  7.2 1.4 %inner.1 = (f32[4,3,2,40,128]{4,3,2,1,0:T(8,128)S(1)}, f32[4,2,32,128]{3,2,1,0:T(8,128)S(1)}, f32[2,3,2,32,128]{4,3,2,1,0:T(8,128)S(1)}, f32[12,2,32,128]{3,2,1,...) custom-call(f32[4,4,32,128]{3,2,1,0:T(8,128)S(1)} %get-tuple-element, ...), custom_call_target="tpu_custom_call" | custom-call | flops 20000000 | bytes 4000000 | tf_op jit(solution)/shard_map/inner/pallas_call | solution.py:447
  8.6 1.8 %collective-permute-done.1.same_ref = f32[2,4,32,128]{3,2,1,0:T(8,128)S(1)} collective-permute-done((f32[2,4,32,128]{3,2,1,0:T(8,128)S(1)}, f32[2,4,32,128]{3,2,1,0:T(8,128)S(1)}, u32[]{:S(2)}, u32[]{:S(2)}) %collective-permute-start.1) | collective-permute-done | bytes 131104 | tf_op jit(solution)/shard_map/ppermute | solution.py:444
  10.4 0.0 collective-permute-done.2.cross_ref
  10.4 1.7 %outer.1 = (f32[10,2,32,128]{3,2,1,0:T(8,128)S(1)}, f32[16,8,128]{2,1,0:T(8,128)}, f32[3,12,2,32,128]{4,3,2,1,0:T(8,128)S(1)}, f32[4,12,2,32,128]{4,3,2,1,0:T(8,128)S(1)}) custom-call(f32[4,3,2,40,128]{4,3,2,1,0:T(8,128)S(1)} %get-tuple-element.18.node_ref, ...), custom_call_target="tpu_custom_call", output_to_operand_aliasing={{2}: (6, {}), {3}: (7, {})} | custom-call | flops 10000000 | bytes 3000000 | tf_op jit(solution)/shard_map/outer/pallas_call | solution.py:465
  12.2 3.0 %collective-permute-start.3 = (f32[10,2,32,128]{3,2,1,0:T(8,128)S(1)}, f32[10,2,32,128]{3,2,1,0:T(8,128)S(1)}, u32[]{:S(2)}, u32[]{:S(2)}) collective-permute-start(f32[10,2,32,128]{3,2,1,0:T(8,128)S(1)} %get-tuple-element.29.give_ref), channel_id=1, source_target_pairs={{0,1},{1,0},{2,3},{3,2},{4,5},{5,4},{6,7},{7,6},{8,9},{9,8},{10,11... | collective-permute-start | bytes 983048 | tf_op jit(solution)/shard_map/ppermute | solution.py:477
  15.2 7.2 %all-to-all-start = ((f32[16,8,128]{2,1,0:T(8,128)}), f32[16,8,128]{2,1,0:T(8,128)S(1)}, u32[]{:S(2)}, u32[]{:S(2)}) async-start(f32[16,8,128]{2,1,0:T(8,128)} %get-tuple-element.26), calls=%async_computation | async-start | bytes 131072 | tf_op jit(solution)/shard_map/all_to_all | solution.py:478
  22.4 0.0 collective-permute-done.3.take_ref
  22.4 2.5 %stress.1.basis_ref = f32[15,128,128]{2,1,0:T(8,128)S(1)} custom-call(f32[4,3,2,40,128]{4,3,2,1,0:T(8,128)S(1)} %get-tuple-element.18.node_ref, f32[4,2,32,128]{3,2,1,0:T(8,128)S(1)} %get-tuple-element.19.elem_ref, f32[2,3,2,32,128]{4,3,2,1,0:T(8,128)S(1)} %get-tuple-element.28.image_ref, f32[10,2,32,128]{3,2,1,0:T(8,128)S(1)} %get-tuple-element.29.give_ref, ...), custom_call_target="tpu_custom_call" | custom-call | flops 20000000 | bytes 4000000 | tf_op jit(solution)/shard_map/stress/pallas_call | solution.py:479
  24.9 0.4 %all-to-all-done.sums_ref = f32[16,8,128]{2,1,0:T(8,128)S(1)} async-done(((f32[16,8,128]{2,1,0:T(8,128)}), f32[16,8,128]{2,1,0:T(8,128)S(1)}, u32[]{:S(2)}, u32[]{:S(2)}) %all-to-all-start) | async-done | bytes 65568 | tf_op jit(solution)/shard_map/all_to_all | solution.py:478
  25.3 1.0 %combine.1 = (f32[3,128,128]{2,1,0:T(8,128)}, f32[6,128,128]{2,1,0:T(8,128)}) custom-call(f32[16,8,128]{2,1,0:T(8,128)S(1)} %all-to-all-done.sums_ref, f32[3,128,128]{2,1,0:T(8,128)S(1)} %get-tuple-element.27.force_ref, f32[15,128,128]{2,1,0:T(8,128)S(1)} %stress.1.basis_ref), custom_call_target="tpu_custom_call" | custom-call | tf_op jit(solution)/shard_map/combine/pallas_call | solution.py:495
Async XLA Ops:
  1.6 5.6 %collective-permute-start = (f32[4,4,32,128]{3,2,1,0:T(8,128)S(1)}, f32[4,4,32,128]{3,2,1,0:T(8,128)S(1)}, u32[]{:S(2)}, u32[]{:S(2)}) collective-permute-start(f32[4,4,32,128]{3,2,1,0:T(8,128)S(1)} %get-tuple-element.17.own_ref), channel_id=1, source_target_pairs={{0,1},{1,0},{2,3},{3,2},{4,5},{5,4},{6,7},{7,6},{8,9},{9,8},{10,11... | collective-permute-start | bytes 786440 | tf_op jit(solution)/shard_map/ppermute | solution.py:442
  2.1 8.3 %collective-permute-start.1 = (f32[2,4,32,128]{3,2,1,0:T(8,128)S(1)}, f32[2,4,32,128]{3,2,1,0:T(8,128)S(1)}, u32[]{:S(2)}, u32[]{:S(2)}) collective-permute-start(f32[2,4,32,128]{3,2,1,0:T(8,128)S(1)} %get-tuple-element.22), channel_id=1, source_target_pairs={{0,2},{2,4},{4,6},{6,8},{8,10},{10,12},{12,14},{3,1},{5,3},{7,5},{... | collective-permute-start | bytes 393224 | tf_op jit(solution)/shard_map/ppermute | solution.py:444
  6.6 3.9 %collective-permute-start.2 = (f32[2,4,32,128]{3,2,1,0:T(8,128)S(1)}, f32[2,4,32,128]{3,2,1,0:T(8,128)S(1)}, u32[]{:S(2)}, u32[]{:S(2)}) collective-permute-start(f32[2,4,32,128]{3,2,1,0:T(8,128)S(1)} %get-tuple-element.23), channel_id=1, source_target_pairs={{1,2},{3,4},{5,6},{7,8},{9,10},{11,12},{13,14},{2,1},{4,3},{6,5},{... | collective-permute-start | bytes 393224 | tf_op jit(solution)/shard_map/ppermute | solution.py:443
  12.2 10.2 %collective-permute-start.3 = (f32[10,2,32,128]{3,2,1,0:T(8,128)S(1)}, f32[10,2,32,128]{3,2,1,0:T(8,128)S(1)}, u32[]{:S(2)}, u32[]{:S(2)}) collective-permute-start(f32[10,2,32,128]{3,2,1,0:T(8,128)S(1)} %get-tuple-element.29.give_ref), channel_id=1, source_target_pairs={{0,1},{1,0},{2,3},{3,2},{4,5},{5,4},{6,7},{7,6},{8,9},{9,8},{10,11... | collective-permute-start | bytes 983048 | tf_op jit(solution)/shard_map/ppermute | solution.py:477
  15.2 10.1 %all-to-all-start = ((f32[16,8,128]{2,1,0:T(8,128)}), f32[16,8,128]{2,1,0:T(8,128)S(1)}, u32[]{:S(2)}, u32[]{:S(2)}) async-start(f32[16,8,128]{2,1,0:T(8,128)} %get-tuple-element.26), calls=%async_computation | async-start | bytes 131072 | tf_op jit(solution)/shard_map/all_to_all | solution.py:478

commit v4 on v3

--- a/solution.py
+++ b/solution.py
@@ -35,7 +35,7 @@
     return jnp.where(edge, turned2, turned), jnp.where(edge, 0.0, turned2)
 
 
-def pack_kernel(force_hbm, modulus_hbm, force_ref, own_ref, same_ref, cross_ref, modulus_ref, sem):
+def pack_kernel(force_hbm, modulus_hbm, own_ref, same_ref, cross_ref, force_ref, modulus_ref, sem):
     core = lax.axis_index("gy")
     cells = own_ref.shape[2]
     copies = [
@@ -64,22 +64,22 @@
     return jnp.where(row == 0, 0.0, pltpu.roll(value, 1, 0))
 
 
-def plane_modes(high, low):
-    sums = [h + l for h, l in zip(high, low)]
-    diffs = [h - l for h, l in zip(high, low)]
-    sums_left, diffs_left = from_left(*sums), from_left(*diffs)
-    out = []
+def store_modes(mode_ref, at, field, high, low=None, last_ref=None):
+    base = 4 * field if last_ref is None else 3 * field
+    left = from_left(*high)
     for block in range(2):
-        s, d, sl, dl = sums[block], diffs[block], sums_left[block], diffs_left[block]
-        out.append((s + sl, d + dl, s - sl, d - dl))
-    return out
-
-
-def store_modes(mode_ref, at, field, kinds, high, low=None):
-    found = plane_modes(high, [below(value) for value in high] if low is None else low)
-    for block in range(2):
-        for kind in range(kinds):
-            mode_ref[at, kinds * field + kind, block] = found[block][kind]
+        value, beside = high[block], left[block]
+        value_low = below(value) if low is None else low[block]
+        beside_low = below(beside)
+        total, total_beside = value + value_low, beside + beside_low
+        slope, slope_beside = value - value_low, beside - beside_low
+        mode_ref[at, base, block] = total + total_beside
+        mode_ref[at, base + 1, block] = slope + slope_beside
+        mode_ref[at, base + 2, block] = total - total_beside
+        if last_ref is None:
+            mode_ref[at, base + 3, block] = slope - slope_beside
+        else:
+            last_ref[at, field, block] = slope - slope_beside
 
 
 def element_modes(low, high):
@@ -179,6 +179,10 @@
     return [[p + q for p, q in zip(a, b)] for a, b in zip(first, second)]
 
 
+def pick(flag, first, second):
+    return [[jnp.where(flag, p, q) for p, q in zip(a, b)] for a, b in zip(first, second)]
+
+
 def assembled(part_ref, at, field, cells):
     here = lambda k, block: part_ref[at, 4 * field + k, block, 0:cells, :]
     above = lambda k, block: part_ref[at, 4 * field + k, block, 1 : cells + 1, :]
@@ -186,7 +190,38 @@
     return [here(0, block) + above(2, block) + beside[block] for block in range(2)]
 
 
-def inner_kernel(own_ref, mate_ref, node_ref, elem_ref, image_ref, edge_part_ref, sums_ref, outer_mode_ref, image_mode_ref, mode_ref, part_ref):
+def mode_stress(low, high, modulus):
+    by_z = [high[f][1] + low[f][1] for f in range(3)]
+    by_x = [high[f][0] - low[f][0] for f in range(3)]
+    by_y = [high[f][2] + low[f][2] for f in range(3)]
+    scaled = modulus * (0.25 * SHEAR)
+    trace = RATIO * (by_z[0] + by_x[1] + by_y[2])
+    return [
+        scaled * (trace + 2.0 * by_z[0]),
+        scaled * (trace + 2.0 * by_x[1]),
+        scaled * (trace + 2.0 * by_y[2]),
+        scaled * (by_x[0] + by_z[1]),
+        scaled * (by_y[1] + by_x[2]),
+        scaled * (by_y[0] + by_z[2]),
+    ]
+
+
+def nodal_average(part_ref, at, k, core, count_x):
+    cells, width = part_ref.shape[3] - 8, part_ref.shape[4]
+    both = [part_ref[at, k, block, 0:cells, :] + part_ref[at, k, block, 1 : cells + 1, :] for block in range(2)]
+    first, second = both
+    lane = lanes((cells, width))
+    row = lax.broadcasted_iota(jnp.int32, (cells, width), 0)
+    mine = jnp.where(core == 0, first, second)
+    turned = pltpu.roll(jnp.where(lane == 0, jnp.where(core == 0, second, 0.0), mine), width - 1, 1)
+    count = jnp.where(row == cells - 1, 1.0, 0.5) * jnp.where((lane == width - 1) & (core == 1), 1.0, 0.5)
+    return (mine + turned) * (count * count_x)
+
+
+def inner_kernel(
+    own_ref, mate_ref, ends_ref, elem_ref, edge_part_ref, sums_ref, edge_mode_ref, image_mode_ref, image_last_ref, side_ref, early_ref,
+    node_ref, mode_ref, part_ref, stress_part_ref,
+):
     core = lax.axis_index("gy")
     cells, width = own_ref.shape[2:]
     tiles = cells // 8
@@ -196,16 +231,19 @@
         for ref, block in ((own_ref, core), (mate_ref, 1 - core)):
             for field in range(3):
                 node_ref[x, field, block, 8 : 8 + cells, :] = ref[x, field]
+                if x in (0, 3):
+                    ends_ref[x // 3, field, block] = ref[x, field]
             elem_ref[x, block] = ref[x, 3]
 
     @pl.loop(0, 4)
     def _(x):
         for field in range(3):
             high, low = ([node_ref[x, field, block, at : at + cells, :] for block in range(2)] for at in (8, 7))
-            store_modes(mode_ref, x, field, 4, high, low)
-
-    outer_mode_ref[2 * (1 - core)] = mode_ref[3 * core]
+            store_modes(mode_ref, x, field, high, low)
+
+    edge_mode_ref[...] = mode_ref[3 * core]
     part_ref[:, :, :, cells : cells + 8, :] = zeros(2, 12, 2, 8, width)
+    stress_part_ref[:, :, :, cells : cells + 8, :] = zeros(2, 6, 2, 8, width)
 
     @pl.loop(0, 2 * tiles, unroll=True)
     def _(t):
@@ -226,26 +264,44 @@
             for k in range(4):
                 edge_part_ref[4 * f + k, block, rows, :] = jnp.where(core == 0, outer[f][k], kept[f][k])
 
+    @pl.loop(0, 2 * tiles, unroll=True)
+    def _(t):
+        block, rows = t // tiles, pl.ds(pl.multiple_of((t % tiles) * 8, 8), 8)
+        load = lambda x: [[mode_ref[x, 4 * f + k, block, rows, :] for k in range(3)] for f in range(3)]
+        low, kept = load(0), None
+        for x in range(1, 4):
+            high = load(x)
+            now = mode_stress(low, high, elem_ref[x, block, rows, :])
+            for k in range(6):
+                if x > 1:
+                    stress_part_ref[x - 2, k, block, rows, :] = kept[k] + now[k]
+                if x != 2:
+                    side_ref[x // 2, k, block, rows, :] = now[k]
+            low, kept = high, now
+
     fold = lambda value: value.reshape(tiles, 8, width).sum(0)
     norm = cross = square = zeros(8, width)
     for i in range(2):
         mine = jnp.where(core == i, 1.0, 0.0)
         for f in range(3):
             values = assembled(part_ref, i, f, cells)
-            store_modes(image_mode_ref, jnp.where(core == 0, 2 + i, i), f, 4, values)
+            store_modes(image_mode_ref, i, f, values, last_ref=image_last_ref)
+            early_ref[i, 6 + f] = jnp.where(core == 0, values[0], values[1])
+            early_ref[i, 9 + f] = own_ref[1 + i, f]
             for block, value in enumerate(values):
-                image_ref[i, f, block] = value
                 force = node_ref[i + 1, f, block, 8 : 8 + cells, :]
                 norm = norm + mine * fold(force * force)
                 cross = cross + mine * fold(force * value)
                 square = square + mine * fold(value * value)
+        for k in range(6):
+            early_ref[i, k] = nodal_average(stress_part_ref, i, k, core, 0.5)
     for k, value in enumerate((norm, cross, square)):
         sums_ref[k] = value
 
 
 def outer_kernel(
-    node_ref, elem_ref, edge_part_ref, part_sums_ref, same_ref, cross_ref, _outer_mode, _image_mode,
-    give_ref, sums_ref, mode_ref, image_mode_ref, part_ref, halo_elem_ref,
+    ends_ref, elem_ref, edge_part_ref, part_sums_ref, edge_mode_ref, image_mode_ref, image_last_ref, same_ref, cross_ref,
+    give_ref, sums_ref, halo_mode_ref, face_mode_ref, part_ref, halo_elem_ref,
 ):
     core, slab = lax.axis_index("gy"), lax.axis_index("gx")
     cells, width = same_ref.shape[2:]
@@ -258,7 +314,7 @@
             same, cross = same_ref[i, f], cross_ref[i, f]
             values = [jnp.where(first_core, same, cross), jnp.where(first_core, cross, same)]
             if f < 3:
-                store_modes(mode_ref, core + i, f, 4, values)
+                store_modes(halo_mode_ref, i, f, values)
             else:
                 halo_elem_ref[i, 0], halo_elem_ref[i, 1] = values
     for f in range(4):
@@ -270,8 +326,10 @@
     @pl.loop(0, 2 * tiles, unroll=True)
     def _(t):
         block, rows = t // tiles, pl.ds(pl.multiple_of((t % tiles) * 8, 8), 8)
-        load = lambda x: [[mode_ref[x, 4 * f + k, block, rows, :] for k in range(4)] for f in range(3)]
-        planes = [load(x) for x in range(3)]
+        load = lambda at: [[halo_mode_ref[at, 4 * f + k, block, rows, :] for k in range(4)] for f in range(3)]
+        edge = [[edge_mode_ref[4 * f + k, block, rows, :] for k in range(4)] for f in range(3)]
+        halo = [load(0), load(1)]
+        planes = [pick(first_core, halo[0], edge), pick(first_core, halo[1], halo[0]), pick(first_core, edge, halo[1])]
         first = halo_elem_ref[near, block, rows, :]
         second = jnp.where(first_core, elem_ref[0, block, rows, :], halo_elem_ref[1, block, rows, :])
         upper, lower = face_forces(mode_forces(element_modes(planes[0], planes[1]), first))
@@ -289,24 +347,30 @@
     norm, cross, square = (part_sums_ref[k] for k in range(3))
     for f in range(3):
         values = [value * clamped for value in assembled(part_ref, 0, f, cells)]
-        store_modes(image_mode_ref, 3 * core, f, 4, values)
+        store_modes(face_mode_ref, 0, f, values)
         for block in range(2):
             give_ref[f, block] = values[block]
         values = assembled(part_ref, 1, f, cells)
-        store_modes(image_mode_ref, 1 + core, f, 4, values)
+        store_modes(face_mode_ref, 1, f, values)
         for block, value in enumerate(values):
             give_ref[3 + f, block] = value
-            force = node_ref[3 * core, f, block, 8 : 8 + cells, :]
+            force = ends_ref[core, f, block]
             norm = norm + fold(force * force)
             cross = cross + fold(force * value)
             square = square + fold(value * value)
 
     def energy_of(t, total):
         block, rows = t // tiles, pl.ds(pl.multiple_of((t % tiles) * 8, 8), 8)
-        load = lambda x: [[image_mode_ref[x, 4 * f + k, block, rows, :] for k in range(4)] for f in range(3)]
-        low = load(0)
+        load = lambda ref, at: [[ref[at, 4 * f + k, block, rows, :] for k in range(4)] for f in range(3)]
+        inner, beyond = (
+            [[image_mode_ref[at, 3 * f + k, block, rows, :] for k in range(3)] + [image_last_ref[at, f, block, rows, :]] for f in range(3)]
+            for at in range(2)
+        )
+        face = load(face_mode_ref, 1)
+        planes = [pick(first_core, load(face_mode_ref, 0), inner), pick(first_core, face, beyond), pick(first_core, inner, face)]
+        low = planes[0]
         for x in range(2):
-            high = load(x + 1)
+            high = planes[x + 1]
             total = total + mode_energy(element_modes(low, high), elem_ref[2 * core + x, block, rows, :])
             low = high
         return total
@@ -320,80 +384,58 @@
 
 
 def stress_kernel(
-    node_ref, elem_ref, image_ref, give_ref, take_ref, basis_ref, plane_ref, outer_elem_ref, mode_ref, part_ref,
+    ends_ref, elem_ref, image_mode_ref, side_ref, give_ref, take_ref,
+    late_ref, middle_ref, outer_mode_ref, face_mode_ref, part_ref, image_part_ref,
 ):
     core, slab = lax.axis_index("gy"), lax.axis_index("gx")
-    last = slab == lax.axis_size("gx") - 1
     cells, width = elem_ref.shape[2:]
     tiles = cells // 8
-    row = lax.broadcasted_iota(jnp.int32, (cells, width), 0)
-    lane = lanes((cells, width))
-    part_ref[:, :, :, cells : cells + 8, :] = jnp.zeros((4, 6, 2, 8, width), jnp.float32)
-    mine, other = 5 * core, 5 * (1 - core)
-
-    for which in range(2):
+    count_last = jnp.where(slab == lax.axis_size("gx") - 1, 1.0, 0.5)
+    zeros = lambda *dims: jnp.zeros(dims, jnp.float32)
+    part_ref[:, :, :, cells : cells + 8, :] = zeros(2, 6, 2, 8, width)
+    image_part_ref[:, :, :, cells : cells + 8, :] = zeros(4, 6, 2, 8, width)
+    for f in range(3):
+        for ref, mine in ((give_ref, core), (take_ref, 1 - core)):
+            blocks = lambda base: [ref[base + f, block] for block in range(2)]
+            store_modes(face_mode_ref, 3 * mine, f, blocks(0))
+            store_modes(face_mode_ref, 1 + mine, f, blocks(3))
+            store_modes(outer_mode_ref, 3 * mine, f, blocks(6))
+        for i in range(2):
+            store_modes(outer_mode_ref, 1 + i, f, [ends_ref[i, f, block] for block in range(2)])
+
+    @pl.loop(0, 2 * tiles, unroll=True)
+    def _(t):
+        block, rows = t // tiles, pl.ds(pl.multiple_of((t % tiles) * 8, 8), 8)
+        load = lambda ref, at, step=4: [[ref[at, step * f + k, block, rows, :] for k in range(3)] for f in range(3)]
+        given, taken = give_ref[9, block, rows, :], take_ref[9, block, rows, :]
+        modulus = [elem_ref[x, block, rows, :] for x in range(4)] + [jnp.where(core == 0, taken, given)]
+        lower = mode_stress(load(outer_mode_ref, 0), load(outer_mode_ref, 1), modulus[0])
+        upper = mode_stress(load(outer_mode_ref, 2), load(outer_mode_ref, 3), modulus[4])
+        for k in range(6):
+            part_ref[0, k, block, rows, :] = lower[k] + side_ref[0, k, block, rows, :]
+            part_ref[1, k, block, rows, :] = side_ref[1, k, block, rows, :] + upper[k]
+        planes = [(face_mode_ref, 0), (face_mode_ref, 1), (image_mode_ref, 0, 3), (image_mode_ref, 1, 3), (face_mode_ref, 2), (face_mode_ref, 3)]
+        low, kept = load(*planes[0]), None
+        for x in range(1, 6):
+            high = load(*planes[x])
+            now = mode_stress(low, high, modulus[x - 1])
+            if kept is not None:
+                for k in range(6):
+                    image_part_ref[x - 2, k, block, rows, :] = kept[k] + now[k]
+            low, kept = high, now
+
+    for i in range(2):
+        count = count_last if i else 0.5
+        for k in range(6):
+            late_ref[i, k] = nodal_average(part_ref, i, k, core, count)
+            late_ref[i, 12 + k] = nodal_average(image_part_ref, 3 * i, k, core, count)
+            middle_ref[i, k] = nodal_average(image_part_ref, 1 + i, k, core, 0.5)
         for f in range(3):
-            for block in range(2):
-                if which == 0:
-                    plane_ref[mine, f, block] = give_ref[6 + f, block]
-                    plane_ref[other, f, block] = take_ref[6 + f, block]
-                    for x in range(4):
-                        plane_ref[1 + x, f, block] = node_ref[x, f, block, 8 : 8 + cells, :]
-                else:
-                    plane_ref[mine, f, block] = give_ref[f, block]
-                    plane_ref[other, f, block] = take_ref[f, block]
-                    plane_ref[1 + 3 * core, f, block] = give_ref[3 + f, block]
-                    plane_ref[4 - 3 * core, f, block] = take_ref[3 + f, block]
-                    for x in range(2):
-                        plane_ref[2 + x, f, block] = image_ref[x, f, block]
-        if which == 0:
-            for block in range(2):
-                outer_elem_ref[block] = jnp.where(core == 0, take_ref[9, block], give_ref[9, block])
-
-        @pl.loop(0, 6)
-        def _(x):
-            for field in range(3):
-                store_modes(mode_ref, x, field, 3, [plane_ref[x, field, block] for block in range(2)])
-
-        @pl.loop(0, 2 * tiles, unroll=True)
-        def _(t):
-            block, rows = t // tiles, pl.ds(pl.multiple_of((t % tiles) * 8, 8), 8)
-            load = lambda x: [[mode_ref[x, 3 * f + k, block, rows, :] for k in range(3)] for f in range(3)]
-            low, kept = load(0), None
-            for x in range(1, 6):
-                high = load(x)
-                by_z = [high[f][1] + low[f][1] for f in range(3)]
-                by_x = [high[f][0] - low[f][0] for f in range(3)]
-                by_y = [high[f][2] + low[f][2] for f in range(3)]
-                scaled = (elem_ref[x - 1, block, rows, :] if x < 5 else outer_elem_ref[block, rows, :]) * (0.25 * SHEAR)
-                trace = RATIO * (by_z[0] + by_x[1] + by_y[2])
-                now = [
-                    scaled * (trace + 2.0 * by_z[0]),
-                    scaled * (trace + 2.0 * by_x[1]),
-                    scaled * (trace + 2.0 * by_y[2]),
-                    scaled * (by_x[0] + by_z[1]),
-                    scaled * (by_y[1] + by_x[2]),
-                    scaled * (by_y[0] + by_z[2]),
-                ]
-                if kept is not None:
-                    for k in range(6):
-                        part_ref[x - 2, k, block, rows, :] = kept[k] + now[k]
-                low, kept = high, now
-
-        for x in range(4):
-            count = jnp.where(row == cells - 1, 1.0, 0.5) * (jnp.where(last, 1.0, 0.5) if x == 3 else 0.5)
-            count = count * jnp.where((lane == width - 1) & (core == 1), 1.0, 0.5)
-            for k in range(6):
-                both = [part_ref[x, k, block, 0:cells, :] + part_ref[x, k, block, 1 : cells + 1, :] for block in range(2)]
-                beside = from_right(*both)
-                value = jnp.where(core == 0, both[0] + beside[0], both[1] + beside[1])
-                basis_ref[6 * which + k, pl.ds(x, cells, stride=4), :] = value * count
-    for x in range(4):
-        for f in range(3):
-            basis_ref[12 + f, pl.ds(x, cells, stride=4), :] = plane_ref[1 + x, f, core]
-
-
-def combine_kernel(sums_ref, force_ref, basis_ref, field_ref, stress_ref):
+            late_ref[i, 6 + f] = jnp.where(core == i, give_ref[3 + f, core], take_ref[3 + f, core])
+            late_ref[i, 9 + f] = ends_ref[i, f, core]
+
+
+def combine_kernel(sums_ref, early_ref, late_ref, middle_ref, field_ref, stress_ref):
     total = jnp.sum(jnp.sum(sums_ref[...], axis=0), axis=1, keepdims=True)
     norm, cross, square, energy = (total[k : k + 1, :] for k in range(4))
     first = norm / cross
@@ -402,12 +444,17 @@
     grown = 1.0 + ratio
     curvature = grown * grown * cross - 2.0 * grown * first * square + first * first * energy
     second = norm_next / curvature
-    weight = jnp.broadcast_to(first + second * grown, force_ref.shape[1:])
-    weight_image = jnp.broadcast_to(-second * first, force_ref.shape[1:])
-    for f in range(3):
-        field_ref[f] = weight * force_ref[f] + weight_image * basis_ref[12 + f]
-    for k in range(6):
-        stress_ref[k] = weight * basis_ref[k] + weight_image * basis_ref[6 + k]
+    weight = jnp.broadcast_to(first + second * grown, early_ref.shape[2:])
+    weight_image = jnp.broadcast_to(-second * first, early_ref.shape[2:])
+    cells = early_ref.shape[2]
+    for x in range(4):
+        rows, i = pl.ds(x, cells, stride=4), (0, 0, 1, 1)[x]
+        first_ref = late_ref if x in (0, 3) else early_ref
+        for f in range(3):
+            field_ref[f, rows, :] = weight * first_ref[i, 9 + f] + weight_image * first_ref[i, 6 + f]
+        for k in range(6):
+            image = late_ref[i, 12 + k] if x in (0, 3) else middle_ref[i, k]
+            stress_ref[k, rows, :] = weight * first_ref[i, k] + weight_image * image
 
 
 def cost(flops, size):
@@ -423,12 +470,12 @@
     shape = lambda *dims: jax.ShapeDtypeStruct(dims, f32)
     scratch = lambda *dims: pltpu.VMEM(dims, f32)
 
-    force, own, same, cross = pl.pallas_call(
+    own, same, cross = pl.pallas_call(
         pack_kernel,
-        out_shape=(shape(3, cells * 4, width), shape(4, 4, cells, width), shape(2, 4, cells, width), shape(2, 4, cells, width)),
+        out_shape=(shape(4, 4, cells, width), shape(2, 4, cells, width), shape(2, 4, cells, width)),
         in_specs=[pl.BlockSpec(memory_space=pl.ANY)] * 2,
-        out_specs=[VMEM] * 4,
-        scratch_shapes=[scratch(cells * 4, width), pltpu.SemaphoreType.DMA((2,))],
+        out_specs=[VMEM] * 3,
+        scratch_shapes=[scratch(3, cells * 4, width), scratch(cells * 4, width), pltpu.SemaphoreType.DMA((2,))],
         compiler_params=LIMIT,
         name="pack",
     )(
@@ -443,63 +490,73 @@
     cross_in = lax.ppermute(cross, both, pairs + [(q, p) for p, q in pairs])
     same_in = lax.ppermute(same, both, up + down)
 
-    modes = lambda planes: shape(planes, 12, 2, cells, width)
-    node, elem, image, edge_part, part_sums, outer_mode, image_mode = pl.pallas_call(
+    ends, elem, edge_part, part_sums, edge_mode, image_mode, image_last, side, early = pl.pallas_call(
         inner_kernel,
         out_shape=(
-            shape(4, 3, 2, 8 + cells, width),
+            shape(2, 3, 2, cells, width),
             shape(4, 2, cells, width),
-            shape(2, 3, 2, cells, width),
             shape(12, 2, cells, width),
             shape(3, 8, width),
-            modes(3),
-            modes(4),
+            shape(12, 2, cells, width),
+            shape(2, 9, 2, cells, width),
+            shape(2, 3, 2, cells, width),
+            shape(2, 6, 2, cells, width),
+            shape(2, 12, cells, width),
         ),
         in_specs=[VMEM] * 2,
-        out_specs=[VMEM] * 7,
-        scratch_shapes=[scratch(4, 12, 2, cells, width), scratch(2, 12, 2, 8 + cells, width)],
+        out_specs=[VMEM] * 9,
+        scratch_shapes=[
+            scratch(4, 3, 2, 8 + cells, width),
+            scratch(4, 12, 2, cells, width),
+            scratch(2, 12, 2, 8 + cells, width),
+            scratch(2, 6, 2, 8 + cells, width),
+        ],
         compiler_params=LIMIT,
         cost_estimate=cost(20_000_000, 4_000_000),
         name="inner",
     )(own, mate)
-    give, sums, _, _ = pl.pallas_call(
+    give, sums = pl.pallas_call(
         outer_kernel,
-        out_shape=(shape(10, 2, cells, width), shape(slabs * cores, 8, width), modes(3), modes(4)),
-        in_specs=[VMEM] * 8,
-        out_specs=[VMEM] * 4,
-        input_output_aliases={6: 2, 7: 3},
-        scratch_shapes=[scratch(2, 12, 2, 8 + cells, width), scratch(2, 2, cells, width)],
+        out_shape=(shape(10, 2, cells, width), shape(slabs * cores, 8, width)),
+        in_specs=[VMEM] * 9,
+        out_specs=[VMEM] * 2,
+        scratch_shapes=[
+            scratch(2, 12, 2, cells, width),
+            scratch(2, 12, 2, cells, width),
+            scratch(2, 12, 2, 8 + cells, width),
+            scratch(2, 2, cells, width),
+        ],
         compiler_params=LIMIT,
         cost_estimate=cost(10_000_000, 3_000_000),
         name="outer",
-    )(node, elem, edge_part, part_sums, same_in, cross_in, outer_mode, image_mode)
+    )(ends, elem, edge_part, part_sums, edge_mode, image_mode, image_last, same_in, cross_in)
 
     take = lax.ppermute(give, "gy", [(0, 1), (1, 0)])
     sums = lax.all_to_all(sums, both, 0, 0, axis_index_groups=[list(range(slabs * cores))[::-1]])
-    basis = pl.pallas_call(
+    late, middle = pl.pallas_call(
         stress_kernel,
-        out_shape=shape(15, cells * 4, width),
-        in_specs=[VMEM] * 5,
-        out_specs=VMEM,
+        out_shape=(shape(2, 18, cells, width), shape(2, 6, cells, width)),
+        in_specs=[VMEM] * 6,
+        out_specs=[VMEM] * 2,
         scratch_shapes=[
-            scratch(6, 3, 2, cells, width),
-            scratch(2, cells, width),
-            scratch(6, 9, 2, cells, width),
+            scratch(4, 12, 2, cells, width),
+            scratch(4, 12, 2, cells, width),
+            scratch(2, 6, 2, 8 + cells, width),
             scratch(4, 6, 2, 8 + cells, width),
         ],
         compiler_params=LIMIT,
         cost_estimate=cost(20_000_000, 4_000_000),
         name="stress",
-    )(node, elem, image, give, take)
+    )(ends, elem, image_mode, side, give, take)
 
     field, stress = pl.pallas_call(
         combine_kernel,
         out_shape=(shape(3, cells * 4, width), shape(6, cells * 4, width)),
-        in_specs=[VMEM] * 3,
+        in_specs=[VMEM] * 4,
         out_specs=[VMEM] * 2,
         compiler_params=LIMIT,
         name="combine",
-    )(sums, force, basis)
+    )(sums, early, late, middle)
     return field.reshape(3, cells, 4, width), stress.reshape(6, cells, 4, width)
 
 

time: 26.5 us -> 26.5 us (level)
  waiting for transfers between devices: 2.25 us -> 3.49 us
  Pallas kernels: 7.57 us -> 6.34 us
    all_to_all x1, waiting for transfers between devices: 0.44 us -> 1.85 us  [per_device(): lax.all_to_all(sums, both, 0, 0, axis_index_groups=[list(range(slabs * co...]
    pallas_call x3, Pallas kernels: 4.86 us -> 3.62 us  [the longest x1 1.54 us: per_device(): pl.pallas_call(inner_kernel, out_shape=(shape(2, 3, 2, cells, width), sha...]
  transfers between devices with their start and end apart: 5 -> 5, of which waited for: 2 -> 2; matrix products, arithmetic and copies ran while one was open for 0% -> 0% of each run, Pallas kernels for 15% -> 10%
where the time goes in v4:
time: 26.5 us; the launch traced here: 26.3 us
  starting transfers between devices  15.8 us (60%)
  Pallas kernels  6.34 us (24%)
  waiting for transfers between devices  3.49 us (13%)
  between operations  0.67 us (3%)
    all_to_all x1, starting transfers between devices, per_device(): lax.all_to_all(sums, both, 0, 0, axis_index_groups=[list(range(slabs * co...  7.2 us
    ppermute x1, starting transfers between devices, per_device(): same_in = lax.ppermute(same, both, up + down)  4.41 us
    ppermute x1, starting transfers between devices, per_device(): take = lax.ppermute(give, 'gy', [(0, 1), (1, 0)])  3 us
    all_to_all x1, waiting for transfers between devices, per_device(): lax.all_to_all(sums, both, 0, 0, axis_index_groups=[list(range(slabs * co...  1.85 us
    pallas_call x1, Pallas kernels, per_device(): pl.pallas_call(outer_kernel, out_shape=(shape(10, 2, cells, width), shape...  1.68 us
    ppermute x1, waiting for transfers between devices, per_device(): same_in = lax.ppermute(same, both, up + down)  1.63 us
    pallas_call x1, Pallas kernels, per_device(): pl.pallas_call(inner_kernel, out_shape=(shape(2, 3, 2, cells, width), sha...  1.54 us
    pallas_call x1, Pallas kernels, per_device(): pl.pallas_call(stress_kernel, out_shape=(shape(2, 18, cells, width), shap...  1.09 us
  transfers between devices with their start and end apart: 5, of which 2 were waited for; matrix products, arithmetic and copies ran while one was open for 0% of the time, Pallas kernels for 10%

profile of v4, /device:TPU:0, one launch (start us, length us, event | category | flops | bytes accessed | tf_op | source)
XLA Modules:
  0.0 26.3 jit_solution(12113576982810203942)
XLA Ops:
  0.6 1.0 %pack.1 = (f32[4,4,32,128]{3,2,1,0:T(8,128)S(1)}, f32[2,4,32,128]{3,2,1,0:T(8,128)S(1)}, f32[2,4,32,128]{3,2,1,0:T(8,128)S(1)}) custom-call(f32[3,128,128]{2,1,0:T(8,128)} %bitcast.4, f32[128,128]{1,0:T(8,128)} %bitcast.5), custom_call_target="tpu_custom_call" | custom-call | tf_op jit(solution)/shard_map/pack/pallas_call | solution.py:473
  1.6 0.5 %collective-permute-start = (f32[4,4,32,128]{3,2,1,0:T(8,128)S(1)}, f32[4,4,32,128]{3,2,1,0:T(8,128)S(1)}, u32[]{:S(2)}, u32[]{:S(2)}) collective-permute-start(f32[4,4,32,128]{3,2,1,0:T(8,128)S(1)} %get-tuple-element.20.own_ref), channel_id=1, source_target_pairs={{0,1},{1,0},{2,3},{3,2},{4,5},{5,4},{6,7},{7,6},{8,9},{9,8},{10,11... | collective-permute-start | bytes 786440 | tf_op jit(solution)/shard_map/ppermute | solution.py:489
  2.1 4.4 %collective-permute-start.1 = (f32[2,4,32,128]{3,2,1,0:T(8,128)S(1)}, f32[2,4,32,128]{3,2,1,0:T(8,128)S(1)}, u32[]{:S(2)}, u32[]{:S(2)}) collective-permute-start(f32[2,4,32,128]{3,2,1,0:T(8,128)S(1)} %get-tuple-element.28), channel_id=1, source_target_pairs={{0,2},{2,4},{4,6},{6,8},{8,10},{10,12},{12,14},{3,1},{5,3},{7,5},{... | collective-permute-start | bytes 393224 | tf_op jit(solution)/shard_map/ppermute | solution.py:491
  6.6 0.7 %collective-permute-start.2 = (f32[2,4,32,128]{3,2,1,0:T(8,128)S(1)}, f32[2,4,32,128]{3,2,1,0:T(8,128)S(1)}, u32[]{:S(2)}, u32[]{:S(2)}) collective-permute-start(f32[2,4,32,128]{3,2,1,0:T(8,128)S(1)} %get-tuple-element.29), channel_id=1, source_target_pairs={{1,2},{3,4},{5,6},{7,8},{9,10},{11,12},{13,14},{2,1},{4,3},{6,5},{... | collective-permute-start | bytes 393224 | tf_op jit(solution)/shard_map/ppermute | solution.py:490
  7.2 0.0 collective-permute-done.mate_ref
  7.2 1.5 %inner.1 = (f32[2,3,2,32,128]{4,3,2,1,0:T(8,128)S(1)}, f32[4,2,32,128]{3,2,1,0:T(8,128)S(1)}, f32[12,2,32,128]{3,2,1,0:T(8,128)S(1)}, f32[3,8,128]{2,1,0:T(8,128...) custom-call(f32[4,4,32,128]{3,2,1,0:T(8,128)S(1)} %get-tuple-element, ...), custom_call_target="tpu_custom_call" | custom-call | flops 20000000 | bytes 4000000 | tf_op jit(solution)/shard_map/inner/pallas_call | solution.py:493
  8.8 1.6 %collective-permute-done.1.same_ref = f32[2,4,32,128]{3,2,1,0:T(8,128)S(1)} collective-permute-done((f32[2,4,32,128]{3,2,1,0:T(8,128)S(1)}, f32[2,4,32,128]{3,2,1,0:T(8,128)S(1)}, u32[]{:S(2)}, u32[]{:S(2)}) %collective-permute-start.1) | collective-permute-done | bytes 131104 | tf_op jit(solution)/shard_map/ppermute | solution.py:491
  10.4 0.0 collective-permute-done.2.cross_ref
  10.4 1.7 %outer.1 = (f32[10,2,32,128]{3,2,1,0:T(8,128)S(1)}, f32[16,8,128]{2,1,0:T(8,128)}) custom-call(f32[2,3,2,32,128]{4,3,2,1,0:T(8,128)S(1)} %get-tuple-element.21.ends_ref, f32[4,2,32,128]{3,2,1,0:T(8,128)S(1)} %get-tuple-element.22.elem_ref, f32[12,2,32,128]{3,2,1,0:T(8,128)S(1)} %get-tuple-element.23.edge_part_ref, ...), custom_call_target="tpu_custom_call" | custom-call | flops 10000000 | bytes 3000000 | tf_op jit(solution)/shard_map/outer/pallas_call | solution.py:518
  12.1 3.0 %collective-permute-start.3 = (f32[10,2,32,128]{3,2,1,0:T(8,128)S(1)}, f32[10,2,32,128]{3,2,1,0:T(8,128)S(1)}, u32[]{:S(2)}, u32[]{:S(2)}) collective-permute-start(f32[10,2,32,128]{3,2,1,0:T(8,128)S(1)} %get-tuple-element.33.give_ref), channel_id=1, source_target_pairs={{0,1},{1,0},{2,3},{3,2},{4,5},{5,4},{6,7},{7,6},{8,9},{9,8},{10,11... | collective-permute-start | bytes 983048 | tf_op jit(solution)/shard_map/ppermute | solution.py:534
  15.1 7.2 %all-to-all-start = ((f32[16,8,128]{2,1,0:T(8,128)}), f32[16,8,128]{2,1,0:T(8,128)S(1)}, u32[]{:S(2)}, u32[]{:S(2)}) async-start(f32[16,8,128]{2,1,0:T(8,128)} %get-tuple-element.30), calls=%async_computation | async-start | bytes 131072 | tf_op jit(solution)/shard_map/all_to_all | solution.py:535
  22.3 0.0 collective-permute-done.3.take_ref
  22.3 1.1 %stress.1 = (f32[2,18,32,128]{3,2,1,0:T(8,128)S(1)}, f32[2,6,32,128]{3,2,1,0:T(8,128)S(1)}) custom-call(f32[2,3,2,32,128]{4,3,2,1,0:T(8,128)S(1)} %get-tuple-element.21.ends_ref, f32[4,2,32,128]{3,2,1,0:T(8,128)S(1)} %get-tuple-element.22.elem_ref, f32[2,9,2,32,128]{4,3,2,1,0:T(8,128)S(1)} %get-tuple-element.26.image_mode_ref, ...), custom_call_target="tpu_custom_call" | custom-call | flops 20000000 | bytes 4000000 | tf_op jit(solution)/shard_map/stress/pallas_call | solution.py:536
  23.4 1.9 %all-to-all-done.sums_ref = f32[16,8,128]{2,1,0:T(8,128)S(1)} async-done(((f32[16,8,128]{2,1,0:T(8,128)}), f32[16,8,128]{2,1,0:T(8,128)S(1)}, u32[]{:S(2)}, u32[]{:S(2)}) %all-to-all-start) | async-done | bytes 65568 | tf_op jit(solution)/shard_map/all_to_all | solution.py:535
  25.3 1.0 %combine.1 = (f32[3,128,128]{2,1,0:T(8,128)}, f32[6,128,128]{2,1,0:T(8,128)}) custom-call(f32[16,8,128]{2,1,0:T(8,128)S(1)} %all-to-all-done.sums_ref, f32[2,12,32,128]{3,2,1,0:T(8,128)S(1)} %get-tuple-element.31.early_ref, f32[2,18,32,128]{3,2,1,0:T(8,128)S(1)} %get-tuple-element.34.late_ref, f32[2,6,32,128]{3,2,1,0:T(8,128)S(1)} %get-tuple-element.35.middle_ref), custom_call_target="tpu_custom_call" | custom-call | tf_op jit(solution)/shard_map/combine/pallas_call | solution.py:552
Async XLA Ops:
  1.6 5.6 %collective-permute-start = (f32[4,4,32,128]{3,2,1,0:T(8,128)S(1)}, f32[4,4,32,128]{3,2,1,0:T(8,128)S(1)}, u32[]{:S(2)}, u32[]{:S(2)}) collective-permute-start(f32[4,4,32,128]{3,2,1,0:T(8,128)S(1)} %get-tuple-element.20.own_ref), channel_id=1, source_target_pairs={{0,1},{1,0},{2,3},{3,2},{4,5},{5,4},{6,7},{7,6},{8,9},{9,8},{10,11... | collective-permute-start | bytes 786440 | tf_op jit(solution)/shard_map/ppermute | solution.py:489
  2.1 8.3 %collective-permute-start.1 = (f32[2,4,32,128]{3,2,1,0:T(8,128)S(1)}, f32[2,4,32,128]{3,2,1,0:T(8,128)S(1)}, u32[]{:S(2)}, u32[]{:S(2)}) collective-permute-start(f32[2,4,32,128]{3,2,1,0:T(8,128)S(1)} %get-tuple-element.28), channel_id=1, source_target_pairs={{0,2},{2,4},{4,6},{6,8},{8,10},{10,12},{12,14},{3,1},{5,3},{7,5},{... | collective-permute-start | bytes 393224 | tf_op jit(solution)/shard_map/ppermute | solution.py:491
  6.6 3.9 %collective-permute-start.2 = (f32[2,4,32,128]{3,2,1,0:T(8,128)S(1)}, f32[2,4,32,128]{3,2,1,0:T(8,128)S(1)}, u32[]{:S(2)}, u32[]{:S(2)}) collective-permute-start(f32[2,4,32,128]{3,2,1,0:T(8,128)S(1)} %get-tuple-element.29), channel_id=1, source_target_pairs={{1,2},{3,4},{5,6},{7,8},{9,10},{11,12},{13,14},{2,1},{4,3},{6,5},{... | collective-permute-start | bytes 393224 | tf_op jit(solution)/shard_map/ppermute | solution.py:490
  12.1 10.2 %collective-permute-start.3 = (f32[10,2,32,128]{3,2,1,0:T(8,128)S(1)}, f32[10,2,32,128]{3,2,1,0:T(8,128)S(1)}, u32[]{:S(2)}, u32[]{:S(2)}) collective-permute-start(f32[10,2,32,128]{3,2,1,0:T(8,128)S(1)} %get-tuple-element.33.give_ref), channel_id=1, source_target_pairs={{0,1},{1,0},{2,3},{3,2},{4,5},{5,4},{6,7},{7,6},{8,9},{9,8},{10,11... | collective-permute-start | bytes 983048 | tf_op jit(solution)/shard_map/ppermute | solution.py:534
  15.1 10.1 %all-to-all-start = ((f32[16,8,128]{2,1,0:T(8,128)}), f32[16,8,128]{2,1,0:T(8,128)S(1)}, u32[]{:S(2)}, u32[]{:S(2)}) async-start(f32[16,8,128]{2,1,0:T(8,128)} %get-tuple-element.30), calls=%async_computation | async-start | bytes 131072 | tf_op jit(solution)/shard_map/all_to_all | solution.py:535

commit v5 on v4

--- a/solution.py
+++ b/solution.py
@@ -219,7 +219,7 @@
 
 
 def inner_kernel(
-    own_ref, mate_ref, ends_ref, elem_ref, edge_part_ref, sums_ref, edge_mode_ref, image_mode_ref, image_last_ref, side_ref, early_ref,
+    own_ref, mate_ref, _arrived, ends_ref, elem_ref, edge_part_ref, sums_ref, edge_mode_ref, image_mode_ref, image_last_ref, side_ref, early_ref,
     node_ref, mode_ref, part_ref, stress_part_ref,
 ):
     core = lax.axis_index("gy")
@@ -503,7 +503,7 @@
             shape(2, 6, 2, cells, width),
             shape(2, 12, cells, width),
         ),
-        in_specs=[VMEM] * 2,
+        in_specs=[VMEM] * 2 + [pl.BlockSpec(memory_space=pl.ANY)],
         out_specs=[VMEM] * 9,
         scratch_shapes=[
             scratch(4, 3, 2, 8 + cells, width),
@@ -514,7 +514,7 @@
         compiler_params=LIMIT,
         cost_estimate=cost(20_000_000, 4_000_000),
         name="inner",
-    )(own, mate)
+    )(own, mate, cross_in)
     give, sums = pl.pallas_call(
         outer_kernel,
         out_shape=(shape(10, 2, cells, width), shape(slabs * cores, 8, width)),

time: 26.5 us -> 26.5 us (level)
  starting transfers between devices: 15.8 us -> 14.6 us
  waiting for transfers between devices: 3.49 us -> 4.64 us
    ppermute x1, starting transfers between devices: 3 us -> 0.01 us  [per_device(): take = lax.ppermute(give, 'gy', [(0, 1), (1, 0)])]
    ppermute x1, starting transfers between devices: 4.41 us -> 5.67 us  [per_device(): same_in = lax.ppermute(same, both, up + down)]
    ppermute x1, waiting for transfers between devices: 1.63 us -> 2.79 us  [per_device(): same_in = lax.ppermute(same, both, up + down)]
    all_to_all x1, starting transfers between devices: 7.2 us -> 7.76 us  [per_device(): lax.all_to_all(sums, both, 0, 0, axis_index_groups=[list(range(slabs * co...]
where the time goes in v5:
time: 26.5 us; the launch traced here: 26.3 us
  starting transfers between devices  14.6 us (55%)
  Pallas kernels  6.35 us (24%)
  waiting for transfers between devices  4.64 us (18%)
  between operations  0.68 us (3%)
    all_to_all x1, starting transfers between devices, per_device(): lax.all_to_all(sums, both, 0, 0, axis_index_groups=[list(range(slabs * co...  7.76 us
    ppermute x1, starting transfers between devices, per_device(): same_in = lax.ppermute(same, both, up + down)  5.67 us
    ppermute x1, waiting for transfers between devices, per_device(): same_in = lax.ppermute(same, both, up + down)  2.79 us
    all_to_all x1, waiting for transfers between devices, per_device(): lax.all_to_all(sums, both, 0, 0, axis_index_groups=[list(range(slabs * co...  1.85 us
    pallas_call x1, Pallas kernels, per_device(): pl.pallas_call(outer_kernel, out_shape=(shape(10, 2, cells, width), shape...  1.68 us
    pallas_call x1, Pallas kernels, per_device(): pl.pallas_call(inner_kernel, out_shape=(shape(2, 3, 2, cells, width), sha...  1.55 us
    pallas_call x1, Pallas kernels, per_device(): pl.pallas_call(stress_kernel, out_shape=(shape(2, 18, cells, width), shap...  1.09 us
    pallas_call x1, Pallas kernels, per_device(): pl.pallas_call(combine_kernel, out_shape=(shape(3, cells * 4, width), sha...  1.04 us
  transfers between devices with their start and end apart: 5, of which 2 were waited for; matrix products, arithmetic and copies ran while one was open for 0% of the time, Pallas kernels for 10%

profile of v5, /device:TPU:0, one launch (start us, length us, event | category | flops | bytes accessed | tf_op | source)
XLA Modules:
  0.0 26.3 jit_solution(7239006493881445945)
XLA Ops:
  0.6 1.0 %pack.1 = (f32[4,4,32,128]{3,2,1,0:T(8,128)S(1)}, f32[2,4,32,128]{3,2,1,0:T(8,128)S(1)}, f32[2,4,32,128]{3,2,1,0:T(8,128)S(1)}) custom-call(f32[3,128,128]{2,1,0:T(8,128)} %bitcast.4, f32[128,128]{1,0:T(8,128)} %bitcast.5), custom_call_target="tpu_custom_call" | custom-call | tf_op jit(solution)/shard_map/pack/pallas_call | solution.py:473
  1.6 0.5 %collective-permute-start = (f32[4,4,32,128]{3,2,1,0:T(8,128)S(1)}, f32[4,4,32,128]{3,2,1,0:T(8,128)S(1)}, u32[]{:S(2)}, u32[]{:S(2)}) collective-permute-start(f32[4,4,32,128]{3,2,1,0:T(8,128)S(1)} %get-tuple-element.20.own_ref), channel_id=1, source_target_pairs={{0,1},{1,0},{2,3},{3,2},{4,5},{5,4},{6,7},{7,6},{8,9},{9,8},{10,11... | collective-permute-start | bytes 786440 | tf_op jit(solution)/shard_map/ppermute | solution.py:489
  2.1 0.7 %collective-permute-start.1 = (f32[2,4,32,128]{3,2,1,0:T(8,128)S(1)}, f32[2,4,32,128]{3,2,1,0:T(8,128)S(1)}, u32[]{:S(2)}, u32[]{:S(2)}) collective-permute-start(f32[2,4,32,128]{3,2,1,0:T(8,128)S(1)} %get-tuple-element.21), channel_id=1, source_target_pairs={{1,2},{3,4},{5,6},{7,8},{9,10},{11,12},{13,14},{2,1},{4,3},{6,5},{... | collective-permute-start | bytes 393224 | tf_op jit(solution)/shard_map/ppermute | solution.py:490
  2.8 5.7 %collective-permute-start.2 = (f32[2,4,32,128]{3,2,1,0:T(8,128)S(1)}, f32[2,4,32,128]{3,2,1,0:T(8,128)S(1)}, u32[]{:S(2)}, u32[]{:S(2)}) collective-permute-start(f32[2,4,32,128]{3,2,1,0:T(8,128)S(1)} %get-tuple-element.29), channel_id=1, source_target_pairs={{0,2},{2,4},{4,6},{6,8},{8,10},{10,12},{12,14},{3,1},{5,3},{7,5},{... | collective-permute-start | bytes 393224 | tf_op jit(solution)/shard_map/ppermute | solution.py:491
  8.5 0.0 collective-permute-done.1._arrived.cross_ref
  8.5 0.0 collective-permute-done.mate_ref
  8.5 1.5 %inner.1 = (f32[2,3,2,32,128]{4,3,2,1,0:T(8,128)S(1)}, f32[4,2,32,128]{3,2,1,0:T(8,128)S(1)}, f32[12,2,32,128]{3,2,1,0:T(8,128)S(1)}, f32[3,8,128]{2,1,0:T(8,128...) custom-call(f32[4,4,32,128]{3,2,1,0:T(8,128)S(1)} %get-tuple-element, ...), custom_call_target="tpu_custom_call" | custom-call | flops 20000000 | bytes 4000000 | tf_op jit(solution)/shard_map/inner/pallas_call | solution.py:493
  10.1 2.8 %collective-permute-done.2.same_ref = f32[2,4,32,128]{3,2,1,0:T(8,128)S(1)} collective-permute-done((f32[2,4,32,128]{3,2,1,0:T(8,128)S(1)}, f32[2,4,32,128]{3,2,1,0:T(8,128)S(1)}, u32[]{:S(2)}, u32[]{:S(2)}) %collective-permute-start.2) | collective-permute-done | bytes 131104 | tf_op jit(solution)/shard_map/ppermute | solution.py:491
  12.9 1.7 %outer.1 = (f32[10,2,32,128]{3,2,1,0:T(8,128)S(1)}, f32[16,8,128]{2,1,0:T(8,128)}) custom-call(f32[2,3,2,32,128]{4,3,2,1,0:T(8,128)S(1)} %get-tuple-element.22.ends_ref, f32[4,2,32,128]{3,2,1,0:T(8,128)S(1)} %get-tuple-element.23.elem_ref, f32[12,2,32,128]{3,2,1,0:T(8,128)S(1)} %get-tuple-element.24.edge_part_ref, ...), custom_call_target="tpu_custom_call" | custom-call | flops 10000000 | bytes 3000000 | tf_op jit(solution)/shard_map/outer/pallas_call | solution.py:518
  14.5 0.0 collective-permute-start.3
  14.5 7.8 %all-to-all-start = ((f32[16,8,128]{2,1,0:T(8,128)}), f32[16,8,128]{2,1,0:T(8,128)S(1)}, u32[]{:S(2)}, u32[]{:S(2)}) async-start(f32[16,8,128]{2,1,0:T(8,128)} %get-tuple-element.30), calls=%async_computation | async-start | bytes 131072 | tf_op jit(solution)/shard_map/all_to_all | solution.py:535
  22.3 0.0 collective-permute-done.3.take_ref
  22.3 1.1 %stress.1 = (f32[2,18,32,128]{3,2,1,0:T(8,128)S(1)}, f32[2,6,32,128]{3,2,1,0:T(8,128)S(1)}) custom-call(f32[2,3,2,32,128]{4,3,2,1,0:T(8,128)S(1)} %get-tuple-element.22.ends_ref, f32[4,2,32,128]{3,2,1,0:T(8,128)S(1)} %get-tuple-element.23.elem_ref, f32[2,9,2,32,128]{4,3,2,1,0:T(8,128)S(1)} %get-tuple-element.27.image_mode_ref, ...), custom_call_target="tpu_custom_call" | custom-call | flops 20000000 | bytes 4000000 | tf_op jit(solution)/shard_map/stress/pallas_call | solution.py:536
  23.4 1.8 %all-to-all-done.sums_ref = f32[16,8,128]{2,1,0:T(8,128)S(1)} async-done(((f32[16,8,128]{2,1,0:T(8,128)}), f32[16,8,128]{2,1,0:T(8,128)S(1)}, u32[]{:S(2)}, u32[]{:S(2)}) %all-to-all-start) | async-done | bytes 65568 | tf_op jit(solution)/shard_map/all_to_all | solution.py:535
  25.2 1.0 %combine.1 = (f32[3,128,128]{2,1,0:T(8,128)}, f32[6,128,128]{2,1,0:T(8,128)}) custom-call(f32[16,8,128]{2,1,0:T(8,128)S(1)} %all-to-all-done.sums_ref, f32[2,12,32,128]{3,2,1,0:T(8,128)S(1)} %get-tuple-element.31.early_ref, f32[2,18,32,128]{3,2,1,0:T(8,128)S(1)} %get-tuple-element.34.late_ref, f32[2,6,32,128]{3,2,1,0:T(8,128)S(1)} %get-tuple-element.35.middle_ref), custom_call_target="tpu_custom_call" | custom-call | tf_op jit(solution)/shard_map/combine/pallas_call | solution.py:552
Async XLA Ops:
  1.6 6.9 %collective-permute-start = (f32[4,4,32,128]{3,2,1,0:T(8,128)S(1)}, f32[4,4,32,128]{3,2,1,0:T(8,128)S(1)}, u32[]{:S(2)}, u32[]{:S(2)}) collective-permute-start(f32[4,4,32,128]{3,2,1,0:T(8,128)S(1)} %get-tuple-element.20.own_ref), channel_id=1, source_target_pairs={{0,1},{1,0},{2,3},{3,2},{4,5},{5,4},{6,7},{7,6},{8,9},{9,8},{10,11... | collective-permute-start | bytes 786440 | tf_op jit(solution)/shard_map/ppermute | solution.py:489
  2.1 6.3 %collective-permute-start.1 = (f32[2,4,32,128]{3,2,1,0:T(8,128)S(1)}, f32[2,4,32,128]{3,2,1,0:T(8,128)S(1)}, u32[]{:S(2)}, u32[]{:S(2)}) collective-permute-start(f32[2,4,32,128]{3,2,1,0:T(8,128)S(1)} %get-tuple-element.21), channel_id=1, source_target_pairs={{1,2},{3,4},{5,6},{7,8},{9,10},{11,12},{13,14},{2,1},{4,3},{6,5},{... | collective-permute-start | bytes 393224 | tf_op jit(solution)/shard_map/ppermute | solution.py:490
  2.8 10.0 %collective-permute-start.2 = (f32[2,4,32,128]{3,2,1,0:T(8,128)S(1)}, f32[2,4,32,128]{3,2,1,0:T(8,128)S(1)}, u32[]{:S(2)}, u32[]{:S(2)}) collective-permute-start(f32[2,4,32,128]{3,2,1,0:T(8,128)S(1)} %get-tuple-element.29), channel_id=1, source_target_pairs={{0,2},{2,4},{4,6},{6,8},{8,10},{10,12},{12,14},{3,1},{5,3},{7,5},{... | collective-permute-start | bytes 393224 | tf_op jit(solution)/shard_map/ppermute | solution.py:491
  14.5 7.8 %collective-permute-start.3 = (f32[10,2,32,128]{3,2,1,0:T(8,128)S(1)}, f32[10,2,32,128]{3,2,1,0:T(8,128)S(1)}, u32[]{:S(2)}, u32[]{:S(2)}) collective-permute-start(f32[10,2,32,128]{3,2,1,0:T(8,128)S(1)} %get-tuple-element.33.give_ref), channel_id=1, source_target_pairs={{0,1},{1,0},{2,3},{3,2},{4,5},{5,4},{6,7},{7,6},{8,9},{9,8},{10,11... | collective-permute-start | bytes 983048 | tf_op jit(solution)/shard_map/ppermute | solution.py:534
  14.5 10.7 %all-to-all-start = ((f32[16,8,128]{2,1,0:T(8,128)}), f32[16,8,128]{2,1,0:T(8,128)S(1)}, u32[]{:S(2)}, u32[]{:S(2)}) async-start(f32[16,8,128]{2,1,0:T(8,128)} %get-tuple-element.30), calls=%async_computation | async-start | bytes 131072 | tf_op jit(solution)/shard_map/all_to_all | solution.py:535

commit v6 on v5

--- a/solution.py
+++ b/solution.py
@@ -376,10 +376,12 @@
         return total
 
     energy = lax.fori_loop(0, 2 * tiles, energy_of, zeros(8, width), unroll=True)
-    line = lax.broadcasted_iota(jnp.int32, (8, width), 0)
-    packed = zeros(8, width)
+    packed = jnp.zeros((8, width), jnp.float32)
     for k, value in enumerate((norm, cross, square, energy)):
-        packed = jnp.where(line == k, jnp.sum(value, axis=0, keepdims=True), packed)
+        value = value + pltpu.roll(value, width // 2, 1)
+        value = value + pltpu.roll(value, width // 4, 1)
+        packed = jnp.where(lanes((8, width)) // (width // 4) == k, value, packed)
+    packed = jnp.sum(packed, axis=0, keepdims=True)
     sums_ref[...] = jnp.broadcast_to(packed[None], sums_ref.shape)
 
 
@@ -436,8 +438,9 @@
 
 
 def combine_kernel(sums_ref, early_ref, late_ref, middle_ref, field_ref, stress_ref):
-    total = jnp.sum(jnp.sum(sums_ref[...], axis=0), axis=1, keepdims=True)
-    norm, cross, square, energy = (total[k : k + 1, :] for k in range(4))
+    total = jnp.sum(sums_ref[...], axis=0)
+    quarter = lanes(total.shape) // (total.shape[1] // 4)
+    norm, cross, square, energy = (jnp.sum(jnp.where(quarter == k, total, 0.0), axis=1, keepdims=True) for k in range(4))
     first = norm / cross
     norm_next = norm - 2.0 * first * cross + first * first * square
     ratio = norm_next / norm
@@ -517,7 +520,7 @@
     )(own, mate, cross_in)
     give, sums = pl.pallas_call(
         outer_kernel,
-        out_shape=(shape(10, 2, cells, width), shape(slabs * cores, 8, width)),
+        out_shape=(shape(10, 2, cells, width), shape(slabs * cores, 1, width)),
         in_specs=[VMEM] * 9,
         out_specs=[VMEM] * 2,
         scratch_shapes=[

time: 26.5 us -> 25.9 us (0.977)
  waiting for transfers between devices: 4.64 us -> 3.98 us
    all_to_all x1, waiting for transfers between devices: 1.85 us -> 1.18 us  [per_device(): lax.all_to_all(sums, both, 0, 0, axis_index_groups=[list(range(slabs * co...]
where the time goes in v6:
time: 25.9 us; the launch traced here: 25.6 us
  starting transfers between devices  14.6 us (56%)
  Pallas kernels  6.41 us (25%)
  waiting for transfers between devices  3.98 us (15%)
  between operations  0.68 us (3%)
    all_to_all x1, starting transfers between devices, per_device(): lax.all_to_all(sums, both, 0, 0, axis_index_groups=[list(range(slabs * co...  7.72 us
    ppermute x1, starting transfers between devices, per_device(): same_in = lax.ppermute(same, both, up + down)  5.67 us
    ppermute x1, waiting for transfers between devices, per_device(): same_in = lax.ppermute(same, both, up + down)  2.79 us
    pallas_call x1, Pallas kernels, per_device(): pl.pallas_call(outer_kernel, out_shape=(shape(10, 2, cells, width), shape...  1.78 us
    pallas_call x1, Pallas kernels, per_device(): pl.pallas_call(inner_kernel, out_shape=(shape(2, 3, 2, cells, width), sha...  1.55 us
    all_to_all x1, waiting for transfers between devices, per_device(): lax.all_to_all(sums, both, 0, 0, axis_index_groups=[list(range(slabs * co...  1.18 us
    pallas_call x1, Pallas kernels, per_device(): pl.pallas_call(stress_kernel, out_shape=(shape(2, 18, cells, width), shap...  1.09 us
    pallas_call x1, Pallas kernels, per_device(): pl.pallas_call(combine_kernel, out_shape=(shape(3, cells * 4, width), sha...  1.01 us
  transfers between devices with their start and end apart: 5, of which 2 were waited for; matrix products, arithmetic and copies ran while one was open for 0% of the time, Pallas kernels for 10%

profile of v6, /device:TPU:0, one launch (start us, length us, event | category | flops | bytes accessed | tf_op | source)
XLA Modules:
  0.0 25.6 jit_solution(15724250042416272808)
XLA Ops:
  0.6 1.0 %pack.1 = (f32[4,4,32,128]{3,2,1,0:T(8,128)S(1)}, f32[2,4,32,128]{3,2,1,0:T(8,128)S(1)}, f32[2,4,32,128]{3,2,1,0:T(8,128)S(1)}) custom-call(f32[3,128,128]{2,1,0:T(8,128)} %bitcast.4, f32[128,128]{1,0:T(8,128)} %bitcast.5), custom_call_target="tpu_custom_call" | custom-call | tf_op jit(solution)/shard_map/pack/pallas_call | solution.py:476
  1.6 0.5 %collective-permute-start = (f32[4,4,32,128]{3,2,1,0:T(8,128)S(1)}, f32[4,4,32,128]{3,2,1,0:T(8,128)S(1)}, u32[]{:S(2)}, u32[]{:S(2)}) collective-permute-start(f32[4,4,32,128]{3,2,1,0:T(8,128)S(1)} %get-tuple-element.20.own_ref), channel_id=1, source_target_pairs={{0,1},{1,0},{2,3},{3,2},{4,5},{5,4},{6,7},{7,6},{8,9},{9,8},{10,11... | collective-permute-start | bytes 786440 | tf_op jit(solution)/shard_map/ppermute | solution.py:492
  2.1 0.7 %collective-permute-start.1 = (f32[2,4,32,128]{3,2,1,0:T(8,128)S(1)}, f32[2,4,32,128]{3,2,1,0:T(8,128)S(1)}, u32[]{:S(2)}, u32[]{:S(2)}) collective-permute-start(f32[2,4,32,128]{3,2,1,0:T(8,128)S(1)} %get-tuple-element.21), channel_id=1, source_target_pairs={{1,2},{3,4},{5,6},{7,8},{9,10},{11,12},{13,14},{2,1},{4,3},{6,5},{... | collective-permute-start | bytes 393224 | tf_op jit(solution)/shard_map/ppermute | solution.py:493
  2.8 5.7 %collective-permute-start.2 = (f32[2,4,32,128]{3,2,1,0:T(8,128)S(1)}, f32[2,4,32,128]{3,2,1,0:T(8,128)S(1)}, u32[]{:S(2)}, u32[]{:S(2)}) collective-permute-start(f32[2,4,32,128]{3,2,1,0:T(8,128)S(1)} %get-tuple-element.29), channel_id=1, source_target_pairs={{0,2},{2,4},{4,6},{6,8},{8,10},{10,12},{12,14},{3,1},{5,3},{7,5},{... | collective-permute-start | bytes 393224 | tf_op jit(solution)/shard_map/ppermute | solution.py:494
  8.5 0.0 collective-permute-done.1._arrived.cross_ref
  8.5 0.0 collective-permute-done.mate_ref
  8.5 1.5 %inner.1 = (f32[2,3,2,32,128]{4,3,2,1,0:T(8,128)S(1)}, f32[4,2,32,128]{3,2,1,0:T(8,128)S(1)}, f32[12,2,32,128]{3,2,1,0:T(8,128)S(1)}, f32[3,8,128]{2,1,0:T(8,128...) custom-call(f32[4,4,32,128]{3,2,1,0:T(8,128)S(1)} %get-tuple-element, ...), custom_call_target="tpu_custom_call" | custom-call | flops 20000000 | bytes 4000000 | tf_op jit(solution)/shard_map/inner/pallas_call | solution.py:496
  10.1 2.8 %collective-permute-done.2.same_ref = f32[2,4,32,128]{3,2,1,0:T(8,128)S(1)} collective-permute-done((f32[2,4,32,128]{3,2,1,0:T(8,128)S(1)}, f32[2,4,32,128]{3,2,1,0:T(8,128)S(1)}, u32[]{:S(2)}, u32[]{:S(2)}) %collective-permute-start.2) | collective-permute-done | bytes 131104 | tf_op jit(solution)/shard_map/ppermute | solution.py:494
  12.9 1.8 %outer.1 = (f32[10,2,32,128]{3,2,1,0:T(8,128)S(1)}, f32[16,1,128]{2,1,0:T(1,128)}) custom-call(f32[2,3,2,32,128]{4,3,2,1,0:T(8,128)S(1)} %get-tuple-element.22.ends_ref, f32[4,2,32,128]{3,2,1,0:T(8,128)S(1)} %get-tuple-element.23.elem_ref, f32[12,2,32,128]{3,2,1,0:T(8,128)S(1)} %get-tuple-element.24.edge_part_ref, ...), custom_call_target="tpu_custom_call" | custom-call | flops 10000000 | bytes 3000000 | tf_op jit(solution)/shard_map/outer/pallas_call | solution.py:521
  14.6 0.0 collective-permute-start.3
  14.6 7.7 %all-to-all-start = ((f32[16,1,128]{2,1,0:T(1,128)}), f32[16,1,128]{2,1,0:T(1,128)S(1)}, u32[]{:S(2)}, u32[]{:S(2)}) async-start(f32[16,1,128]{2,1,0:T(1,128)} %get-tuple-element.30), calls=%async_computation | async-start | bytes 16384 | tf_op jit(solution)/shard_map/all_to_all | solution.py:538
  22.4 0.0 collective-permute-done.3.take_ref
  22.4 1.1 %stress.1 = (f32[2,18,32,128]{3,2,1,0:T(8,128)S(1)}, f32[2,6,32,128]{3,2,1,0:T(8,128)S(1)}) custom-call(f32[2,3,2,32,128]{4,3,2,1,0:T(8,128)S(1)} %get-tuple-element.22.ends_ref, f32[4,2,32,128]{3,2,1,0:T(8,128)S(1)} %get-tuple-element.23.elem_ref, f32[2,9,2,32,128]{4,3,2,1,0:T(8,128)S(1)} %get-tuple-element.27.image_mode_ref, ...), custom_call_target="tpu_custom_call" | custom-call | flops 20000000 | bytes 4000000 | tf_op jit(solution)/shard_map/stress/pallas_call | solution.py:539
  23.5 1.2 %all-to-all-done.sums_ref = f32[16,1,128]{2,1,0:T(1,128)S(1)} async-done(((f32[16,1,128]{2,1,0:T(1,128)}), f32[16,1,128]{2,1,0:T(1,128)S(1)}, u32[]{:S(2)}, u32[]{:S(2)}) %all-to-all-start) | async-done | bytes 8224 | tf_op jit(solution)/shard_map/all_to_all | solution.py:538
  24.6 1.0 %combine.1 = (f32[3,128,128]{2,1,0:T(8,128)}, f32[6,128,128]{2,1,0:T(8,128)}) custom-call(f32[16,1,128]{2,1,0:T(1,128)S(1)} %all-to-all-done.sums_ref, f32[2,12,32,128]{3,2,1,0:T(8,128)S(1)} %get-tuple-element.31.early_ref, f32[2,18,32,128]{3,2,1,0:T(8,128)S(1)} %get-tuple-element.34.late_ref, f32[2,6,32,128]{3,2,1,0:T(8,128)S(1)} %get-tuple-element.35.middle_ref), custom_call_target="tpu_custom_call" | custom-call | tf_op jit(solution)/shard_map/combine/pallas_call | solution.py:555
Async XLA Ops:
  1.6 6.9 %collective-permute-start = (f32[4,4,32,128]{3,2,1,0:T(8,128)S(1)}, f32[4,4,32,128]{3,2,1,0:T(8,128)S(1)}, u32[]{:S(2)}, u32[]{:S(2)}) collective-permute-start(f32[4,4,32,128]{3,2,1,0:T(8,128)S(1)} %get-tuple-element.20.own_ref), channel_id=1, source_target_pairs={{0,1},{1,0},{2,3},{3,2},{4,5},{5,4},{6,7},{7,6},{8,9},{9,8},{10,11... | collective-permute-start | bytes 786440 | tf_op jit(solution)/shard_map/ppermute | solution.py:492
  2.1 6.3 %collective-permute-start.1 = (f32[2,4,32,128]{3,2,1,0:T(8,128)S(1)}, f32[2,4,32,128]{3,2,1,0:T(8,128)S(1)}, u32[]{:S(2)}, u32[]{:S(2)}) collective-permute-start(f32[2,4,32,128]{3,2,1,0:T(8,128)S(1)} %get-tuple-element.21), channel_id=1, source_target_pairs={{1,2},{3,4},{5,6},{7,8},{9,10},{11,12},{13,14},{2,1},{4,3},{6,5},{... | collective-permute-start | bytes 393224 | tf_op jit(solution)/shard_map/ppermute | solution.py:493
  2.8 10.0 %collective-permute-start.2 = (f32[2,4,32,128]{3,2,1,0:T(8,128)S(1)}, f32[2,4,32,128]{3,2,1,0:T(8,128)S(1)}, u32[]{:S(2)}, u32[]{:S(2)}) collective-permute-start(f32[2,4,32,128]{3,2,1,0:T(8,128)S(1)} %get-tuple-element.29), channel_id=1, source_target_pairs={{0,2},{2,4},{4,6},{6,8},{8,10},{10,12},{12,14},{3,1},{5,3},{7,5},{... | collective-permute-start | bytes 393224 | tf_op jit(solution)/shard_map/ppermute | solution.py:494
  14.6 7.7 %collective-permute-start.3 = (f32[10,2,32,128]{3,2,1,0:T(8,128)S(1)}, f32[10,2,32,128]{3,2,1,0:T(8,128)S(1)}, u32[]{:S(2)}, u32[]{:S(2)}) collective-permute-start(f32[10,2,32,128]{3,2,1,0:T(8,128)S(1)} %get-tuple-element.33.give_ref), channel_id=1, source_target_pairs={{0,1},{1,0},{2,3},{3,2},{4,5},{5,4},{6,7},{7,6},{8,9},{9,8},{10,11... | collective-permute-start | bytes 983048 | tf_op jit(solution)/shard_map/ppermute | solution.py:537
  14.6 10.0 %all-to-all-start = ((f32[16,1,128]{2,1,0:T(1,128)}), f32[16,1,128]{2,1,0:T(1,128)S(1)}, u32[]{:S(2)}, u32[]{:S(2)}) async-start(f32[16,1,128]{2,1,0:T(1,128)} %get-tuple-element.30), calls=%async_computation | async-start | bytes 16384 | tf_op jit(solution)/shard_map/all_to_all | solution.py:538

commit v7 on v6

--- a/solution.py
+++ b/solution.py
@@ -38,20 +38,17 @@
 def pack_kernel(force_hbm, modulus_hbm, own_ref, same_ref, cross_ref, force_ref, modulus_ref, sem):
     core = lax.axis_index("gy")
     cells = own_ref.shape[2]
-    copies = [
-        pltpu.make_async_copy(force_hbm, force_ref, sem.at[0]),
-        pltpu.make_async_copy(modulus_hbm, modulus_ref, sem.at[1]),
-    ]
+    copies = [pltpu.make_async_copy(force_hbm.at[field], force_ref.at[field], sem.at[field]) for field in range(3)]
+    copies.append(pltpu.make_async_copy(modulus_hbm, modulus_ref, sem.at[3]))
     for copy in copies:
         copy.start()
-    for copy in copies:
-        copy.wait()
 
     def plane(field, x):
         rows = pl.ds(x, cells, stride=4)
         return force_ref[field, rows, :] if field < 3 else modulus_ref[rows, :]
 
     for field in range(4):
+        copies[field].wait()
         for x in range(4):
             own_ref[x, field] = plane(field, x)
         for i in range(2):
@@ -478,7 +475,7 @@
         out_shape=(shape(4, 4, cells, width), shape(2, 4, cells, width), shape(2, 4, cells, width)),
         in_specs=[pl.BlockSpec(memory_space=pl.ANY)] * 2,
         out_specs=[VMEM] * 3,
-        scratch_shapes=[scratch(3, cells * 4, width), scratch(cells * 4, width), pltpu.SemaphoreType.DMA((2,))],
+        scratch_shapes=[scratch(3, cells * 4, width), scratch(cells * 4, width), pltpu.SemaphoreType.DMA((4,))],
         compiler_params=LIMIT,
         name="pack",
     )(

time: 25.9 us -> 25.9 us (level)
  no operation moved by 1% of the time
where the time goes in v7:
time: 25.9 us; the launch traced here: 25.6 us
  starting transfers between devices  14.6 us (56%)
  Pallas kernels  6.41 us (25%)
  waiting for transfers between devices  3.98 us (15%)
  between operations  0.68 us (3%)
    all_to_all x1, starting transfers between devices, per_device(): lax.all_to_all(sums, both, 0, 0, axis_index_groups=[list(range(slabs * co...  7.72 us
    ppermute x1, starting transfers between devices, per_device(): same_in = lax.ppermute(same, both, up + down)  5.67 us
    ppermute x1, waiting for transfers between devices, per_device(): same_in = lax.ppermute(same, both, up + down)  2.79 us
    pallas_call x1, Pallas kernels, per_device(): pl.pallas_call(outer_kernel, out_shape=(shape(10, 2, cells, width), shape...  1.78 us
    pallas_call x1, Pallas kernels, per_device(): pl.pallas_call(inner_kernel, out_shape=(shape(2, 3, 2, cells, width), sha...  1.55 us
    all_to_all x1, waiting for transfers between devices, per_device(): lax.all_to_all(sums, both, 0, 0, axis_index_groups=[list(range(slabs * co...  1.18 us
    pallas_call x1, Pallas kernels, per_device(): pl.pallas_call(stress_kernel, out_shape=(shape(2, 18, cells, width), shap...  1.09 us
    pallas_call x1, Pallas kernels, per_device(): pl.pallas_call(combine_kernel, out_shape=(shape(3, cells * 4, width), sha...  1.01 us
  transfers between devices with their start and end apart: 5, of which 2 were waited for; matrix products, arithmetic and copies ran while one was open for 0% of the time, Pallas kernels for 10%

profile of v7, /device:TPU:0, one launch (start us, length us, event | category | flops | bytes accessed | tf_op | source)
XLA Modules:
  0.0 25.6 jit_solution(12176275841736914801)
XLA Ops:
  0.6 1.0 %pack.1 = (f32[4,4,32,128]{3,2,1,0:T(8,128)S(1)}, f32[2,4,32,128]{3,2,1,0:T(8,128)S(1)}, f32[2,4,32,128]{3,2,1,0:T(8,128)S(1)}) custom-call(f32[3,128,128]{2,1,0:T(8,128)} %bitcast.4, f32[128,128]{1,0:T(8,128)} %bitcast.5), custom_call_target="tpu_custom_call" | custom-call | tf_op jit(solution)/shard_map/pack/pallas_call | solution.py:473
  1.6 0.5 %collective-permute-start = (f32[4,4,32,128]{3,2,1,0:T(8,128)S(1)}, f32[4,4,32,128]{3,2,1,0:T(8,128)S(1)}, u32[]{:S(2)}, u32[]{:S(2)}) collective-permute-start(f32[4,4,32,128]{3,2,1,0:T(8,128)S(1)} %get-tuple-element.20.own_ref), channel_id=1, source_target_pairs={{0,1},{1,0},{2,3},{3,2},{4,5},{5,4},{6,7},{7,6},{8,9},{9,8},{10,11... | collective-permute-start | bytes 786440 | tf_op jit(solution)/shard_map/ppermute | solution.py:489
  2.1 0.7 %collective-permute-start.1 = (f32[2,4,32,128]{3,2,1,0:T(8,128)S(1)}, f32[2,4,32,128]{3,2,1,0:T(8,128)S(1)}, u32[]{:S(2)}, u32[]{:S(2)}) collective-permute-start(f32[2,4,32,128]{3,2,1,0:T(8,128)S(1)} %get-tuple-element.21), channel_id=1, source_target_pairs={{1,2},{3,4},{5,6},{7,8},{9,10},{11,12},{13,14},{2,1},{4,3},{6,5},{... | collective-permute-start | bytes 393224 | tf_op jit(solution)/shard_map/ppermute | solution.py:490
  2.8 5.7 %collective-permute-start.2 = (f32[2,4,32,128]{3,2,1,0:T(8,128)S(1)}, f32[2,4,32,128]{3,2,1,0:T(8,128)S(1)}, u32[]{:S(2)}, u32[]{:S(2)}) collective-permute-start(f32[2,4,32,128]{3,2,1,0:T(8,128)S(1)} %get-tuple-element.29), channel_id=1, source_target_pairs={{0,2},{2,4},{4,6},{6,8},{8,10},{10,12},{12,14},{3,1},{5,3},{7,5},{... | collective-permute-start | bytes 393224 | tf_op jit(solution)/shard_map/ppermute | solution.py:491
  8.5 0.0 collective-permute-done.1._arrived.cross_ref
  8.5 0.0 collective-permute-done.mate_ref
  8.5 1.5 %inner.1 = (f32[2,3,2,32,128]{4,3,2,1,0:T(8,128)S(1)}, f32[4,2,32,128]{3,2,1,0:T(8,128)S(1)}, f32[12,2,32,128]{3,2,1,0:T(8,128)S(1)}, f32[3,8,128]{2,1,0:T(8,128...) custom-call(f32[4,4,32,128]{3,2,1,0:T(8,128)S(1)} %get-tuple-element, ...), custom_call_target="tpu_custom_call" | custom-call | flops 20000000 | bytes 4000000 | tf_op jit(solution)/shard_map/inner/pallas_call | solution.py:493
  10.1 2.8 %collective-permute-done.2.same_ref = f32[2,4,32,128]{3,2,1,0:T(8,128)S(1)} collective-permute-done((f32[2,4,32,128]{3,2,1,0:T(8,128)S(1)}, f32[2,4,32,128]{3,2,1,0:T(8,128)S(1)}, u32[]{:S(2)}, u32[]{:S(2)}) %collective-permute-start.2) | collective-permute-done | bytes 131104 | tf_op jit(solution)/shard_map/ppermute | solution.py:491
  12.8 1.8 %outer.1 = (f32[10,2,32,128]{3,2,1,0:T(8,128)S(1)}, f32[16,1,128]{2,1,0:T(1,128)}) custom-call(f32[2,3,2,32,128]{4,3,2,1,0:T(8,128)S(1)} %get-tuple-element.22.ends_ref, f32[4,2,32,128]{3,2,1,0:T(8,128)S(1)} %get-tuple-element.23.elem_ref, f32[12,2,32,128]{3,2,1,0:T(8,128)S(1)} %get-tuple-element.24.edge_part_ref, ...), custom_call_target="tpu_custom_call" | custom-call | flops 10000000 | bytes 3000000 | tf_op jit(solution)/shard_map/outer/pallas_call | solution.py:518
  14.6 0.0 collective-permute-start.3
  14.6 7.7 %all-to-all-start = ((f32[16,1,128]{2,1,0:T(1,128)}), f32[16,1,128]{2,1,0:T(1,128)S(1)}, u32[]{:S(2)}, u32[]{:S(2)}) async-start(f32[16,1,128]{2,1,0:T(1,128)} %get-tuple-element.30), calls=%async_computation | async-start | bytes 16384 | tf_op jit(solution)/shard_map/all_to_all | solution.py:535
  22.4 0.0 collective-permute-done.3.take_ref
  22.4 1.1 %stress.1 = (f32[2,18,32,128]{3,2,1,0:T(8,128)S(1)}, f32[2,6,32,128]{3,2,1,0:T(8,128)S(1)}) custom-call(f32[2,3,2,32,128]{4,3,2,1,0:T(8,128)S(1)} %get-tuple-element.22.ends_ref, f32[4,2,32,128]{3,2,1,0:T(8,128)S(1)} %get-tuple-element.23.elem_ref, f32[2,9,2,32,128]{4,3,2,1,0:T(8,128)S(1)} %get-tuple-element.27.image_mode_ref, ...), custom_call_target="tpu_custom_call" | custom-call | flops 20000000 | bytes 4000000 | tf_op jit(solution)/shard_map/stress/pallas_call | solution.py:536
  23.5 1.2 %all-to-all-done.sums_ref = f32[16,1,128]{2,1,0:T(1,128)S(1)} async-done(((f32[16,1,128]{2,1,0:T(1,128)}), f32[16,1,128]{2,1,0:T(1,128)S(1)}, u32[]{:S(2)}, u32[]{:S(2)}) %all-to-all-start) | async-done | bytes 8224 | tf_op jit(solution)/shard_map/all_to_all | solution.py:535
  24.6 1.0 %combine.1 = (f32[3,128,128]{2,1,0:T(8,128)}, f32[6,128,128]{2,1,0:T(8,128)}) custom-call(f32[16,1,128]{2,1,0:T(1,128)S(1)} %all-to-all-done.sums_ref, f32[2,12,32,128]{3,2,1,0:T(8,128)S(1)} %get-tuple-element.31.early_ref, f32[2,18,32,128]{3,2,1,0:T(8,128)S(1)} %get-tuple-element.34.late_ref, f32[2,6,32,128]{3,2,1,0:T(8,128)S(1)} %get-tuple-element.35.middle_ref), custom_call_target="tpu_custom_call" | custom-call | tf_op jit(solution)/shard_map/combine/pallas_call | solution.py:552
Async XLA Ops:
  1.6 6.9 %collective-permute-start = (f32[4,4,32,128]{3,2,1,0:T(8,128)S(1)}, f32[4,4,32,128]{3,2,1,0:T(8,128)S(1)}, u32[]{:S(2)}, u32[]{:S(2)}) collective-permute-start(f32[4,4,32,128]{3,2,1,0:T(8,128)S(1)} %get-tuple-element.20.own_ref), channel_id=1, source_target_pairs={{0,1},{1,0},{2,3},{3,2},{4,5},{5,4},{6,7},{7,6},{8,9},{9,8},{10,11... | collective-permute-start | bytes 786440 | tf_op jit(solution)/shard_map/ppermute | solution.py:489
  2.1 6.3 %collective-permute-start.1 = (f32[2,4,32,128]{3,2,1,0:T(8,128)S(1)}, f32[2,4,32,128]{3,2,1,0:T(8,128)S(1)}, u32[]{:S(2)}, u32[]{:S(2)}) collective-permute-start(f32[2,4,32,128]{3,2,1,0:T(8,128)S(1)} %get-tuple-element.21), channel_id=1, source_target_pairs={{1,2},{3,4},{5,6},{7,8},{9,10},{11,12},{13,14},{2,1},{4,3},{6,5},{... | collective-permute-start | bytes 393224 | tf_op jit(solution)/shard_map/ppermute | solution.py:490
  2.8 10.0 %collective-permute-start.2 = (f32[2,4,32,128]{3,2,1,0:T(8,128)S(1)}, f32[2,4,32,128]{3,2,1,0:T(8,128)S(1)}, u32[]{:S(2)}, u32[]{:S(2)}) collective-permute-start(f32[2,4,32,128]{3,2,1,0:T(8,128)S(1)} %get-tuple-element.29), channel_id=1, source_target_pairs={{0,2},{2,4},{4,6},{6,8},{8,10},{10,12},{12,14},{3,1},{5,3},{7,5},{... | collective-permute-start | bytes 393224 | tf_op jit(solution)/shard_map/ppermute | solution.py:491
  14.6 7.7 %collective-permute-start.3 = (f32[10,2,32,128]{3,2,1,0:T(8,128)S(1)}, f32[10,2,32,128]{3,2,1,0:T(8,128)S(1)}, u32[]{:S(2)}, u32[]{:S(2)}) collective-permute-start(f32[10,2,32,128]{3,2,1,0:T(8,128)S(1)} %get-tuple-element.33.give_ref), channel_id=1, source_target_pairs={{0,1},{1,0},{2,3},{3,2},{4,5},{5,4},{6,7},{7,6},{8,9},{9,8},{10,11... | collective-permute-start | bytes 983048 | tf_op jit(solution)/shard_map/ppermute | solution.py:534
  14.6 10.0 %all-to-all-start = ((f32[16,1,128]{2,1,0:T(1,128)}), f32[16,1,128]{2,1,0:T(1,128)S(1)}, u32[]{:S(2)}, u32[]{:S(2)}) async-start(f32[16,1,128]{2,1,0:T(1,128)} %get-tuple-element.30), calls=%async_computation | async-start | bytes 16384 | tf_op jit(solution)/shard_map/all_to_all | solution.py:535
